TPU v7x, 128 devices: a whole 4x4x4 slice. The times are simulated.
128 devices in a mesh: row: 16 (over x, z), col: 8 (over y, core).
Axes of the slice: x: 4, y: 4, z: 4, core: 2. Of those that a mesh axis runs over, the one named last changes fastest.
Arguments:
- initial_estimate0: float32 [96, 256, 2048], P(None, 'row', 'col'), may hold values from 0.1 to 1
- clutter: float32 [256, 2048], P('row', 'col'), may hold values from 0 to 1.5
- counts: int32 [128, 96, 128], P(('row', 'col')), may hold values from 1 to 10000
- antenna_settings: float32 [128, 5, 128], P(('row', 'col')), as said below
- tile_block_list: int32 [16, 8, 32], P('row', 'col'), may hold values from 0 to 127, as said below
- tile_block_count: int32 [16, 8], P('row', 'col'), may hold values from 1 to 32
Outputs:
- estimate: float32 [96, 256, 2048], P(None, 'row', 'col')
Inputs may be any that keep to these rules, and one draw needn't show every extreme that they name: `tile_block_list`: block b's owner group along row is b // 8; entry i of a tile's list is used only when i < tile_block_count, and unused entries hold 0; the listed blocks of one tile are distinct; every block is listed by some tile; one tile lists at most 2 blocks of one owner group, and the tiles of some column list 32 blocks each. `antenna_settings`: radii and gains are positive.
All inputs are finite; a program needn't handle non-finite values.
Results may differ from a plain program's by a relative error of at most 0.0003.
Values sent between devices are 32-bit elements; how exact they have to be, the bound alone decides.
No kernel may reach another device: no remote copies, remote signals or barrier semaphores. Data moves between devices by JAX's collectives and lax.ppermute only.
A program may use at most 64 MiB of HBM per device.

v0:
```python
import jax
import jax.numpy as jnp
from jax import lax
from jax.sharding import PartitionSpec as P

ITERS = 2


def coverage(settings_rows, terrain_loss, pixel_row, pixel_column):
    antenna_row = settings_rows[:, 0, :, None]
    antenna_column = settings_rows[:, 1, :, None]
    antenna_radius = settings_rows[:, 2, :, None]
    antenna_gain = settings_rows[:, 3, :, None]
    antenna_group = settings_rows[:, 4, :, None]
    row_distance = pixel_row[None, None, :] - antenna_row
    column_distance = pixel_column[None, None, :] - antenna_column
    return (
        antenna_gain
        * jnp.exp(-antenna_group * terrain_loss[None, None, :])
        / (
            1.0
            + (row_distance * row_distance + column_distance * column_distance)
            / (antenna_radius * antenna_radius)
        )
    )


def shards(initial_estimate0, clutter, counts, antenna_settings, tile_block_list, tile_block_count):
    highest = lax.Precision.HIGHEST
    map_count, rows_tile, cols_tile = initial_estimate0.shape
    n_pixels = rows_tile * cols_tile
    antenna_count = antenna_settings.shape[2]
    slot_count = tile_block_list.shape[2]
    block_numbers = tile_block_list.reshape(slot_count)
    listed = tile_block_count.reshape(())
    slot_index = jnp.arange(slot_count, dtype=jnp.int32)
    slot_live = slot_index < listed
    estimate = initial_estimate0.reshape(map_count, n_pixels)
    antenna_records = lax.all_gather(antenna_settings, ("row", "col"), axis=0, tiled=True)
    local_row = jnp.repeat(jnp.arange(rows_tile, dtype=jnp.int32), cols_tile)
    local_col = jnp.tile(jnp.arange(cols_tile, dtype=jnp.int32), rows_tile)
    pixel_row = (lax.axis_index("row") * rows_tile + local_row).astype(jnp.float32) + 0.5
    pixel_column = (lax.axis_index("col") * cols_tile + local_col).astype(jnp.float32) + 0.5
    terrain_loss = clutter.reshape(n_pixels)
    n_turns = (listed + 3) // 4

    def group_cover(turn_index):
        group_ids = lax.dynamic_slice(block_numbers, (turn_index * 4,), (4,))
        group_live = (turn_index * 4 + jnp.arange(4, dtype=jnp.int32) < listed).astype(jnp.float32)
        return (
            coverage(antenna_records[group_ids], terrain_loss, pixel_row, pixel_column)
            * group_live[:, None, None]
        )

    sensitivity = jnp.zeros((n_pixels,), jnp.float32)
    for sweep in range(ITERS):

        def forward_turn(turn_index, state):
            partial_sums, sens_sum = state
            coverage_value = group_cover(turn_index)
            partial_value = jnp.einsum("tp,sap->sta", estimate, coverage_value, precision=highest)
            partial_sums = lax.dynamic_update_slice(
                partial_sums, partial_value, (turn_index * 4, 0, 0)
            )
            if sweep == 0:
                sens_sum = sens_sum + jnp.sum(coverage_value, axis=(0, 1))
            return (partial_sums, sens_sum)

        initial_parts = jnp.zeros((slot_count, map_count, antenna_count), jnp.float32)
        partial_sums, sensitivity = lax.fori_loop(
            0, n_turns, forward_turn, (initial_parts, sensitivity)
        )
        wanted = jnp.arange(lax.axis_size(("row", "col")) * counts.shape[0], dtype=jnp.int32)
        picker = ((block_numbers[None, :] == wanted[:, None]) & slot_live[None, :]).astype(
            jnp.float32
        )
        projected_counts = lax.psum_scatter(
            jnp.einsum("rm,mta->rta", picker, partial_sums, precision=highest),
            ("row", "col"),
            scatter_dimension=0,
            tiled=True,
        )
        ratios = counts.astype(jnp.float32) / projected_counts
        shard_rows = lax.all_gather(ratios, ("row", "col"), axis=0, tiled=True)
        n_rows = shard_rows.shape[0]
        take_picker = (
            block_numbers[:, None] == jnp.arange(n_rows, dtype=jnp.int32)[None, :]
        ).astype(jnp.float32)
        returned_ratio = jnp.einsum("mn,nta->mta", take_picker, shard_rows, precision=highest)

        def backward_turn(turn_index, backsum):
            coverage_value = group_cover(turn_index)
            group_fraction = lax.dynamic_slice(
                returned_ratio, (turn_index * 4, 0, 0), (4, map_count, antenna_count)
            )
            return backsum + jnp.einsum(
                "sta,sap->tp", group_fraction, coverage_value, precision=highest
            )

        backsum = lax.fori_loop(
            0, n_turns, backward_turn, jnp.zeros((map_count, n_pixels), jnp.float32)
        )
        estimate = estimate * backsum / sensitivity[None, :]
    return estimate.reshape(map_count, rows_tile, cols_tile)


def solution(mesh):
    in_specs = (
        P(None, "row", "col"),
        P("row", "col"),
        P(("row", "col"), None, None),
        P(("row", "col"), None, None),
        P("row", "col", None),
        P("row", "col"),
    )
    out_specs = P(None, "row", "col")
    return jax.shard_map(shards, mesh=mesh, in_specs=in_specs, out_specs=out_specs, check_vma=False)
```

profile of v0, /device:TPU:24, one launch (start us, length us, event | category | flops | bytes accessed | tf_op | source)
XLA Modules:
  0.0 1156.3 jit_solution(1581064215839538641)
XLA Ops:
  7.9 40.3 %all_gather.9 = f32[128,5,128]{2,1,0:T(8,128)} all-gather(f32[1,5,128]{2,1,0:T(8,128)S(1)} %copy.11), channel_id=1, replica_groups=mesh['row'=16,'col'=8] {'row','col'}, dimensions={0}, use_global_device_ids=true | all-gather | bytes 330240 | tf_op jit(solution)/shard_map/all_gather | solution.py:39
  51.0 167.4 %while.46 = (s32[]{:T(128)}, f32[32,96,128]{2,0,1:T(8,128)S(1)}, f32[4096]{0:T(1024)S(1)}, s32[]{:T(128)}, s32[32]{0:T(128)}, /*index=5*/f32[128,5,128]{2,1,0:T(...) while((s32[]{:T(128)}, f32[32,96,128]{2,0,1:T(8,128)S(1)}, ...), condition=%wide.region_2.3_spmd.clone, body=%wide.region_0.2_spmd.clone.sunk | while | flops 2464180224 | bytes 2523459 | solution.py:70
  55.1 12.0 %fusion.158 = f32[4,96,128]{2,1,0:T(8,128)S(1)} fusion(f32[96,4096]{1,0:T(8,128)S(1)} %get-tuple-element.832, f32[4]{0:T(128)S(1)} %compare_convert_fusion.8, f32[4,128]{1,0:T(4,128)S(1)} %bitcast.214, f32[4,128]{1,0:T(4,128)S(1)} %bitcast.208, f32[4096]{0:T(1024)S(1)} %bitcast.191, f32[4,128]{1,0:T(4,128)S(1)} %bitcast.210, ...), kind=kOutput, calls=%fused_computation.16.clone.1 | convolution fusion | flops 2438987776 | bytes 1828880 | tf_op jit(solution)/shard_map/while/body/tp,sap->sta/dot_general | solution.py:61
  75.9 12.0 %fusion.158 = f32[4,96,128]{2,1,0:T(8,128)S(1)} fusion(f32[96,4096]{1,0:T(8,128)S(1)} %get-tuple-element.832, f32[4]{0:T(128)S(1)} %compare_convert_fusion.8, f32[4,128]{1,0:T(4,128)S(1)} %bitcast.214, f32[4,128]{1,0:T(4,128)S(1)} %bitcast.208, f32[4096]{0:T(1024)S(1)} %bitcast.191, f32[4,128]{1,0:T(4,128)S(1)} %bitcast.210, ...), kind=kOutput, calls=%fused_computation.16.clone.1 | convolution fusion | flops 2438987776 | bytes 1828880 | tf_op jit(solution)/shard_map/while/body/tp,sap->sta/dot_general | solution.py:61
  96.7 12.0 %fusion.158 = f32[4,96,128]{2,1,0:T(8,128)S(1)} fusion(f32[96,4096]{1,0:T(8,128)S(1)} %get-tuple-element.832, f32[4]{0:T(128)S(1)} %compare_convert_fusion.8, f32[4,128]{1,0:T(4,128)S(1)} %bitcast.214, f32[4,128]{1,0:T(4,128)S(1)} %bitcast.208, f32[4096]{0:T(1024)S(1)} %bitcast.191, f32[4,128]{1,0:T(4,128)S(1)} %bitcast.210, ...), kind=kOutput, calls=%fused_computation.16.clone.1 | convolution fusion | flops 2438987776 | bytes 1828880 | tf_op jit(solution)/shard_map/while/body/tp,sap->sta/dot_general | solution.py:61
  117.5 12.0 %fusion.158 = f32[4,96,128]{2,1,0:T(8,128)S(1)} fusion(f32[96,4096]{1,0:T(8,128)S(1)} %get-tuple-element.832, f32[4]{0:T(128)S(1)} %compare_convert_fusion.8, f32[4,128]{1,0:T(4,128)S(1)} %bitcast.214, f32[4,128]{1,0:T(4,128)S(1)} %bitcast.208, f32[4096]{0:T(1024)S(1)} %bitcast.191, f32[4,128]{1,0:T(4,128)S(1)} %bitcast.210, ...), kind=kOutput, calls=%fused_computation.16.clone.1 | convolution fusion | flops 2438987776 | bytes 1828880 | tf_op jit(solution)/shard_map/while/body/tp,sap->sta/dot_general | solution.py:61
  138.4 12.0 %fusion.158 = f32[4,96,128]{2,1,0:T(8,128)S(1)} fusion(f32[96,4096]{1,0:T(8,128)S(1)} %get-tuple-element.832, f32[4]{0:T(128)S(1)} %compare_convert_fusion.8, f32[4,128]{1,0:T(4,128)S(1)} %bitcast.214, f32[4,128]{1,0:T(4,128)S(1)} %bitcast.208, f32[4096]{0:T(1024)S(1)} %bitcast.191, f32[4,128]{1,0:T(4,128)S(1)} %bitcast.210, ...), kind=kOutput, calls=%fused_computation.16.clone.1 | convolution fusion | flops 2438987776 | bytes 1828880 | tf_op jit(solution)/shard_map/while/body/tp,sap->sta/dot_general | solution.py:61
  159.2 12.0 %fusion.158 = f32[4,96,128]{2,1,0:T(8,128)S(1)} fusion(f32[96,4096]{1,0:T(8,128)S(1)} %get-tuple-element.832, f32[4]{0:T(128)S(1)} %compare_convert_fusion.8, f32[4,128]{1,0:T(4,128)S(1)} %bitcast.214, f32[4,128]{1,0:T(4,128)S(1)} %bitcast.208, f32[4096]{0:T(1024)S(1)} %bitcast.191, f32[4,128]{1,0:T(4,128)S(1)} %bitcast.210, ...), kind=kOutput, calls=%fused_computation.16.clone.1 | convolution fusion | flops 2438987776 | bytes 1828880 | tf_op jit(solution)/shard_map/while/body/tp,sap->sta/dot_general | solution.py:61
  180.0 12.0 %fusion.158 = f32[4,96,128]{2,1,0:T(8,128)S(1)} fusion(f32[96,4096]{1,0:T(8,128)S(1)} %get-tuple-element.832, f32[4]{0:T(128)S(1)} %compare_convert_fusion.8, f32[4,128]{1,0:T(4,128)S(1)} %bitcast.214, f32[4,128]{1,0:T(4,128)S(1)} %bitcast.208, f32[4096]{0:T(1024)S(1)} %bitcast.191, f32[4,128]{1,0:T(4,128)S(1)} %bitcast.210, ...), kind=kOutput, calls=%fused_computation.16.clone.1 | convolution fusion | flops 2438987776 | bytes 1828880 | tf_op jit(solution)/shard_map/while/body/tp,sap->sta/dot_general | solution.py:61
  228.1 208.6 %reduce-scatter.3.cloned.1.call-done = f32[1,96,128]{2,1,0:T(8,128)} async-done(((f32[128,96,128]{2,1,0:T(8,128)}), f32[1,96,128]{2,1,0:T(8,128)}) %reduce-scatter.3.cloned.1.call-update) | async-done | bytes 49168 | tf_op jit(solution)/shard_map/reduce_scatter | solution.py:77
  438.4 67.7 %all-gather.3.cloned.1.call-done = f32[128,96,128]{2,1,0:T(8,128)} async-done(((f32[1,96,128]{2,1,0:T(8,128)}), f32[128,96,128]{2,1,0:T(8,128)}) %all-gather.3.cloned.1.call-update) | async-done | bytes 6291472 | tf_op jit(solution)/shard_map/all_gather | solution.py:84
  515.7 102.0 %while.47 = (s32[]{:T(128)}, f32[96,4096]{1,0:T(8,128)S(1)}, s32[]{:T(128)}, f32[32,96,128]{2,0,1:T(8,128)}, s32[32]{0:T(128)S(1)}, /*index=5*/f32[128,5,128]{2,...) while((s32[]{:T(128)}, f32[96,4096]{1,0:T(8,128)S(1)}, ...), condition=%wide.region_5.6_spmd.clone, body=%wide.region_4.5_spmd.clone.sunk | while | flops 2439407616 | bytes 3971371 | solution.py:100
  619.3 128.8 %while.48 = (s32[]{:T(128)}, f32[32,96,128]{2,0,1:T(8,128)S(1)}, s32[]{:T(128)}, s32[32]{0:T(128)S(1)}, f32[128,5,128]{2,1,0:T(8,128)}, /*index=5*/f32[16,256]{1...) while((s32[]{:T(128)}, f32[32,96,128]{2,0,1:T(8,128)S(1)}, ...), condition=%wide.region_7.8_spmd.clone, body=%wide.region_6.7_spmd.clone.sunk | while | flops 2439014400 | bytes 2398507 | solution.py:70
  622.2 13.4 %fusion.167 = f32[4,96,128]{2,1,0:T(8,128)S(1)} fusion(f32[96,4096]{1,0:T(8,128)} %get-tuple-element.916, f32[4]{0:T(128)S(1)} %compare_convert_fusion.10, f32[4,128]{1,0:T(4,128)S(1)} %bitcast.230, f32[4,128]{1,0:T(4,128)S(1)} %bitcast.227, f32[4096]{0:T(1024)S(1)} %bitcast.200, f32[4,128]{1,0:T(4,128)S(1)} %bitcast.228, f32[4096]{0:T(1024)S(1)} %bitcast.204, ...), kind=kOutput, calls=%fused_computation.85.clone.1 | convolution fusion | flops 2438987776 | bytes 1828880 | tf_op jit(solution)/shard_map/while/body/tp,sap->sta/dot_general | solution.py:61
  638.2 13.4 %fusion.167 = f32[4,96,128]{2,1,0:T(8,128)S(1)} fusion(f32[96,4096]{1,0:T(8,128)} %get-tuple-element.916, f32[4]{0:T(128)S(1)} %compare_convert_fusion.10, f32[4,128]{1,0:T(4,128)S(1)} %bitcast.230, f32[4,128]{1,0:T(4,128)S(1)} %bitcast.227, f32[4096]{0:T(1024)S(1)} %bitcast.200, f32[4,128]{1,0:T(4,128)S(1)} %bitcast.228, f32[4096]{0:T(1024)S(1)} %bitcast.204, ...), kind=kOutput, calls=%fused_computation.85.clone.1 | convolution fusion | flops 2438987776 | bytes 1828880 | tf_op jit(solution)/shard_map/while/body/tp,sap->sta/dot_general | solution.py:61
  654.2 13.4 %fusion.167 = f32[4,96,128]{2,1,0:T(8,128)S(1)} fusion(f32[96,4096]{1,0:T(8,128)} %get-tuple-element.916, f32[4]{0:T(128)S(1)} %compare_convert_fusion.10, f32[4,128]{1,0:T(4,128)S(1)} %bitcast.230, f32[4,128]{1,0:T(4,128)S(1)} %bitcast.227, f32[4096]{0:T(1024)S(1)} %bitcast.200, f32[4,128]{1,0:T(4,128)S(1)} %bitcast.228, f32[4096]{0:T(1024)S(1)} %bitcast.204, ...), kind=kOutput, calls=%fused_computation.85.clone.1 | convolution fusion | flops 2438987776 | bytes 1828880 | tf_op jit(solution)/shard_map/while/body/tp,sap->sta/dot_general | solution.py:61
  670.2 13.4 %fusion.167 = f32[4,96,128]{2,1,0:T(8,128)S(1)} fusion(f32[96,4096]{1,0:T(8,128)} %get-tuple-element.916, f32[4]{0:T(128)S(1)} %compare_convert_fusion.10, f32[4,128]{1,0:T(4,128)S(1)} %bitcast.230, f32[4,128]{1,0:T(4,128)S(1)} %bitcast.227, f32[4096]{0:T(1024)S(1)} %bitcast.200, f32[4,128]{1,0:T(4,128)S(1)} %bitcast.228, f32[4096]{0:T(1024)S(1)} %bitcast.204, ...), kind=kOutput, calls=%fused_computation.85.clone.1 | convolution fusion | flops 2438987776 | bytes 1828880 | tf_op jit(solution)/shard_map/while/body/tp,sap->sta/dot_general | solution.py:61
  686.2 13.4 %fusion.167 = f32[4,96,128]{2,1,0:T(8,128)S(1)} fusion(f32[96,4096]{1,0:T(8,128)} %get-tuple-element.916, f32[4]{0:T(128)S(1)} %compare_convert_fusion.10, f32[4,128]{1,0:T(4,128)S(1)} %bitcast.230, f32[4,128]{1,0:T(4,128)S(1)} %bitcast.227, f32[4096]{0:T(1024)S(1)} %bitcast.200, f32[4,128]{1,0:T(4,128)S(1)} %bitcast.228, f32[4096]{0:T(1024)S(1)} %bitcast.204, ...), kind=kOutput, calls=%fused_computation.85.clone.1 | convolution fusion | flops 2438987776 | bytes 1828880 | tf_op jit(solution)/shard_map/while/body/tp,sap->sta/dot_general | solution.py:61
  702.3 13.4 %fusion.167 = f32[4,96,128]{2,1,0:T(8,128)S(1)} fusion(f32[96,4096]{1,0:T(8,128)} %get-tuple-element.916, f32[4]{0:T(128)S(1)} %compare_convert_fusion.10, f32[4,128]{1,0:T(4,128)S(1)} %bitcast.230, f32[4,128]{1,0:T(4,128)S(1)} %bitcast.227, f32[4096]{0:T(1024)S(1)} %bitcast.200, f32[4,128]{1,0:T(4,128)S(1)} %bitcast.228, f32[4096]{0:T(1024)S(1)} %bitcast.204, ...), kind=kOutput, calls=%fused_computation.85.clone.1 | convolution fusion | flops 2438987776 | bytes 1828880 | tf_op jit(solution)/shard_map/while/body/tp,sap->sta/dot_general | solution.py:61
  718.3 13.4 %fusion.167 = f32[4,96,128]{2,1,0:T(8,128)S(1)} fusion(f32[96,4096]{1,0:T(8,128)} %get-tuple-element.916, f32[4]{0:T(128)S(1)} %compare_convert_fusion.10, f32[4,128]{1,0:T(4,128)S(1)} %bitcast.230, f32[4,128]{1,0:T(4,128)S(1)} %bitcast.227, f32[4096]{0:T(1024)S(1)} %bitcast.200, f32[4,128]{1,0:T(4,128)S(1)} %bitcast.228, f32[4096]{0:T(1024)S(1)} %bitcast.204, ...), kind=kOutput, calls=%fused_computation.85.clone.1 | convolution fusion | flops 2438987776 | bytes 1828880 | tf_op jit(solution)/shard_map/while/body/tp,sap->sta/dot_general | solution.py:61
  734.3 13.4 %fusion.167 = f32[4,96,128]{2,1,0:T(8,128)S(1)} fusion(f32[96,4096]{1,0:T(8,128)} %get-tuple-element.916, f32[4]{0:T(128)S(1)} %compare_convert_fusion.10, f32[4,128]{1,0:T(4,128)S(1)} %bitcast.230, f32[4,128]{1,0:T(4,128)S(1)} %bitcast.227, f32[4096]{0:T(1024)S(1)} %bitcast.200, f32[4,128]{1,0:T(4,128)S(1)} %bitcast.228, f32[4096]{0:T(1024)S(1)} %bitcast.204, ...), kind=kOutput, calls=%fused_computation.85.clone.1 | convolution fusion | flops 2438987776 | bytes 1828880 | tf_op jit(solution)/shard_map/while/body/tp,sap->sta/dot_general | solution.py:61
  757.1 210.0 %reduce-scatter.5.cloned.1.call-done = f32[1,96,128]{2,1,0:T(8,128)} async-done(((f32[128,96,128]{2,1,0:T(8,128)}), f32[1,96,128]{2,1,0:T(8,128)}) %reduce-scatter.5.cloned.1.call-update) | async-done | bytes 49168 | tf_op jit(solution)/shard_map/reduce_scatter | solution.py:77
  968.6 67.3 %all-gather.5.cloned.1.call-done = f32[128,96,128]{2,1,0:T(8,128)} async-done(((f32[1,96,128]{2,1,0:T(8,128)}), f32[128,96,128]{2,1,0:T(8,128)}) %all-gather.5.cloned.1.call-update) | async-done | bytes 6291472 | tf_op jit(solution)/shard_map/all_gather | solution.py:84
  1045.4 102.2 %while.49 = (s32[]{:T(128)}, f32[96,4096]{1,0:T(8,128)S(1)}, s32[]{:T(128)}, f32[32,96,128]{2,0,1:T(8,128)}, s32[32]{0:T(128)S(1)}, /*index=5*/f32[128,5,128]{2,...) while((s32[]{:T(128)}, f32[96,4096]{1,0:T(8,128)S(1)}, ...), condition=%wide.region_10.11_spmd.clone, body=%wide.region_9.10_spmd.clone.sunk | while | flops 2439407616 | bytes 3971371 | solution.py:100
  (398 shorter events, 352.5 us)
Async XLA Ops:
  6.5 430.2 %reduce-scatter.3.cloned.1.call-start = ((), (), s32[]{:S(2)}) async-start(), calls=%async_computation.2 | async-start | bytes 6340608 | tf_op jit(solution)/shard_map/reduce_scatter | solution.py:77
  218.4 399.4 %copy-start.2 = (f32[4096]{0:T(1024)}, f32[4096]{0:T(1024)S(1)}, u32[]{:S(2)}) copy-start(f32[4096]{0:T(1024)S(1)} %get-tuple-element.225) | copy-start | bytes 49156
  218.4 9.6 copy-start.7
  228.0 208.7 %copy-start.4 = (s32[1,96,128]{2,1,0:T(8,128)S(1)}, s32[1,96,128]{2,1,0:T(8,128)}, u32[]{:S(2)}) copy-start(s32[1,96,128]{2,1,0:T(8,128)} %param.16) | copy-start | bytes 147460
  228.0 278.1 %copy-start.6 = (s32[32]{0:T(128)S(1)}, s32[32]{0:T(128)}, u32[]{:S(2)}) copy-start(s32[32]{0:T(128)} %get-tuple-element.989) | copy-start | bytes 388
  228.1 287.6 %copy-start = (f32[16,256]{1,0:T(8,128)S(1)}, f32[16,256]{1,0:T(8,128)}, u32[]{:S(2)}) copy-start(f32[16,256]{1,0:T(8,128)} %get-tuple-element.973) | copy-start | bytes 49156
  228.1 278.1 %all-gather.3.cloned.1.call-start = ((), (), s32[]{:S(2)}) async-start(), calls=%async_computation.3 | async-start | bytes 6340608 | tf_op jit(solution)/shard_map/all_gather | solution.py:84
  438.2 528.9 %reduce-scatter.5.cloned.1.call-start = ((), (), s32[]{:S(2)}) async-start(), calls=%async_computation.4 | async-start | bytes 6340608 | tf_op jit(solution)/shard_map/reduce_scatter | solution.py:77
  619.3 128.8 %copy-start.8 = (pred[32]{0:T(512)(128)(4,1)S(1)}, pred[32]{0:T(512)(128)(4,1)}, u32[]{:S(2)}) copy-start(pred[32]{0:T(512)(128)(4,1)} %copy-done.7) | copy-start | bytes 100
  757.0 210.1 %copy-start.5 = (s32[1,96,128]{2,1,0:T(8,128)S(1)}, s32[1,96,128]{2,1,0:T(8,128)}, u32[]{:S(2)}) copy-start(s32[1,96,128]{2,1,0:T(8,128)} %param.16) | copy-start | bytes 147460
  757.1 278.8 %all-gather.5.cloned.1.call-start = ((), (), s32[]{:S(2)}) async-start(), calls=%async_computation.5 | async-start | bytes 6340608 | tf_op jit(solution)/shard_map/all_gather | solution.py:84
  1045.4 102.2 %copy-start.1 = (f32[96,4096]{1,0:T(8,128)S(1)}, f32[96,4096]{1,0:T(8,128)}, u32[]{:S(2)}) copy-start(f32[96,4096]{1,0:T(8,128)} %get-tuple-element.979) | copy-start | bytes 4718596
  1045.4 102.2 %copy-start.3 = (f32[4096]{0:T(1024)S(1)}, f32[4096]{0:T(1024)}, u32[]{:S(2)}) copy-start(f32[4096]{0:T(1024)} %copy-done.2) | copy-start | bytes 49156
Sparse Core Ops, SparseCore 0:
  228.2 208.4 reduce-scatter.2
  440.3 65.7 all-gather.2
  757.2 209.8 reduce-scatter.4
  970.1 65.7 all-gather.4
where the time goes:
time: 1160 us
  waiting for transfers between devices  554 us (48%)
  matrix products  375 us (32%)
  local copies, waits for them, and re-layouts  95.2 us (8%)
  other arithmetic  72.6 us (6%)
  blocking collectives  40.3 us (3%)
  between operations  14.2 us (1%)
    reduce_scatter x2, waiting for transfers between devices, shards(): lax.psum_scatter(jnp.einsum('rm,mta->rta', picker, partial_sums, precisio...  419 us
    dot_general x16, matrix products, forward_turn(): jnp.einsum('tp,sap->sta', estimate, coverage_value, precision=highest)  203 us
    dot_general x16, matrix products, backward_turn(): jnp.einsum('sta,sap->tp', group_fraction, coverage_value, precision=highest)  148 us
    all_gather x2, waiting for transfers between devices, shards(): shard_rows = lax.all_gather(ratios, ('row', 'col'), axis=0, tiled=True)  135 us
    gather x32, local copies, waits for them, and re-layouts, group_cover(): antenna_records[group_ids]  51 us
    all_gather x1, blocking collectives, shards(): lax.all_gather(antenna_settings, ('row', 'col'), axis=0, tiled=True)  40.3 us
    reduce_sum x8, other arithmetic, forward_turn(): sens_sum = sens_sum + jnp.sum(coverage_value, axis=(0, 1))  38.6 us
  transfers between devices with their start and end apart: 4, of which 4 were waited for; matrix products, arithmetic and copies ran while one was open for 0% of the time, Pallas kernels for 0%

commit v1 on v0

v1 whole, which is shorter than its diff:
```python
import functools
import jax
import jax.numpy as jnp
from jax import lax
from jax.experimental import pallas as pl
from jax.experimental.pallas import tpu as pltpu
from jax.sharding import PartitionSpec as P

ITERS = 2
LOG2E = 1.4426950408889634
CLUTTER_MAX = 1.5
STEP = 4
LO_SCALE = 65536.0
LO_TYPE = jnp.float8_e5m2
BIG = 1e38
f32 = jnp.float32
bf16 = jnp.bfloat16


def split(x):
    hi = x.astype(bf16)
    return hi, (x - hi.astype(f32)).astype(bf16)


def antenna_scale(record):
    return record[3:4, :] * jnp.exp2(jnp.maximum(record[4:5, :] * (-LOG2E * CLUTTER_MAX), 0.0))


def build_kernel(tab, origin, records, clut, est2, hi, lo, part, *, rows, cols):
    step = pl.program_id(0)
    maps = part.shape[1]
    for k in range(STEP):
        block = tab[step * STEP + k]
        lanes = pl.ds(k * 128, 128)

        @pl.when(block >= 0)
        def _():
            record = records[block]
            antenna_row = record[0:1, :]
            inv = 1.0 / (record[2:3, :] * record[2:3, :])
            slope = record[4:5, :] * (-LOG2E)
            peak = jnp.exp2(jnp.maximum(slope * CLUTTER_MAX, 0.0))
            inv = inv * peak
            column = (
                origin[1] + lax.broadcasted_iota(jnp.int32, (cols, 128), 0)
            ).astype(f32) + 0.5
            across = column - record[1:2, :]
            across = jnp.minimum(across * across * inv, BIG)
            slope8 = jnp.broadcast_to(slope, (8, 128))

            @pl.loop(0, rows)
            def _(r):
                down = (origin[0] + r).astype(f32) + 0.5 - antenna_row
                down = jnp.minimum(peak + down * down * inv, BIG)
                at = pl.multiple_of(r * cols, cols)
                power = jnp.exp2(clut[pl.ds(at, cols), :] * slope)
                den = across + down
                guess = pl.reciprocal(den, approx=True)
                guess = guess * (2.0 - den * guess)
                value = power * guess
                top = value.astype(bf16)
                hi[pl.ds(at, cols), lanes] = top
                lo[pl.ds(at, cols), lanes] = (
                    (value - top.astype(f32)) * LO_SCALE
                ).astype(LO_TYPE)

        @pl.when(block < 0)
        def _():
            hi[:, lanes] = jnp.zeros((rows * cols, 128), bf16)
            lo[:, lanes] = jnp.zeros((rows * cols, 128), LO_TYPE)

    forward_dot(tab, step, records, est2, hi, lo, part, maps)


def forward_dot(tab, step, records, est2, hi, lo, part, maps):
    both = jnp.dot(est2[...], hi[...], preferred_element_type=f32)
    low = jnp.dot(est2[:maps, :], lo[...].astype(bf16), preferred_element_type=f32)
    total = both[:maps, :] + (both[maps:, :] + low * (1.0 / LO_SCALE))
    for k in range(STEP):
        scale = antenna_scale(records[jnp.maximum(tab[step * STEP + k], 0)])
        part[k] = total[:, k * 128 : (k + 1) * 128] * scale


def forward_kernel(tab, records, est2, hi, lo, part):
    forward_dot(tab, pl.program_id(0), records, est2, hi, lo, part, part.shape[1])


def backward_kernel(tab, records, ratios, est, sens_in, hi, lo, est_out, *rest, first):
    if first:
        est2_out, sens_out, acc = rest
    else:
        (acc,) = rest
    step = pl.program_id(0)
    maps = est.shape[0]
    n_pixels = est.shape[1]

    @pl.when(step == 0)
    def _():
        acc[...] = jnp.zeros_like(acc)

    lhs = []
    low = []
    for k in range(STEP):
        block = tab[step * STEP + k]
        live = block >= 0
        scale = antenna_scale(records[jnp.maximum(block, 0)])
        ratio = jnp.where(live, ratios[k] * scale, 0.0)
        parts = [ratio]
        if first:
            ones = jnp.where(live, jnp.broadcast_to(scale, (16, 128)), 0.0)
            parts.append(ones)
        stack = jnp.concatenate(parts, axis=0)
        top, rest_of = split(stack)
        lhs.append(jnp.concatenate([top, rest_of], axis=0))
        low.append((top.astype(f32) * (1.0 / LO_SCALE)).astype(bf16))
    lhs = jnp.concatenate(lhs, axis=1)
    low = jnp.concatenate(low, axis=1)
    height = low.shape[0]
    chunk = 512
    dims = (((1,), (1,)), ((), ()))

    @pl.loop(0, n_pixels // chunk)
    def _(c):
        at = pl.multiple_of(c * chunk, chunk)
        wide = lax.dot_general(lhs, hi[pl.ds(at, chunk), :], dims, preferred_element_type=f32)
        thin = lax.dot_general(
            low, lo[pl.ds(at, chunk), :].astype(bf16), dims, preferred_element_type=f32
        )
        acc[:, pl.ds(at, chunk)] += wide[:height, :] + (wide[height:, :] + thin)

    @pl.when(step == pl.num_programs(0) - 1)
    def _():
        if first:
            sens = acc[maps : maps + 1, :]
            sens_out[...] = jnp.broadcast_to(sens, sens_out.shape)
        else:
            sens = sens_in[0:1, :]
        new = est[...] * acc[:maps, :] / sens
        est_out[...] = new
        if first:
            top, rest_of = split(new)
            est2_out[:maps, :] = top
            est2_out[maps:, :] = rest_of


def combine_kernel(tab, recv, out):
    out[...] = jnp.zeros_like(out)

    @pl.loop(0, recv.shape[0])
    def _(i):
        local = tab[i]

        @pl.when(local >= 0)
        def _():
            out[local] = out[local] + recv[i]


def pick_kernel(tab, table, out):
    @pl.loop(0, out.shape[0])
    def _(i):
        out[i] = table[jnp.maximum(tab[i], 0)]


def params(mib):
    return pltpu.CompilerParams(vmem_limit_bytes=mib << 20)


def spec(shape, index):
    return pl.BlockSpec(shape, index)


def whole(shape):
    return pl.BlockSpec(shape, lambda *_: (0,) * len(shape))


def build(tab, origin, records, clut, est2, rows, cols):
    slots = tab.shape[0]
    maps2, n_pixels = est2.shape
    maps = maps2 // 2
    wide = STEP * 128
    return pl.pallas_call(
        functools.partial(build_kernel, rows=rows, cols=cols),
        grid_spec=pltpu.PrefetchScalarGridSpec(
            num_scalar_prefetch=2,
            grid=(slots // STEP,),
            in_specs=[whole(records.shape), whole(clut.shape), whole(est2.shape)],
            out_specs=[
                spec((n_pixels, wide), lambda i, *_: (0, i)),
                spec((n_pixels, wide), lambda i, *_: (0, i)),
                spec((STEP, maps, 128), lambda i, *_: (i, 0, 0)),
            ],
        ),
        out_shape=[
            jax.ShapeDtypeStruct((n_pixels, slots * 128), bf16),
            jax.ShapeDtypeStruct((n_pixels, slots * 128), LO_TYPE),
            jax.ShapeDtypeStruct((slots, maps, 128), f32),
        ],
        compiler_params=params(56),
        name="build_cover",
    )(tab, origin, records, clut, est2)


def forward(tab, records, est2, hi, lo):
    slots = tab.shape[0]
    maps2, n_pixels = est2.shape
    maps = maps2 // 2
    wide = STEP * 128
    return pl.pallas_call(
        forward_kernel,
        grid_spec=pltpu.PrefetchScalarGridSpec(
            num_scalar_prefetch=1,
            grid=(slots // STEP,),
            in_specs=[
                whole(records.shape),
                whole(est2.shape),
                spec((n_pixels, wide), lambda i, *_: (0, i)),
                spec((n_pixels, wide), lambda i, *_: (0, i)),
            ],
            out_specs=spec((STEP, maps, 128), lambda i, *_: (i, 0, 0)),
        ),
        out_shape=jax.ShapeDtypeStruct((slots, maps, 128), f32),
        compiler_params=params(56),
        name="forward_product",
    )(tab, records, est2, hi, lo)


def backward(tab, records, ratios, est, sens, hi, lo, first):
    slots = tab.shape[0]
    maps, n_pixels = est.shape
    wide = STEP * 128
    out_specs = [whole((maps, n_pixels))]
    out_shape = [jax.ShapeDtypeStruct((maps, n_pixels), f32)]
    if first:
        out_specs += [whole((2 * maps, n_pixels)), whole((8, n_pixels))]
        out_shape += [
            jax.ShapeDtypeStruct((2 * maps, n_pixels), bf16),
            jax.ShapeDtypeStruct((8, n_pixels), f32),
        ]
    return pl.pallas_call(
        functools.partial(backward_kernel, first=first),
        grid_spec=pltpu.PrefetchScalarGridSpec(
            num_scalar_prefetch=1,
            grid=(slots // STEP,),
            in_specs=[
                whole(records.shape),
                spec((STEP, maps, 128), lambda i, *_: (i, 0, 0)),
                whole(est.shape),
                whole(sens.shape),
                spec((n_pixels, wide), lambda i, *_: (0, i)),
                spec((n_pixels, wide), lambda i, *_: (0, i)),
            ],
            out_specs=out_specs,
            scratch_shapes=[pltpu.VMEM((maps + (16 if first else 0), n_pixels), f32)],
        ),
        out_shape=out_shape,
        compiler_params=params(56),
        name="backward_product",
    )(tab, records, ratios, est, sens, hi, lo)


def combine(tab, recv, n_out):
    return pl.pallas_call(
        combine_kernel,
        grid_spec=pltpu.PrefetchScalarGridSpec(
            num_scalar_prefetch=1,
            grid=(1,),
            in_specs=[whole(recv.shape)],
            out_specs=whole((n_out,) + recv.shape[1:]),
        ),
        out_shape=jax.ShapeDtypeStruct((n_out,) + recv.shape[1:], f32),
        compiler_params=params(32),
        name="combine_slots",
    )(tab, recv)


def pick(tab, table):
    shape = (tab.shape[0],) + table.shape[1:]
    return pl.pallas_call(
        pick_kernel,
        grid_spec=pltpu.PrefetchScalarGridSpec(
            num_scalar_prefetch=1,
            grid=(1,),
            in_specs=[whole(table.shape)],
            out_specs=whole(shape),
        ),
        out_shape=jax.ShapeDtypeStruct(shape, f32),
        compiler_params=params(32),
        name="pick_slots",
    )(tab, table)


def slot_tables(lists, listed, n_groups, per_group):
    slots = lists.shape[1]
    index = jnp.arange(slots, dtype=jnp.int32)
    live = index[None, :] < listed[:, None]
    group = jnp.where(live, lists // per_group, -1)
    same = (group[:, :, None] == group[:, None, :]) & (index[None, None, :] < index[None, :, None])
    place = jnp.sum(same.astype(jnp.int32), axis=2)
    groups = jnp.arange(n_groups, dtype=jnp.int32)
    hit = (group[:, None, None, :] == groups[None, None, :, None]) & (
        place[:, None, None, :] == jnp.arange(2, dtype=jnp.int32)[None, :, None, None]
    )
    return jnp.sum(jnp.where(hit, lists[:, None, None, :] + 1, 0), axis=3) - 1


def shards(initial_estimate0, clutter, counts, antenna_settings, tile_block_list, tile_block_count):
    maps, rows, cols = initial_estimate0.shape
    n_pixels = rows * cols
    n_row = lax.axis_size("row")
    n_col = lax.axis_size("col")
    row = lax.axis_index("row")
    col = lax.axis_index("col")
    slots = tile_block_list.shape[2]

    record = jnp.zeros((8, 128), f32)
    record = lax.dynamic_update_slice(record, antenna_settings[0], (0, 0))
    meta = jnp.concatenate(
        [tile_block_list.reshape(slots), tile_block_count.reshape(1)]
    ).astype(f32)
    record = lax.dynamic_update_slice(record, meta[None, :], (5, 0))
    mine = lax.all_to_all(jnp.broadcast_to(record, (n_col, 8, 128)), "col", 0, 0, tiled=True)
    every = lax.all_to_all(
        jnp.broadcast_to(mine, (n_row, n_col, 8, 128)), "row", 0, 0, tiled=True
    )
    records = every.reshape(n_row * n_col, 8, 128)
    column_meta = lax.dynamic_index_in_dim(every[:, :, 5, :], col, 1, keepdims=False)
    column_meta = column_meta.astype(jnp.int32)
    tables = slot_tables(column_meta[:, :slots], column_meta[:, slots], n_row, n_col)
    tab = lax.dynamic_index_in_dim(tables, row, 0, keepdims=False).reshape(2 * n_row)
    theirs = lax.dynamic_index_in_dim(tables, row, 2, keepdims=False)
    theirs = jnp.where(theirs >= 0, theirs - row * n_col, -1).T.reshape(2 * n_row)

    origin = jnp.stack([row * rows, col * cols]).astype(jnp.int32)
    est = initial_estimate0.reshape(maps, n_pixels)
    clut = jnp.broadcast_to(clutter.reshape(n_pixels, 1), (n_pixels, 128))
    top = est.astype(bf16)
    est2 = jnp.concatenate([top, (est - top.astype(f32)).astype(bf16)], axis=0)
    sens = jnp.zeros((8, n_pixels), f32)
    wanted = counts[0].astype(f32)

    hi, lo, part = build(tab, origin, records, clut, est2, rows, cols)
    for sweep in range(ITERS):
        if sweep > 0:
            part = forward(tab, records, est2, hi, lo)
        part = part.reshape(2, n_row, maps, 128)
        recv = lax.all_to_all(part, "row", 1, 1, tiled=True)
        group_sum = combine(theirs, recv.reshape(2 * n_row, maps, 128), n_col)
        pieces = lax.all_to_all(group_sum, "col", 0, 0, tiled=True)
        ratio = wanted / jnp.sum(pieces, axis=0)
        table = lax.all_gather(ratio, "col", axis=0, tiled=False)
        sent = pick(theirs, table).reshape(2, n_row, maps, 128)
        back = lax.all_to_all(sent, "row", 1, 1, tiled=True).reshape(2 * n_row, maps, 128)
        if sweep == 0:
            est, est2, sens = backward(tab, records, back, est, sens, hi, lo, True)
        else:
            (est,) = backward(tab, records, back, est, sens, hi, lo, False)
    return est.reshape(maps, rows, cols)


def solution(mesh):
    in_specs = (
        P(None, "row", "col"),
        P("row", "col"),
        P(("row", "col"), None, None),
        P(("row", "col"), None, None),
        P("row", "col", None),
        P("row", "col"),
    )
    out_specs = P(None, "row", "col")
    return jax.shard_map(shards, mesh=mesh, in_specs=in_specs, out_specs=out_specs, check_vma=False)
```

time: 1160 us -> 351 us (0.30)
  the two profiles are of different devices: /device:TPU:24 before, /device:TPU:0 now
where the time goes in v1:
time: 351 us; the launch traced here: 352 us
  Pallas kernels  157 us (45%)
  blocking collectives  127 us (36%)
  waiting for transfers between devices  27.2 us (8%)
  local copies, waits for them, and re-layouts  19.6 us (6%)
  starting transfers between devices  16.1 us (5%)
  other arithmetic  4.2 us (1%)
    pallas_call x2, Pallas kernels, backward(): pl.pallas_call(functools.partial(backward_kernel, first=first), grid_spec...  74.9 us
    pallas_call x1, Pallas kernels, build(): pl.pallas_call(functools.partial(build_kernel, rows=rows, cols=cols), gri...  55.6 us
    all_to_all x2, blocking collectives, shards(): lax.all_to_all(sent, 'row', 1, 1, tiled=True).reshape(2 * n_row, maps, 128)  52.9 us
    all_gather x2, blocking collectives, shards(): table = lax.all_gather(ratio, 'col', axis=0, tiled=False)  26 us
    all_to_all x1, blocking collectives, shards(): recv = lax.all_to_all(part, 'row', 1, 1, tiled=True)  25.4 us
    all_to_all x2, blocking collectives, shards(): pieces = lax.all_to_all(group_sum, 'col', 0, 0, tiled=True)  22.7 us
    pallas_call x1, Pallas kernels, forward(): pl.pallas_call(forward_kernel, grid_spec=pltpu.PrefetchScalarGridSpec(num...  22.5 us
    all_to_all x1, waiting for transfers between devices, shards(): recv = lax.all_to_all(part, 'row', 1, 1, tiled=True)  15.8 us
  transfers between devices with their start and end apart: 3, of which 3 were waited for; matrix products, arithmetic and copies ran while one was open for 1% of the time, Pallas kernels for 0%

profile of v1, /device:TPU:0, one launch (start us, length us, event | category | flops | bytes accessed | tf_op | source)
XLA Modules:
  0.0 352.0 jit_solution(340279946864468128)
XLA Ops:
  2.8 4.6 %all-to-all-start = ((f32[8,8,128]{2,1,0:T(8,128)}), f32[8,8,128]{2,1,0:T(8,128)S(1)}, u32[]{:S(2)}, u32[]{:S(2)}) async-start(f32[8,8,128]{2,1,0:T(8,128)} %broadcast_in_dim.28), calls=%async_computation | async-start | bytes 65536 | tf_op jit(solution)/shard_map/all_to_all | solution.py:321
  7.3 2.5 copy.42
  11.0 1.8 all-to-all-done
  13.7 7.9 %all-to-all-start.1 = ((f32[16,8,8,128]{3,2,1,0:T(8,128)}), f32[16,8,8,128]{3,2,1,0:T(8,128)S(1)}, u32[]{:S(2)}, u32[]{:S(2)}) async-start(f32[16,8,8,128]{3,2,1,0:T(8,128)} %broadcast_in_dim.29), calls=%async_computation.1 | async-start | bytes 1048576 | tf_op jit(solution)/shard_map/all_to_all | solution.py:322
  23.4 9.6 %all-to-all-done.1 = f32[16,8,8,128]{3,2,1,0:T(8,128)S(1)} async-done(((f32[16,8,8,128]{3,2,1,0:T(8,128)}), f32[16,8,8,128]{3,2,1,0:T(8,128)S(1)}, u32[]{:S(2)}, u32[]{:S(2)}) %all-to-all-start.1) | async-done | bytes 524320 | tf_op jit(solution)/shard_map/all_to_all | solution.py:322
  35.1 2.0 broadcast_in_dim.52.clut
  37.1 55.6 %build_cover.1 = (bf16[4096,4096]{1,0:T(8,128)(2,1)}, f8e5m2[4096,4096]{1,0:T(32,128)(4,1)}, f32[32,96,128]{2,1,0:T(8,128)}) custom-call(s32[32]{0:T(128)} %reshape.118.tab, s32[2]{0:T(128)} %pad_add_fusion.origin, f32[128,8,128]{2,1,0:T(8,128)} %bitcast.35, f32[4096,128]{1,0:T(8,128)} %broadcast_in_dim.52.clut, bf16[192,4096]{1,0:T(8,128)(2,1)} %pad_maximum_fusion.est2), custom_call_target="tpu_custom_call" | custom-call | tf_op jit(solution)/shard_map/build_cover/pallas_call | solution.py:181
  92.7 2.7 copy.32
  95.4 3.7 %all-to-all-start.2 = ((f32[2,16,96,128]{3,2,0,1:T(8,128)}), f32[2,16,96,128]{3,2,0,1:T(8,128)S(1)}, u32[]{:S(2)}, u32[]{:S(2)}) async-start(f32[2,16,96,128]{3,2,0,1:T(8,128)} %copy.32), calls=%async_computation.2 | async-start | bytes 3145728 | tf_op jit(solution)/shard_map/all_to_all | solution.py:346
  99.4 15.8 %all-to-all-done.2 = f32[2,16,96,128]{3,2,0,1:T(8,128)S(1)} async-done(((f32[2,16,96,128]{3,2,0,1:T(8,128)}), f32[2,16,96,128]{3,2,0,1:T(8,128)S(1)}, u32[]{:S(2)}, u32[]{:S(2)}) %all-to-all-start.2) | async-done | bytes 1572896 | tf_op jit(solution)/shard_map/all_to_all | solution.py:346
  116.5 11.3 %all_to_all.40 = f32[8,96,128]{2,1,0:T(8,128)S(1)} all-to-all(f32[8,96,128]{2,1,0:T(8,128)S(1)} %combine_slots.2), channel_id=1, replica_groups=mesh['row'=16,'col'=8] {'col'}, dimensions={0} | all-to-all | bytes 786432 | tf_op jit(solution)/shard_map/all_to_all | solution.py:348
  127.9 13.0 %all_gather.8.table = f32[8,96,128]{2,1,0:T(8,128)S(1)} all-gather(f32[1,96,128]{2,1,0:T(8,128)S(1)} %bitcast_divide_fusion.1), channel_id=1, replica_groups=mesh['row'=16,'col'=8] {'col'}, dimensions={0}, use_global_device_ids=true | all-gather | bytes 442368 | tf_op jit(solution)/shard_map/all_gather | solution.py:350
  141.8 26.5 %all_to_all.41 = f32[2,16,96,128]{3,2,0,1:T(8,128)S(1)} all-to-all(f32[2,16,96,128]{3,2,0,1:T(8,128)S(1)} %copy.34), channel_id=1, replica_groups=mesh['row'=16,'col'=8] {'row'}, dimensions={1} | all-to-all | bytes 3145728 | tf_op jit(solution)/shard_map/all_to_all | solution.py:352
  168.3 1.3 copy.35
  170.2 37.7 %backward_product.2 = (f32[96,4096]{1,0:T(8,128)}, bf16[192,4096]{1,0:T(8,128)(2,1)}, f32[8,4096]{1,0:T(8,128)}) custom-call(s32[32]{0:T(128)} %reshape.118.tab, f32[128,8,128]{2,1,0:T(8,128)} %bitcast.36, f32[32,96,128]{2,1,0:T(8,128)} %bitcast.40, f32[96,4096]{1,0:T(8,128)} %bitcast.34, f32[8,4096]{1,0:T(8,128)} %broadcast_in_dim.53.sens_in, ...), custom_call_target="tpu_custom_call" | custom-call | tf_op jit(solution)/shard_map/backward_product/pallas_call | solution.py:239
  207.9 22.5 %forward_product.1 = f32[32,96,128]{2,1,0:T(8,128)} custom-call(s32[32]{0:T(128)} %reshape.118.tab, f32[128,8,128]{2,1,0:T(8,128)} %bitcast.37, bf16[192,4096]{1,0:T(8,128)(2,1)} %get-tuple-element.14.est2, bf16[4096,4096]{1,0:T(8,128)(2,1)} %get-tuple-element.12.hi, f8e5m2[4096,4096]{1,0:T(32,128)(4,1)} %get-tuple-element.13.lo), custom_call_target="tpu_custom_call" | custom-call | tf_op jit(solution)/shard_map/forward_product/pallas_call | solution.py:208
  230.4 1.5 copy.36
  232.0 25.4 %all_to_all.42 = f32[2,16,96,128]{3,2,0,1:T(8,128)S(1)} all-to-all(f32[2,16,96,128]{3,2,0,1:T(8,128)S(1)} %copy.36), channel_id=1, replica_groups=mesh['row'=16,'col'=8] {'row'}, dimensions={1} | all-to-all | bytes 3145728 | tf_op jit(solution)/shard_map/all_to_all | solution.py:346
  258.6 11.4 %all_to_all.43 = f32[8,96,128]{2,1,0:T(8,128)S(1)} all-to-all(f32[8,96,128]{2,1,0:T(8,128)S(1)} %combine_slots.3), channel_id=1, replica_groups=mesh['row'=16,'col'=8] {'col'}, dimensions={0} | all-to-all | bytes 786432 | tf_op jit(solution)/shard_map/all_to_all | solution.py:348
  270.1 13.0 %all_gather.9.table = f32[8,96,128]{2,1,0:T(8,128)S(1)} all-gather(f32[1,96,128]{2,1,0:T(8,128)S(1)} %bitcast_divide_fusion), channel_id=1, replica_groups=mesh['row'=16,'col'=8] {'col'}, dimensions={0}, use_global_device_ids=true | all-gather | bytes 442368 | tf_op jit(solution)/shard_map/all_gather | solution.py:350
  284.0 26.5 %all_to_all.44 = f32[2,16,96,128]{3,2,0,1:T(8,128)S(1)} all-to-all(f32[2,16,96,128]{3,2,0,1:T(8,128)S(1)} %copy.38), channel_id=1, replica_groups=mesh['row'=16,'col'=8] {'row'}, dimensions={1} | all-to-all | bytes 3145728 | tf_op jit(solution)/shard_map/all_to_all | solution.py:352
  310.5 1.3 copy.39
  311.8 37.2 %backward_product.3 = f32[96,4096]{1,0:T(8,128)} custom-call(s32[32]{0:T(128)} %reshape.118.tab, f32[128,8,128]{2,1,0:T(8,128)} %bitcast.38, f32[32,96,128]{2,1,0:T(8,128)} %bitcast.39, f32[96,4096]{1,0:T(8,128)} %get-tuple-element.15.est, f32[8,4096]{1,0:T(8,128)} %get-tuple-element.16.sens_in, bf16[4096,4096]{1,0:T(8,128)(2,1)} %get-tuple-element.12.hi, ...), custom_call_target="tpu_custom_call" | custom-call | tf_op jit(solution)/shard_map/backward_product/pallas_call | solution.py:239
  349.0 3.0 copy.43
  (46 shorter events, 13.5 us)
Async XLA Ops:
  2.8 10.0 %all-to-all-start = ((f32[8,8,128]{2,1,0:T(8,128)}), f32[8,8,128]{2,1,0:T(8,128)S(1)}, u32[]{:S(2)}, u32[]{:S(2)}) async-start(f32[8,8,128]{2,1,0:T(8,128)} %broadcast_in_dim.28), calls=%async_computation | async-start | bytes 65536 | tf_op jit(solution)/shard_map/all_to_all | solution.py:321
  9.9 1.2 copy-start
  11.0 11.1 %copy-start.3 = (f32[16,256]{1,0:T(8,128)S(1)}, f32[16,256]{1,0:T(8,128)}, u32[]{:S(2)}) copy-start(f32[16,256]{1,0:T(8,128)} %param.7) | copy-start | bytes 49156
  13.7 19.3 %all-to-all-start.1 = ((f32[16,8,8,128]{3,2,1,0:T(8,128)}), f32[16,8,8,128]{3,2,1,0:T(8,128)S(1)}, u32[]{:S(2)}, u32[]{:S(2)}) async-start(f32[16,8,8,128]{3,2,1,0:T(8,128)} %broadcast_in_dim.29), calls=%async_computation.1 | async-start | bytes 1048576 | tf_op jit(solution)/shard_map/all_to_all | solution.py:322
  33.0 4.1 %copy-start.1 = (f32[16,8,8,128]{3,2,1,0:T(8,128)}, f32[16,8,8,128]{3,2,1,0:T(8,128)S(1)}, u32[]{:S(2)}) copy-start(f32[16,8,8,128]{3,2,1,0:T(8,128)S(1)} %all-to-all-done.1) | copy-start | bytes 1572868
  95.4 19.8 %all-to-all-start.2 = ((f32[2,16,96,128]{3,2,0,1:T(8,128)}), f32[2,16,96,128]{3,2,0,1:T(8,128)S(1)}, u32[]{:S(2)}, u32[]{:S(2)}) async-start(f32[2,16,96,128]{3,2,0,1:T(8,128)} %copy.32), calls=%async_computation.2 | async-start | bytes 3145728 | tf_op jit(solution)/shard_map/all_to_all | solution.py:346
  115.3 12.5 %copy-start.2 = (s32[1,96,128]{2,1,0:T(8,128)S(1)}, s32[1,96,128]{2,1,0:T(8,128)}, u32[]{:S(2)}) copy-start(s32[1,96,128]{2,1,0:T(8,128)} %param.8) | copy-start | bytes 147460

commit v2 on v1

v2 whole, which is shorter than its diff:
```python
import functools
import jax
import jax.numpy as jnp
from jax import lax
from jax.experimental import pallas as pl
from jax.experimental.pallas import tpu as pltpu
from jax.sharding import PartitionSpec as P

ITERS = 2
LOG2E = 1.4426950408889634
CLUTTER_MAX = 1.5
STEP = 4
STORE = 65536.0
INV_MAX = 1e37
SENS_ROWS = 16
LO_TYPE = jnp.float8_e5m2
BIG = 1e38
f32 = jnp.float32
bf16 = jnp.bfloat16


def split(x):
    hi = x.astype(bf16)
    return hi, (x - hi.astype(f32)).astype(bf16)


def antenna_scale(record):
    peak = jnp.exp2(jnp.maximum(record[4:5, :] * (-LOG2E * CLUTTER_MAX), 0.0))
    return record[3:4, :] * (peak * (1.0 / STORE))


def any_live(tab, step):
    live = tab[step * STEP] >= 0
    for k in range(1, STEP):
        live = jnp.logical_or(live, tab[step * STEP + k] >= 0)
    return live


def build_kernel(tab, origin, records, clut, est, hi, lo, part, *rest, rows, cols, first):
    step = pl.program_id(0)
    maps = part.shape[1]
    if first:
        est2, across = rest

        @pl.when(step == 0)
        def _():
            top, remainder = split(est[...])
            est2[:maps, :] = top
            est2[maps:, :] = remainder
    else:
        (across,) = rest
        est2 = est

    @pl.when(any_live(tab, step))
    def _():
        for k in range(STEP):
            block = tab[step * STEP + k]
            live = block >= 0
            record = records[jnp.maximum(block, 0)]
            slope = jnp.where(live, record[4:5, :] * (-LOG2E), 0.0)
            peak = jnp.exp2(jnp.maximum(slope * CLUTTER_MAX, 0.0)) * (1.0 / STORE)
            inv = jnp.minimum(1.0 / (record[2:3, :] * record[2:3, :]), INV_MAX) * peak
            inv = jnp.where(live, inv, 0.0)
            peak = jnp.where(live, peak, jnp.inf)
            down = (
                origin[0] + lax.broadcasted_iota(jnp.int32, (rows, 128), 0)
            ).astype(f32) + (0.5 - record[0:1, :])
            down = peak + down * down * inv
            stack = [down, inv, record[1:2, :], slope, jnp.zeros((125 - rows, 128), f32)]
            turned = jnp.concatenate(stack, axis=0).T
            column = (
                origin[1] + lax.broadcasted_iota(jnp.int32, (1, cols), 1)
            ).astype(f32) + 0.5
            gap = column - turned[:, rows + 1 : rows + 2]
            across[k] = gap * gap * turned[:, rows : rows + 1]
            size = 32
            for a in range(0, 128, size):
                tilt = jnp.broadcast_to(turned[a : a + size, rows + 2 : rows + 3], (size, cols))
                side = across[k, a : a + size, :]
                at = slice(k * 128 + a, k * 128 + a + size)
                for r in range(rows):
                    den = side + turned[a : a + size, r : r + 1]
                    value = jnp.exp2(clut[r : r + 1, :] * tilt) / den
                    top = value.astype(bf16)
                    hi[at, r * cols : (r + 1) * cols] = top
                    lo[at, r * cols : (r + 1) * cols] = (value - top.astype(f32)).astype(LO_TYPE)
        forward_dot(tab, step, records, est2, hi, part, maps)


def forward_dot(tab, step, records, est2, hi, part, maps):
    both = lax.dot_general(
        est2[...], hi[...], (((1,), (1,)), ((), ())), preferred_element_type=f32
    )
    total = both[:maps, :] + both[maps:, :]
    for k in range(STEP):
        scale = antenna_scale(records[jnp.maximum(tab[step * STEP + k], 0)])
        part[k] = total[:, k * 128 : (k + 1) * 128] * scale


def forward_kernel(tab, records, est2, hi, part):
    step = pl.program_id(0)

    @pl.when(any_live(tab, step))
    def _():
        forward_dot(tab, step, records, est2, hi, part, part.shape[1])


def backward_kernel(tab, records, ratios, carry, est, hi, lo, *rest, start, last, sweep):
    step = pl.program_id(0)
    maps, n_pixels = est.shape
    if last and sweep == 0:
        est_out, est2_out, sens_out, acc = rest
    elif last:
        sens_in, est_out, acc = rest
    else:
        (acc,) = rest

    @pl.when(step == 0)
    def _():
        if start:
            acc[...] = jnp.zeros_like(acc)
        else:
            acc[...] = carry[...]

    @pl.when(any_live(tab, step))
    def _():
        wide = []
        thin = []
        for k in range(STEP):
            block = tab[step * STEP + k]
            live = block >= 0
            scale = antenna_scale(records[jnp.maximum(block, 0)])
            stack = jnp.where(live, ratios[k] * scale, 0.0)
            if sweep == 0:
                ones = jnp.where(live, jnp.broadcast_to(scale, (SENS_ROWS, 128)), 0.0)
                stack = jnp.concatenate([stack, ones], axis=0)
            top, remainder = split(stack)
            wide.append(jnp.concatenate([top, remainder], axis=0))
            thin.append(top)
        wide = jnp.concatenate(wide, axis=1)
        thin = jnp.concatenate(thin, axis=1)
        height = thin.shape[0]
        chunk = 512
        for at in range(0, n_pixels, chunk):
            both = jnp.dot(wide, hi[:, at : at + chunk], preferred_element_type=f32)
            low = jnp.dot(thin, lo[:, at : at + chunk], preferred_element_type=f32)
            acc[:, at : at + chunk] += both[:height, :] + (both[height:, :] + low)

    if last:

        @pl.when(step == pl.num_programs(0) - 1)
        def _():
            if sweep == 0:
                sens = acc[maps : maps + 1, :]
                sens_out[...] = jnp.broadcast_to(sens, sens_out.shape)
            else:
                sens = sens_in[0:1, :]
            new = est[...] * acc[:maps, :] / sens
            est_out[...] = new
            if sweep == 0:
                top, remainder = split(new)
                est2_out[:maps, :] = top
                est2_out[maps:, :] = remainder


def combine_kernel(tab, recv0, recv1, out):
    out[...] = jnp.zeros_like(out)
    half = recv0.shape[0]
    for j, recv in enumerate((recv0, recv1)):

        @pl.loop(0, half)
        def _(i):
            local = tab[j * half + i]

            @pl.when(local >= 0)
            def _():
                out[local] = out[local] + recv[i]


def pick_kernel(tab, table, out0, out1):
    half = out0.shape[0]

    @pl.loop(0, half)
    def _(i):
        out0[i] = table[jnp.maximum(tab[i], 0)]
        out1[i] = table[jnp.maximum(tab[half + i], 0)]


def params(mib):
    return pltpu.CompilerParams(vmem_limit_bytes=mib << 20)


def spec(shape, index):
    return pl.BlockSpec(shape, index)


def whole(shape):
    return pl.BlockSpec(shape, lambda *_: (0,) * len(shape))


def build(tab, origin, records, clut, est, maps, rows, cols, first):
    slots = tab.shape[0]
    n_pixels = rows * cols
    tall = STEP * 128
    out_specs = [
        spec((tall, n_pixels), lambda i, *_: (i, 0)),
        spec((tall, n_pixels), lambda i, *_: (i, 0)),
        spec((STEP, maps, 128), lambda i, *_: (i, 0, 0)),
    ]
    out_shape = [
        jax.ShapeDtypeStruct((slots * 128, n_pixels), bf16),
        jax.ShapeDtypeStruct((slots * 128, n_pixels), LO_TYPE),
        jax.ShapeDtypeStruct((slots, maps, 128), f32),
    ]
    if first:
        out_specs.append(whole((2 * maps, n_pixels)))
        out_shape.append(jax.ShapeDtypeStruct((2 * maps, n_pixels), bf16))
    return pl.pallas_call(
        functools.partial(build_kernel, rows=rows, cols=cols, first=first),
        grid_spec=pltpu.PrefetchScalarGridSpec(
            num_scalar_prefetch=2,
            grid=(slots // STEP,),
            in_specs=[whole(records.shape), whole(clut.shape), whole(est.shape)],
            out_specs=out_specs,
            scratch_shapes=[pltpu.VMEM((STEP, 128, cols), f32)],
        ),
        out_shape=out_shape,
        compiler_params=params(56),
        name="build_cover",
    )(tab, origin, records, clut, est)


def forward(tab, records, est2, hi):
    slots = tab.shape[0]
    maps2, n_pixels = est2.shape
    maps = maps2 // 2
    tall = STEP * 128
    return pl.pallas_call(
        forward_kernel,
        grid_spec=pltpu.PrefetchScalarGridSpec(
            num_scalar_prefetch=1,
            grid=(slots // STEP,),
            in_specs=[
                whole(records.shape),
                whole(est2.shape),
                spec((tall, n_pixels), lambda i, *_: (i, 0)),
            ],
            out_specs=spec((STEP, maps, 128), lambda i, *_: (i, 0, 0)),
        ),
        out_shape=jax.ShapeDtypeStruct((slots, maps, 128), f32),
        compiler_params=params(56),
        name="forward_product",
    )(tab, records, est2, hi)


def backward(tab, records, ratios, carry, est, hi, lo, sens, start, last, sweep):
    slots = tab.shape[0]
    maps, n_pixels = est.shape
    tall = STEP * 128
    height = maps + (SENS_ROWS if sweep == 0 else 0)
    if carry is None:
        carry = jnp.zeros((8, 128), f32)
    operands = [records, ratios, carry, est, hi, lo]
    in_specs = [
        whole(records.shape),
        spec((STEP, maps, 128), lambda i, *_: (i, 0, 0)),
        whole(carry.shape),
        whole(est.shape),
        spec((tall, n_pixels), lambda i, *_: (i, 0)),
        spec((tall, n_pixels), lambda i, *_: (i, 0)),
    ]
    scratch = [pltpu.VMEM((height, n_pixels), f32)]
    if not last:
        out_specs = [whole((height, n_pixels))]
        out_shape = [jax.ShapeDtypeStruct((height, n_pixels), f32)]
        scratch = []
    else:
        out_specs = [whole((maps, n_pixels))]
        out_shape = [jax.ShapeDtypeStruct((maps, n_pixels), f32)]
        if sweep == 0:
            out_specs += [whole((2 * maps, n_pixels)), whole((8, n_pixels))]
            out_shape += [
                jax.ShapeDtypeStruct((2 * maps, n_pixels), bf16),
                jax.ShapeDtypeStruct((8, n_pixels), f32),
            ]
        else:
            operands.append(sens)
            in_specs.append(whole(sens.shape))
    return pl.pallas_call(
        functools.partial(backward_kernel, start=start, last=last, sweep=sweep),
        grid_spec=pltpu.PrefetchScalarGridSpec(
            num_scalar_prefetch=1,
            grid=(slots // STEP,),
            in_specs=in_specs,
            out_specs=out_specs,
            scratch_shapes=scratch,
        ),
        out_shape=out_shape,
        compiler_params=params(56),
        name="backward_product",
    )(tab, *operands)


def combine(tab, recv0, recv1, n_out):
    return pl.pallas_call(
        combine_kernel,
        grid_spec=pltpu.PrefetchScalarGridSpec(
            num_scalar_prefetch=1,
            grid=(1,),
            in_specs=[whole(recv0.shape), whole(recv1.shape)],
            out_specs=whole((n_out,) + recv0.shape[1:]),
        ),
        out_shape=jax.ShapeDtypeStruct((n_out,) + recv0.shape[1:], f32),
        compiler_params=params(32),
        name="combine_slots",
    )(tab, recv0, recv1)


def pick(tab, table):
    shape = (tab.shape[0] // 2,) + table.shape[1:]
    return pl.pallas_call(
        pick_kernel,
        grid_spec=pltpu.PrefetchScalarGridSpec(
            num_scalar_prefetch=1,
            grid=(1,),
            in_specs=[whole(table.shape)],
            out_specs=[whole(shape), whole(shape)],
        ),
        out_shape=[jax.ShapeDtypeStruct(shape, f32)] * 2,
        compiler_params=params(32),
        name="pick_slots",
    )(tab, table)


def slot_tables(lists, listed, n_groups, per_group):
    slots = lists.shape[1]
    index = jnp.arange(slots, dtype=jnp.int32)
    live = index[None, :] < listed[:, None]
    group = jnp.where(live, lists // per_group, -1)
    same = (group[:, :, None] == group[:, None, :]) & (index[None, None, :] < index[None, :, None])
    place = jnp.sum(same.astype(jnp.int32), axis=2)
    groups = jnp.arange(n_groups, dtype=jnp.int32)
    hit = (group[:, None, None, :] == groups[None, None, :, None]) & (
        place[:, None, None, :] == jnp.arange(2, dtype=jnp.int32)[None, :, None, None]
    )
    return jnp.sum(jnp.where(hit, lists[:, None, None, :] + 1, 0), axis=3) - 1


def shards(initial_estimate0, clutter, counts, antenna_settings, tile_block_list, tile_block_count):
    maps, rows, cols = initial_estimate0.shape
    n_pixels = rows * cols
    n_row = lax.axis_size("row")
    n_col = lax.axis_size("col")
    row = lax.axis_index("row")
    col = lax.axis_index("col")
    slots = tile_block_list.shape[2]

    record = jnp.zeros((8, 128), f32)
    record = lax.dynamic_update_slice(record, antenna_settings[0], (0, 0))
    meta = jnp.concatenate(
        [tile_block_list.reshape(slots), tile_block_count.reshape(1)]
    ).astype(f32)
    record = lax.dynamic_update_slice(record, meta[None, :], (5, 0))
    mine = lax.all_to_all(jnp.broadcast_to(record, (n_col, 8, 128)), "col", 0, 0, tiled=True)
    every = lax.all_to_all(
        jnp.broadcast_to(mine, (n_row, n_col, 8, 128)), "row", 0, 0, tiled=True
    )
    records = every.reshape(n_row * n_col, 8, 128)
    column_meta = lax.dynamic_index_in_dim(every[:, :, 5, :], col, 1, keepdims=False)
    column_meta = column_meta.astype(jnp.int32)
    tables = slot_tables(column_meta[:, :slots], column_meta[:, slots], n_row, n_col)
    tab = lax.dynamic_index_in_dim(tables, row, 0, keepdims=False).reshape(2 * n_row)
    theirs = lax.dynamic_index_in_dim(tables, row, 2, keepdims=False)
    theirs = jnp.where(theirs >= 0, theirs - row * n_col, -1).T.reshape(2 * n_row)

    origin = jnp.stack([row * rows, col * cols]).astype(jnp.int32)
    est = initial_estimate0.reshape(maps, n_pixels)
    wanted = counts[0].astype(f32)
    tabs = (tab[:n_row], tab[n_row:])

    hi0, lo0, part0, est2 = build(
        tabs[0], origin, records, clutter, est, maps, rows, cols, True
    )
    recv0 = lax.all_to_all(part0, "row", 0, 0, tiled=True)
    hi1, lo1, part1 = build(tabs[1], origin, records, clutter, est2, maps, rows, cols, False)
    recv1 = lax.all_to_all(part1, "row", 0, 0, tiled=True)
    sens = None
    for sweep in range(ITERS):
        if sweep > 0:
            part0 = forward(tabs[0], records, est2, hi0)
            recv0 = lax.all_to_all(part0, "row", 0, 0, tiled=True)
            part1 = forward(tabs[1], records, est2, hi1)
            recv1 = lax.all_to_all(part1, "row", 0, 0, tiled=True)
        group_sum = combine(theirs, recv0, recv1, n_col)
        pieces = lax.all_to_all(group_sum, "col", 0, 0, tiled=True)
        ratio = wanted / jnp.sum(pieces, axis=0)
        table = lax.all_gather(ratio, "col", axis=0, tiled=False)
        sent0, sent1 = pick(theirs, table)
        back0 = lax.all_to_all(sent0, "row", 0, 0, tiled=True)
        back1 = lax.all_to_all(sent1, "row", 0, 0, tiled=True)
        (carry,) = backward(
            tabs[0], records, back0, None, est, hi0, lo0, sens, True, False, sweep
        )
        done = backward(
            tabs[1], records, back1, carry, est, hi1, lo1, sens, False, True, sweep
        )
        if sweep == 0:
            est, est2, sens = done
        else:
            (est,) = done
    return est.reshape(maps, rows, cols)


def solution(mesh):
    in_specs = (
        P(None, "row", "col"),
        P("row", "col"),
        P(("row", "col"), None, None),
        P(("row", "col"), None, None),
        P("row", "col", None),
        P("row", "col"),
    )
    out_specs = P(None, "row", "col")
    return jax.shard_map(shards, mesh=mesh, in_specs=in_specs, out_specs=out_specs, check_vma=False)
```

time: 351 us -> 308 us (0.88); the launches traced: 352 us -> 303 us
  Pallas kernels: 157 us -> 104 us
  starting transfers between devices: 16.1 us -> 36.4 us
  local copies, waits for them, and re-layouts: 19.6 us -> 10.3 us
  blocking collectives: 127 us -> 121 us
    pallas_call x3 -> x6, Pallas kernels: 131 us -> 81.1 us  [the longest x4 51.6 us: backward(): pl.pallas_call(functools.partial(backward_kernel, start=start, last=last,...]
    all_to_all x2 -> x5, starting transfers between devices: 8.26 us -> 28.5 us  [the longest x2 15.5 us: shards(): recv0 = lax.all_to_all(part0, 'row', 0, 0, tiled=True)]
    all_to_all x3 -> x4, blocking collectives: 78.3 us -> 62.7 us  [the longest x2 36.5 us: shards(): back0 = lax.all_to_all(sent0, 'row', 0, 0, tiled=True)]
    all_to_all x2, blocking collectives: 22.7 us -> 32 us  [shards(): pieces = lax.all_to_all(group_sum, 'col', 0, 0, tiled=True)]
    reshape x5 -> x0, local copies, waits for them, and re-layouts: 5.05 us -> none  [the longest x2 4.21 us: shards(): part = part.reshape(2, n_row, maps, 128)]
    pallas_call x1 -> x2, Pallas kernels: 22.5 us -> 17.9 us  [forward(): pl.pallas_call(forward_kernel, grid_spec=pltpu.PrefetchScalarGridSpec(num...]
    all_to_all x2 -> x5, waiting for transfers between devices: 17.6 us -> 18.9 us  [the longest x1 11.6 us: shards(): recv1 = lax.all_to_all(part1, 'row', 0, 0, tiled=True)]
    unnamed x12 -> x13, local copies, waits for them, and re-layouts: 7.18 us -> 7.75 us
  transfers between devices with their start and end apart: 3 -> 6, of which waited for: 3 -> 5; matrix products, arithmetic and copies ran while one was open for 1% -> 1% of each run, Pallas kernels for 0% -> 15%
where the time goes in v2:
time: 308 us; the launch traced here: 303 us
  blocking collectives  121 us (39%)
  Pallas kernels  104 us (34%)
  starting transfers between devices  36.4 us (12%)
  waiting for transfers between devices  27.4 us (9%)
  local copies, waits for them, and re-layouts  10.3 us (3%)
    pallas_call x4, Pallas kernels, backward(): pl.pallas_call(functools.partial(backward_kernel, start=start, last=last,...  51.6 us
    all_to_all x2, blocking collectives, shards(): back0 = lax.all_to_all(sent0, 'row', 0, 0, tiled=True)  36.5 us
    all_to_all x2, blocking collectives, shards(): pieces = lax.all_to_all(group_sum, 'col', 0, 0, tiled=True)  32 us
    pallas_call x2, Pallas kernels, build(): pl.pallas_call(functools.partial(build_kernel, rows=rows, cols=cols, firs...  29.6 us
    all_gather x2, blocking collectives, shards(): table = lax.all_gather(ratio, 'col', axis=0, tiled=False)  26 us
    pallas_call x2, Pallas kernels, forward(): pl.pallas_call(forward_kernel, grid_spec=pltpu.PrefetchScalarGridSpec(num...  17.9 us
    all_to_all x1, blocking collectives, shards(): recv1 = lax.all_to_all(part1, 'row', 0, 0, tiled=True)  16.3 us
    all_to_all x2, starting transfers between devices, shards(): recv0 = lax.all_to_all(part0, 'row', 0, 0, tiled=True)  15.5 us
  transfers between devices with their start and end apart: 6, of which 5 were waited for; matrix products, arithmetic and copies ran while one was open for 1% of the time, Pallas kernels for 15%

profile of v2, /device:TPU:0, one launch (start us, length us, event | category | flops | bytes accessed | tf_op | source)
XLA Modules:
  0.0 302.9 jit_solution(5495650002498454869)
XLA Ops:
  2.3 9.8 %all_to_all.60 = f32[8,8,128]{2,1,0:T(8,128)S(1)} all-to-all(f32[8,8,128]{2,1,0:T(8,128)S(1)} %broadcast_in_dim.17), channel_id=1, replica_groups=mesh['row'=16,'col'=8] {'col'}, dimensions={0} | all-to-all | bytes 65536 | tf_op jit(solution)/shard_map/all_to_all | solution.py:364
  13.0 7.9 %all-to-all-start.1 = ((f32[16,8,8,128]{3,2,1,0:T(8,128)}), f32[16,8,8,128]{3,2,1,0:T(8,128)S(1)}, u32[]{:S(2)}, u32[]{:S(2)}) async-start(f32[16,8,8,128]{3,2,1,0:T(8,128)} %broadcast_in_dim.18), calls=%async_computation.1 | async-start | bytes 1048576 | tf_op jit(solution)/shard_map/all_to_all | solution.py:365
  23.8 8.5 %all-to-all-done.1 = f32[16,8,8,128]{3,2,1,0:T(8,128)S(1)} async-done(((f32[16,8,8,128]{3,2,1,0:T(8,128)}), f32[16,8,8,128]{3,2,1,0:T(8,128)S(1)}, u32[]{:S(2)}, u32[]{:S(2)}) %all-to-all-start.1) | async-done | bytes 524320 | tf_op jit(solution)/shard_map/all_to_all | solution.py:365
  34.4 18.8 %build_cover.2 = (bf16[2048,4096]{1,0:T(8,128)(2,1)}, f8e5m2[2048,4096]{1,0:T(32,128)(4,1)}, f32[16,96,128]{2,1,0:T(8,128)}, bf16[192,4096]{1,0:T(8,128)(2,1)}) custom-call(s32[16]{0:T(128)} %get-tuple-element.35.tab, s32[2]{0:T(128)} %pad_add_fusion.origin, f32[128,8,128]{2,1,0:T(8,128)} %bitcast.23, f32[16,256]{1,0:T(8,128)} %clut.3, f32[96,4096]{1,0:T(8,128)} %bitcast.31), custom_call_target="tpu_custom_call" | custom-call | tf_op jit(solution)/shard_map/build_cover/pallas_call | solution.py:218
  53.1 5.2 %all-to-all-start.2 = ((f32[16,96,128]{2,1,0:T(8,128)}), f32[16,96,128]{2,1,0:T(8,128)S(1)}, u32[]{:S(2)}, u32[]{:S(2)}) async-start(f32[16,96,128]{2,1,0:T(8,128)} %get-tuple-element.19), calls=%async_computation.2 | async-start | bytes 1572864 | tf_op jit(solution)/shard_map/all_to_all | solution.py:384
  58.4 10.8 %build_cover.3 = (bf16[2048,4096]{1,0:T(8,128)(2,1)}, f8e5m2[2048,4096]{1,0:T(32,128)(4,1)}, f32[16,96,128]{2,1,0:T(8,128)}) custom-call(s32[16]{0:T(128)} %get-tuple-element.36.tab, s32[2]{0:T(128)} %pad_add_fusion.origin, f32[128,8,128]{2,1,0:T(8,128)} %bitcast.24, f32[16,256]{1,0:T(8,128)} %clut.3, bf16[192,4096]{1,0:T(8,128)(2,1)} %get-tuple-element.20.est), custom_call_target="tpu_custom_call" | custom-call | tf_op jit(solution)/shard_map/build_cover/pallas_call | solution.py:218
  70.8 5.6 %all-to-all-start.3 = ((f32[16,96,128]{2,1,0:T(8,128)}), f32[16,96,128]{2,1,0:T(8,128)S(1)}, u32[]{:S(2)}, u32[]{:S(2)}) async-start(f32[16,96,128]{2,1,0:T(8,128)} %get-tuple-element.21), calls=%async_computation.3 | async-start | bytes 1572864 | tf_op jit(solution)/shard_map/all_to_all | solution.py:386
  76.7 11.6 %all-to-all-done.3.recv1 = f32[16,96,128]{2,1,0:T(8,128)S(1)} async-done(((f32[16,96,128]{2,1,0:T(8,128)}), f32[16,96,128]{2,1,0:T(8,128)S(1)}, u32[]{:S(2)}, u32[]{:S(2)}) %all-to-all-start.3) | async-done | bytes 786464 | tf_op jit(solution)/shard_map/all_to_all | solution.py:386
  89.3 16.0 %all_to_all.61 = f32[8,96,128]{2,1,0:T(8,128)S(1)} all-to-all(f32[8,96,128]{2,1,0:T(8,128)S(1)} %combine_slots.2), channel_id=1, replica_groups=mesh['row'=16,'col'=8] {'col'}, dimensions={0} | all-to-all | bytes 786432 | tf_op jit(solution)/shard_map/all_to_all | solution.py:395
  105.4 13.0 %all_gather.8.table = f32[8,96,128]{2,1,0:T(8,128)S(1)} all-gather(f32[1,96,128]{2,1,0:T(8,128)S(1)} %bitcast_divide_fusion.1), channel_id=1, replica_groups=mesh['row'=16,'col'=8] {'col'}, dimensions={0}, use_global_device_ids=true | all-gather | bytes 442368 | tf_op jit(solution)/shard_map/all_gather | solution.py:397
  120.0 18.2 %all_to_all.62.ratios = f32[16,96,128]{2,1,0:T(8,128)} all-to-all(f32[16,96,128]{2,1,0:T(8,128)S(1)} %get-tuple-element.23), channel_id=1, replica_groups=mesh['row'=16,'col'=8] {'row'}, dimensions={0} | all-to-all | bytes 1572864 | tf_op jit(solution)/shard_map/all_to_all | solution.py:399
  138.2 3.8 %all-to-all-start.5 = ((f32[16,96,128]{2,1,0:T(8,128)}), f32[16,96,128]{2,1,0:T(8,128)S(1)}, u32[]{:S(2)}, u32[]{:S(2)}) async-start(f32[16,96,128]{2,1,0:T(8,128)} %get-tuple-element.22), calls=%async_computation.5 | async-start | bytes 1572864 | tf_op jit(solution)/shard_map/all_to_all | solution.py:400
  142.6 13.3 %backward_product.4.carry = f32[112,4096]{1,0:T(8,128)} custom-call(s32[16]{0:T(128)} %get-tuple-element.35.tab, f32[128,8,128]{2,1,0:T(8,128)} %bitcast.25, f32[16,96,128]{2,1,0:T(8,128)} %all_to_all.62.ratios, f32[8,128]{1,0:T(8,128)} %broadcast_1_carry.2.carry, f32[96,4096]{1,0:T(8,128)} %bitcast.32, bf16[2048,4096]{1,0:T(8,128)(2,1)} %get-tuple-element.24.hi, ...), custom_call_target="tpu_custom_call" | custom-call | tf_op jit(solution)/shard_map/backward_product/pallas_call | solution.py:289
  156.8 13.0 %backward_product.5 = (f32[96,4096]{1,0:T(8,128)}, bf16[192,4096]{1,0:T(8,128)(2,1)}, f32[8,4096]{1,0:T(8,128)}) custom-call(s32[16]{0:T(128)} %get-tuple-element.36.tab, f32[128,8,128]{2,1,0:T(8,128)} %bitcast.26, f32[16,96,128]{2,1,0:T(8,128)} %copy-done.2, f32[112,4096]{1,0:T(8,128)} %backward_product.4.carry, f32[96,4096]{1,0:T(8,128)} %bitcast.33, ...), custom_call_target="tpu_custom_call" | custom-call | tf_op jit(solution)/shard_map/backward_product/pallas_call | solution.py:289
  169.8 9.7 %forward_product.2 = f32[16,96,128]{2,1,0:T(8,128)} custom-call(s32[16]{0:T(128)} %get-tuple-element.35.tab, f32[128,8,128]{2,1,0:T(8,128)} %bitcast.27, bf16[192,4096]{1,0:T(8,128)(2,1)} %get-tuple-element.28.est2, bf16[2048,4096]{1,0:T(8,128)(2,1)} %get-tuple-element.24.hi), custom_call_target="tpu_custom_call" | custom-call | tf_op jit(solution)/shard_map/forward_product/pallas_call | solution.py:238
  179.5 10.3 %all-to-all-start.7 = ((f32[16,96,128]{2,1,0:T(8,128)}), f32[16,96,128]{2,1,0:T(8,128)S(1)}, u32[]{:S(2)}, u32[]{:S(2)}) async-start(f32[16,96,128]{2,1,0:T(8,128)} %forward_product.2), calls=%async_computation.7 | async-start | bytes 1572864 | tf_op jit(solution)/shard_map/all_to_all | solution.py:391
  189.9 8.1 %forward_product.3 = f32[16,96,128]{2,1,0:T(8,128)} custom-call(s32[16]{0:T(128)} %get-tuple-element.36.tab, f32[128,8,128]{2,1,0:T(8,128)} %bitcast.28, bf16[192,4096]{1,0:T(8,128)(2,1)} %get-tuple-element.28.est2, bf16[2048,4096]{1,0:T(8,128)(2,1)} %get-tuple-element.26.hi), custom_call_target="tpu_custom_call" | custom-call | tf_op jit(solution)/shard_map/forward_product/pallas_call | solution.py:238
  198.0 5.1 %all-to-all-done.7.recv0 = f32[16,96,128]{2,1,0:T(8,128)S(1)} async-done(((f32[16,96,128]{2,1,0:T(8,128)}), f32[16,96,128]{2,1,0:T(8,128)S(1)}, u32[]{:S(2)}, u32[]{:S(2)}) %all-to-all-start.7) | async-done | bytes 786464 | tf_op jit(solution)/shard_map/all_to_all | solution.py:391
  203.1 16.3 %all_to_all.63.recv1 = f32[16,96,128]{2,1,0:T(8,128)S(1)} all-to-all(f32[16,96,128]{2,1,0:T(8,128)} %forward_product.3), channel_id=1, replica_groups=mesh['row'=16,'col'=8] {'row'}, dimensions={0} | all-to-all | bytes 1572864 | tf_op jit(solution)/shard_map/all_to_all | solution.py:393
  220.5 16.1 %all_to_all.64 = f32[8,96,128]{2,1,0:T(8,128)S(1)} all-to-all(f32[8,96,128]{2,1,0:T(8,128)S(1)} %combine_slots.3), channel_id=1, replica_groups=mesh['row'=16,'col'=8] {'col'}, dimensions={0} | all-to-all | bytes 786432 | tf_op jit(solution)/shard_map/all_to_all | solution.py:395
  236.6 13.0 %all_gather.9.table = f32[8,96,128]{2,1,0:T(8,128)S(1)} all-gather(f32[1,96,128]{2,1,0:T(8,128)S(1)} %bitcast_divide_fusion), channel_id=1, replica_groups=mesh['row'=16,'col'=8] {'col'}, dimensions={0}, use_global_device_ids=true | all-gather | bytes 442368 | tf_op jit(solution)/shard_map/all_gather | solution.py:397
  251.2 18.4 %all_to_all.65.ratios = f32[16,96,128]{2,1,0:T(8,128)} all-to-all(f32[16,96,128]{2,1,0:T(8,128)S(1)} %get-tuple-element.30), channel_id=1, replica_groups=mesh['row'=16,'col'=8] {'row'}, dimensions={0} | all-to-all | bytes 1572864 | tf_op jit(solution)/shard_map/all_to_all | solution.py:399
  273.2 13.1 %backward_product.6.carry = f32[96,4096]{1,0:T(8,128)} custom-call(s32[16]{0:T(128)} %get-tuple-element.35.tab, f32[128,8,128]{2,1,0:T(8,128)} %bitcast.29, f32[16,96,128]{2,1,0:T(8,128)} %all_to_all.65.ratios, f32[8,128]{1,0:T(8,128)} %broadcast_1_carry.2.carry, f32[96,4096]{1,0:T(8,128)} %get-tuple-element.31.est, ...), custom_call_target="tpu_custom_call" | custom-call | tf_op jit(solution)/shard_map/backward_product/pallas_call | solution.py:289
  287.8 12.1 %backward_product.7 = f32[96,4096]{1,0:T(8,128)} custom-call(s32[16]{0:T(128)} %get-tuple-element.36.tab, f32[128,8,128]{2,1,0:T(8,128)} %bitcast.30, f32[16,96,128]{2,1,0:T(8,128)} %copy-done.1, f32[96,4096]{1,0:T(8,128)} %backward_product.6.carry, f32[96,4096]{1,0:T(8,128)} %get-tuple-element.31.est, bf16[2048,4096]{1,0:T(8,128)(2,1)} %get-tuple-element.26.hi, ...), custom_call_target="tpu_custom_call" | custom-call | tf_op jit(solution)/shard_map/backward_product/pallas_call | solution.py:289
  (47 shorter events, 24.3 us)
Async XLA Ops:
  0.0 20.9 %copy-start.3 = (f32[96,16,256]{2,1,0:T(8,128)S(1)}, f32[96,16,256]{2,1,0:T(8,128)}, u32[]{:S(2)}) copy-start(f32[96,16,256]{2,1,0:T(8,128)} %param.6) | copy-start | bytes 4718596
  13.0 19.3 %all-to-all-start.1 = ((f32[16,8,8,128]{3,2,1,0:T(8,128)}), f32[16,8,8,128]{3,2,1,0:T(8,128)S(1)}, u32[]{:S(2)}, u32[]{:S(2)}) async-start(f32[16,8,8,128]{3,2,1,0:T(8,128)} %broadcast_in_dim.18), calls=%async_computation.1 | async-start | bytes 1048576 | tf_op jit(solution)/shard_map/all_to_all | solution.py:365
  32.3 2.1 copy-start
  53.1 17.6 %all-to-all-start.2 = ((f32[16,96,128]{2,1,0:T(8,128)}), f32[16,96,128]{2,1,0:T(8,128)S(1)}, u32[]{:S(2)}, u32[]{:S(2)}) async-start(f32[16,96,128]{2,1,0:T(8,128)} %get-tuple-element.19), calls=%async_computation.2 | async-start | bytes 1572864 | tf_op jit(solution)/shard_map/all_to_all | solution.py:384
  70.8 17.5 %all-to-all-start.3 = ((f32[16,96,128]{2,1,0:T(8,128)}), f32[16,96,128]{2,1,0:T(8,128)S(1)}, u32[]{:S(2)}, u32[]{:S(2)}) async-start(f32[16,96,128]{2,1,0:T(8,128)} %get-tuple-element.21), calls=%async_computation.3 | async-start | bytes 1572864 | tf_op jit(solution)/shard_map/all_to_all | solution.py:386
  76.7 28.7 %copy-start.4 = (s32[1,96,128]{2,1,0:T(8,128)S(1)}, s32[1,96,128]{2,1,0:T(8,128)}, u32[]{:S(2)}) copy-start(s32[1,96,128]{2,1,0:T(8,128)} %param.8) | copy-start | bytes 147460
  138.2 17.7 %all-to-all-start.5 = ((f32[16,96,128]{2,1,0:T(8,128)}), f32[16,96,128]{2,1,0:T(8,128)S(1)}, u32[]{:S(2)}, u32[]{:S(2)}) async-start(f32[16,96,128]{2,1,0:T(8,128)} %get-tuple-element.22), calls=%async_computation.5 | async-start | bytes 1572864 | tf_op jit(solution)/shard_map/all_to_all | solution.py:400
  155.9 0.9 copy-start.2
  179.5 23.6 %all-to-all-start.7 = ((f32[16,96,128]{2,1,0:T(8,128)}), f32[16,96,128]{2,1,0:T(8,128)S(1)}, u32[]{:S(2)}, u32[]{:S(2)}) async-start(f32[16,96,128]{2,1,0:T(8,128)} %forward_product.2), calls=%async_computation.7 | async-start | bytes 1572864 | tf_op jit(solution)/shard_map/all_to_all | solution.py:391
  269.6 17.3 %all-to-all-start.10 = ((f32[16,96,128]{2,1,0:T(8,128)}), f32[16,96,128]{2,1,0:T(8,128)S(1)}, u32[]{:S(2)}, u32[]{:S(2)}) async-start(f32[16,96,128]{2,1,0:T(8,128)} %get-tuple-element.29), calls=%async_computation.10 | async-start | bytes 1572864 | tf_op jit(solution)/shard_map/all_to_all | solution.py:400
  286.9 0.9 copy-start.1

commit v3 on v2

v3 whole, which is shorter than its diff:
```python
import functools
import jax
import jax.numpy as jnp
from jax import lax
from jax.experimental import pallas as pl
from jax.experimental.pallas import tpu as pltpu
from jax.sharding import PartitionSpec as P

ITERS = 2
LOG2E = 1.4426950408889634
CLUTTER_MAX = 1.5
STEP = 4
STORE = 65536.0
INV_MAX = 1e37
SENS_ROWS = 16
LO_TYPE = jnp.float8_e5m2
BIG = 1e38
f32 = jnp.float32
bf16 = jnp.bfloat16


def split(x):
    hi = x.astype(bf16)
    return hi, (x - hi.astype(f32)).astype(bf16)


def wide_pair(x):
    top = lax.reduce_precision(x, 8, 7)
    pair = jnp.stack([top, x - top], axis=1)
    pair = jnp.pad(pair, ((0, 0), (0, 0), (0, 128 - x.shape[1])))
    return pair.reshape(x.shape[0], 256).astype(bf16)


def antenna_scale(record):
    peak = jnp.exp2(jnp.maximum(record[4:5, :] * (-LOG2E * CLUTTER_MAX), 0.0))
    return record[3:4, :] * (peak * (1.0 / STORE))


def any_live(tab, step):
    live = tab[step * STEP] >= 0
    for k in range(1, STEP):
        live = jnp.logical_or(live, tab[step * STEP + k] >= 0)
    return live


def build_kernel(tab, origin, records, clut, est2, *rest, rows, cols):
    hi, lo, part, across = rest[-4:]
    step = pl.program_id(0)
    maps = part.shape[1]

    @pl.when(any_live(tab, step))
    def _():
        for k in range(STEP):
            block = tab[step * STEP + k]
            live = block >= 0
            record = records[jnp.maximum(block, 0)]
            slope = jnp.where(live, record[4:5, :] * (-LOG2E), 0.0)
            peak = jnp.exp2(jnp.maximum(slope * CLUTTER_MAX, 0.0)) * (1.0 / STORE)
            inv = jnp.minimum(1.0 / (record[2:3, :] * record[2:3, :]), INV_MAX) * peak
            inv = jnp.where(live, inv, 0.0)
            peak = jnp.where(live, peak, jnp.inf)
            down = (
                origin[0] + lax.broadcasted_iota(jnp.int32, (rows, 128), 0)
            ).astype(f32) + (0.5 - record[0:1, :])
            down = peak + down * down * inv
            stack = [down, inv, record[1:2, :], slope, jnp.zeros((125 - rows, 128), f32)]
            turned = jnp.concatenate(stack, axis=0).T
            column = (
                origin[1] + lax.broadcasted_iota(jnp.int32, (1, cols), 1)
            ).astype(f32) + 0.5
            gap = column - turned[:, rows + 1 : rows + 2]
            across[k] = gap * gap * turned[:, rows : rows + 1]
            size = 32
            for a in range(0, 128, size):
                tilt = jnp.broadcast_to(turned[a : a + size, rows + 2 : rows + 3], (size, cols))
                side = across[k, a : a + size, :]
                at = slice(k * 128 + a, k * 128 + a + size)
                for r in range(rows):
                    den = side + turned[a : a + size, r : r + 1]
                    value = jnp.exp2(clut[r : r + 1, :] * tilt) / den
                    top = value.astype(bf16)
                    hi[at, r * cols : (r + 1) * cols] = top
                    lo[at, r * cols : (r + 1) * cols] = (value - top.astype(f32)).astype(LO_TYPE)
        forward_dot(tab, step, records, est2, hi, part, maps)


def forward_dot(tab, step, records, est2, hi, part, maps):
    both = jnp.dot(hi[...], est2[...], preferred_element_type=f32)
    total = both[:, :128] + both[:, 128:]
    for k in range(STEP):
        scale = antenna_scale(records[jnp.maximum(tab[step * STEP + k], 0)])
        part[k] = total[k * 128 : (k + 1) * 128, :].T[:maps, :] * scale


def forward_kernel(tab, records, est2, hi, part):
    step = pl.program_id(0)

    @pl.when(any_live(tab, step))
    def _():
        forward_dot(tab, step, records, est2, hi, part.at[:, 0], part.shape[2])


def backward_kernel(tab, records, ratios, est, hi, lo, *rest, sweep):
    step = pl.program_id(0)
    maps, n_pixels = est.shape
    if sweep == 0:
        est_out, est2_out, sens_out, acc = rest
    else:
        sens_in, est_out, acc = rest

    @pl.when(step == 0)
    def _():
        acc[...] = jnp.zeros_like(acc)

    @pl.when(any_live(tab, step))
    def _():
        wide = []
        thin = []
        for k in range(STEP):
            block = tab[step * STEP + k]
            live = block >= 0
            scale = antenna_scale(records[jnp.maximum(block, 0)])
            stack = jnp.where(live, ratios[k, 0] * scale, 0.0)
            if sweep == 0:
                ones = jnp.where(live, jnp.broadcast_to(scale, (SENS_ROWS, 128)), 0.0)
                stack = jnp.concatenate([stack, ones], axis=0)
            top, remainder = split(stack)
            wide.append(jnp.concatenate([top, remainder], axis=0))
            thin.append(top)
        wide = jnp.concatenate(wide, axis=1)
        thin = jnp.concatenate(thin, axis=1)
        height = thin.shape[0]
        chunk = 512
        for at in range(0, n_pixels, chunk):
            both = jnp.dot(wide, hi[:, at : at + chunk], preferred_element_type=f32)
            low = jnp.dot(thin, lo[:, at : at + chunk], preferred_element_type=f32)
            acc[:, at : at + chunk] += both[:height, :] + (both[height:, :] + low)

    @pl.when(step == pl.num_programs(0) - 1)
    def _():
        if sweep == 0:
            sens = acc[maps : maps + 1, :]
            sens_out[...] = jnp.broadcast_to(sens, sens_out.shape)
            new = est[...] * acc[:maps, :] / sens
            est_out[...] = new
            turned = jnp.concatenate([new, jnp.zeros((128 - maps, n_pixels), f32)], axis=0).T
            top, remainder = split(turned)
            est2_out[:, :128] = top
            est2_out[:, 128:] = remainder
        else:
            rows, cols = est_out.shape[1:]
            for r in range(rows):
                at = slice(r * cols, (r + 1) * cols)
                est_out[:, r, :] = est[:, at] * acc[:maps, at] / sens_in[0:1, at]


def combine_kernel(tab, *refs):
    out = refs[-1]
    recv = refs[:-1]
    groups = recv[0].shape[0]
    out[...] = jnp.zeros_like(out)
    for j in range(2):

        @pl.loop(0, groups)
        def _(i):
            local = tab[j * groups + i]

            @pl.when(local >= 0)
            def _():
                piece = recv[j][i] if len(recv) == 2 else recv[0][i, j]
                out[local] = out[local] + piece


def pick_kernel(tab, table, out):
    groups = out.shape[0]

    @pl.loop(0, groups)
    def _(i):
        for j in range(2):
            out[i, j] = table[jnp.maximum(tab[j * groups + i], 0)]


def params(mib):
    return pltpu.CompilerParams(vmem_limit_bytes=mib << 20)


def spec(shape, index):
    return pl.BlockSpec(shape, index)


def whole(shape):
    return pl.BlockSpec(shape, lambda *_: (0,) * len(shape))


def build(tab, origin, records, clut, est2, maps, rows, cols, half, stored):
    slots = tab.shape[0]
    n_pixels = rows * cols
    tall = STEP * 128
    steps = slots // STEP
    operands = [records, clut, est2]
    in_specs = [whole(x.shape) for x in operands]
    aliases = {}
    if half:
        operands += list(stored)
        in_specs += [pl.BlockSpec(memory_space=pl.ANY)] * 2
        aliases = {5: 0, 6: 1}
    return pl.pallas_call(
        functools.partial(build_kernel, rows=rows, cols=cols),
        grid_spec=pltpu.PrefetchScalarGridSpec(
            num_scalar_prefetch=2,
            grid=(steps,),
            in_specs=in_specs,
            out_specs=[
                spec((tall, n_pixels), lambda i, *_: (half * steps + i, 0)),
                spec((tall, n_pixels), lambda i, *_: (half * steps + i, 0)),
                spec((STEP, maps, 128), lambda i, *_: (i, 0, 0)),
            ],
            scratch_shapes=[pltpu.VMEM((STEP, 128, cols), f32)],
        ),
        out_shape=[
            jax.ShapeDtypeStruct((2 * slots * 128, n_pixels), bf16),
            jax.ShapeDtypeStruct((2 * slots * 128, n_pixels), LO_TYPE),
            jax.ShapeDtypeStruct((slots, maps, 128), f32),
        ],
        input_output_aliases=aliases,
        compiler_params=params(56),
        name="build_cover",
    )(tab, origin, *operands)


def place_spec(slots, maps):
    per = slots // 2 // STEP
    return spec((STEP, 1, maps, 128), lambda i, *_: (i % per, i // per, 0, 0))


def forward(tab, records, est2, hi, maps):
    slots = tab.shape[0]
    n_pixels = est2.shape[0]
    tall = STEP * 128
    return pl.pallas_call(
        forward_kernel,
        grid_spec=pltpu.PrefetchScalarGridSpec(
            num_scalar_prefetch=1,
            grid=(slots // STEP,),
            in_specs=[
                whole(records.shape),
                whole(est2.shape),
                spec((tall, n_pixels), lambda i, *_: (i, 0)),
            ],
            out_specs=place_spec(slots, maps),
        ),
        out_shape=jax.ShapeDtypeStruct((slots // 2, 2, maps, 128), f32),
        compiler_params=params(56),
        name="forward_product",
    )(tab, records, est2, hi)


def backward(tab, records, ratios, est, hi, lo, sens, sweep, rows, cols):
    slots = tab.shape[0]
    maps, n_pixels = est.shape
    tall = STEP * 128
    height = maps + (SENS_ROWS if sweep == 0 else 0)
    operands = [records, ratios, est, hi, lo]
    in_specs = [
        whole(records.shape),
        place_spec(slots, maps),
        whole(est.shape),
        spec((tall, n_pixels), lambda i, *_: (i, 0)),
        spec((tall, n_pixels), lambda i, *_: (i, 0)),
    ]
    if sweep == 0:
        shapes = [((maps, n_pixels), f32), ((n_pixels, 256), bf16), ((8, n_pixels), f32)]
    else:
        shapes = [((maps, rows, cols), f32)]
        operands.append(sens)
        in_specs.append(whole(sens.shape))
    return pl.pallas_call(
        functools.partial(backward_kernel, sweep=sweep),
        grid_spec=pltpu.PrefetchScalarGridSpec(
            num_scalar_prefetch=1,
            grid=(slots // STEP,),
            in_specs=in_specs,
            out_specs=[whole(shape) for shape, _ in shapes],
            scratch_shapes=[pltpu.VMEM((height, n_pixels), f32)],
        ),
        out_shape=[jax.ShapeDtypeStruct(shape, dtype) for shape, dtype in shapes],
        compiler_params=params(56),
        name="backward_product",
    )(tab, *operands)


def combine(tab, recv, n_out):
    shape = (n_out,) + recv[0].shape[-2:]
    return pl.pallas_call(
        combine_kernel,
        grid_spec=pltpu.PrefetchScalarGridSpec(
            num_scalar_prefetch=1,
            grid=(1,),
            in_specs=[whole(x.shape) for x in recv],
            out_specs=whole(shape),
        ),
        out_shape=jax.ShapeDtypeStruct(shape, f32),
        compiler_params=params(32),
        name="combine_slots",
    )(tab, *recv)


def pick(tab, table):
    shape = (tab.shape[0] // 2, 2) + table.shape[1:]
    return pl.pallas_call(
        pick_kernel,
        grid_spec=pltpu.PrefetchScalarGridSpec(
            num_scalar_prefetch=1,
            grid=(1,),
            in_specs=[whole(table.shape)],
            out_specs=whole(shape),
        ),
        out_shape=jax.ShapeDtypeStruct(shape, f32),
        compiler_params=params(32),
        name="pick_slots",
    )(tab, table)


def slot_tables(lists, listed, n_groups, per_group):
    slots = lists.shape[1]
    index = jnp.arange(slots, dtype=jnp.int32)
    live = index[None, :] < listed[:, None]
    group = jnp.where(live, lists // per_group, -1)
    same = (group[:, :, None] == group[:, None, :]) & (index[None, None, :] < index[None, :, None])
    place = jnp.sum(same.astype(jnp.int32), axis=2)
    groups = jnp.arange(n_groups, dtype=jnp.int32)
    hit = (group[:, None, None, :] == groups[None, None, :, None]) & (
        place[:, None, None, :] == jnp.arange(2, dtype=jnp.int32)[None, :, None, None]
    )
    return jnp.sum(jnp.where(hit, lists[:, None, None, :] + 1, 0), axis=3) - 1


def shards(initial_estimate0, clutter, counts, antenna_settings, tile_block_list, tile_block_count):
    maps, rows, cols = initial_estimate0.shape
    n_pixels = rows * cols
    n_row = lax.axis_size("row")
    n_col = lax.axis_size("col")
    row = lax.axis_index("row")
    col = lax.axis_index("col")
    slots = tile_block_list.shape[2]

    record = jnp.zeros((8, 128), f32)
    record = lax.dynamic_update_slice(record, antenna_settings[0], (0, 0))
    meta = jnp.concatenate(
        [tile_block_list.reshape(slots), tile_block_count.reshape(1)]
    ).astype(f32)
    record = lax.dynamic_update_slice(record, meta[None, :], (5, 0))
    mine = lax.all_to_all(jnp.broadcast_to(record, (n_col, 8, 128)), "col", 0, 0, tiled=True)
    every = lax.all_to_all(
        jnp.broadcast_to(mine, (n_row, n_col, 8, 128)), "row", 0, 0, tiled=True
    )
    records = every.reshape(n_row * n_col, 8, 128)
    own = slot_tables(
        tile_block_list.reshape(1, slots), tile_block_count.reshape(1), n_row, n_col
    )
    tab = own.reshape(2 * n_row)
    column_meta = lax.dynamic_index_in_dim(every[:, :, 5, :], col, 1, keepdims=False)
    column_meta = column_meta.astype(jnp.int32)
    tables = slot_tables(column_meta[:, :slots], column_meta[:, slots], n_row, n_col)
    theirs = lax.dynamic_index_in_dim(tables, row, 2, keepdims=False)
    theirs = jnp.where(theirs >= 0, theirs - row * n_col, -1).T.reshape(2 * n_row)

    origin = jnp.stack([row * rows, col * cols]).astype(jnp.int32)
    est = initial_estimate0.reshape(maps, n_pixels)
    est2 = wide_pair(initial_estimate0.transpose(1, 2, 0).reshape(n_pixels, maps))
    wanted = counts[0].astype(f32)
    tabs = (tab[:n_row], tab[n_row:])

    hi, lo, part = build(tabs[0], origin, records, clutter, est2, maps, rows, cols, 0, None)
    recv0 = lax.all_to_all(part, "row", 0, 0, tiled=True)
    hi, lo, part = build(tabs[1], origin, records, clutter, est2, maps, rows, cols, 1, (hi, lo))
    recv1 = lax.all_to_all(part, "row", 0, 0, tiled=True)
    recv = (recv0, recv1)
    sens = None
    for sweep in range(ITERS):
        if sweep > 0:
            part = forward(tab, records, est2, hi, maps)
            recv = (lax.all_to_all(part, "row", 0, 0, tiled=True),)
        group_sum = combine(theirs, recv, n_col)
        pieces = lax.all_to_all(group_sum, "col", 0, 0, tiled=True)
        ratio = wanted / jnp.sum(pieces, axis=0)
        table = lax.all_to_all(
            jnp.broadcast_to(ratio, (n_col,) + ratio.shape), "col", 0, 0, tiled=True
        )
        sent = pick(theirs, table)
        back = lax.all_to_all(sent, "row", 0, 0, tiled=True)
        done = backward(tab, records, back, est, hi, lo, sens, sweep, rows, cols)
        if sweep == 0:
            est, est2, sens = done
    return done[0]


def solution(mesh):
    in_specs = (
        P(None, "row", "col"),
        P("row", "col"),
        P(("row", "col"), None, None),
        P(("row", "col"), None, None),
        P("row", "col", None),
        P("row", "col"),
    )
    out_specs = P(None, "row", "col")
    return jax.shard_map(shards, mesh=mesh, in_specs=in_specs, out_specs=out_specs, check_vma=False)
```

time: 308 us -> 285 us (0.925); the launches traced: 303 us -> 283 us
  blocking collectives: 121 us -> 103 us
  waiting for transfers between devices: 27.4 us -> 40.8 us
  Pallas kernels: 104 us -> 91.3 us
  starting transfers between devices: 36.4 us -> 27.8 us
  local copies, waits for them, and re-layouts: 10.3 us -> 14.6 us
    all_gather x2 -> x0, blocking collectives: 26 us -> none  [shards(): table = lax.all_gather(ratio, 'col', axis=0, tiled=False)]
    all_to_all x5 -> x4, waiting for transfers between devices: 18.9 us -> 33.1 us  [the longest x1 19.4 us: shards(): back = lax.all_to_all(sent, 'row', 0, 0, tiled=True)]
    all_to_all x4, blocking collectives: 62.7 us -> 74.1 us  [the longest x1 25.9 us: shards(): back = lax.all_to_all(sent, 'row', 0, 0, tiled=True)]
    pallas_call x6 -> x4, Pallas kernels: 81.1 us -> 71.1 us  [the longest x2 42.7 us: backward(): pl.pallas_call(functools.partial(backward_kernel, sweep=sweep), grid_spec...]
    all_to_all x5 -> x4, starting transfers between devices: 28.5 us -> 19.9 us  [the longest x1 6.54 us: shards(): recv1 = lax.all_to_all(part, 'row', 0, 0, tiled=True)]
    pallas_call x2 -> x1, Pallas kernels: 17.9 us -> 15.5 us  [forward(): pl.pallas_call(forward_kernel, grid_spec=pltpu.PrefetchScalarGridSpec(num...]
    unnamed x13 -> x8, local copies, waits for them, and re-layouts: 7.75 us -> 6.28 us
  transfers between devices with their start and end apart: 6 -> 5, of which waited for: 5 -> 5; matrix products, arithmetic and copies ran while one was open for 1% -> 5% of each run, Pallas kernels for 15% -> 4%
where the time goes in v3:
time: 285 us; the launch traced here: 283 us
  blocking collectives  103 us (36%)
  Pallas kernels  91.3 us (32%)
  waiting for transfers between devices  40.8 us (14%)
  starting transfers between devices  27.8 us (10%)
  local copies, waits for them, and re-layouts  14.6 us (5%)
  other arithmetic  4.91 us (2%)
    pallas_call x2, Pallas kernels, backward(): pl.pallas_call(functools.partial(backward_kernel, sweep=sweep), grid_spec...  42.7 us
    all_to_all x2, blocking collectives, shards(): pieces = lax.all_to_all(group_sum, 'col', 0, 0, tiled=True)  29 us
    pallas_call x2, Pallas kernels, build(): pl.pallas_call(functools.partial(build_kernel, rows=rows, cols=cols), gri...  28.4 us
    all_to_all x1, blocking collectives, shards(): back = lax.all_to_all(sent, 'row', 0, 0, tiled=True)  25.9 us
    all_to_all x1, blocking collectives, shards(): recv = (lax.all_to_all(part, 'row', 0, 0, tiled=True),)  25.5 us
    all_to_all x2, blocking collectives, shards(): lax.all_to_all(jnp.broadcast_to(ratio, (n_col,) + ratio.shape), 'col', 0,...  22.7 us
    all_to_all x1, waiting for transfers between devices, shards(): back = lax.all_to_all(sent, 'row', 0, 0, tiled=True)  19.4 us
    pallas_call x1, Pallas kernels, forward(): pl.pallas_call(forward_kernel, grid_spec=pltpu.PrefetchScalarGridSpec(num...  15.5 us
  transfers between devices with their start and end apart: 5, of which 5 were waited for; matrix products, arithmetic and copies ran while one was open for 5% of the time, Pallas kernels for 4%

profile of v3, /device:TPU:0, one launch (start us, length us, event | category | flops | bytes accessed | tf_op | source)
XLA Modules:
  0.0 283.4 jit_solution(15531140776993593162)
XLA Ops:
  2.8 4.6 %all-to-all-start = ((f32[8,8,128]{2,1,0:T(8,128)}), f32[8,8,128]{2,1,0:T(8,128)S(1)}, u32[]{:S(2)}, u32[]{:S(2)}) async-start(f32[8,8,128]{2,1,0:T(8,128)} %broadcast_in_dim.37), calls=%async_computation | async-start | bytes 65536 | tf_op jit(solution)/shard_map/all_to_all | solution.py:353
  8.9 1.6 reshape.401
  11.1 1.7 all-to-all-done
  13.6 7.9 %all-to-all-start.1 = ((f32[16,8,8,128]{3,2,1,0:T(8,128)}), f32[16,8,8,128]{3,2,1,0:T(8,128)S(1)}, u32[]{:S(2)}, u32[]{:S(2)}) async-start(f32[16,8,8,128]{3,2,1,0:T(8,128)} %broadcast_in_dim.38), calls=%async_computation.1 | async-start | bytes 1048576 | tf_op jit(solution)/shard_map/all_to_all | solution.py:354
  22.1 2.5 copy.25.est2
  25.2 7.8 %all-to-all-done.1 = f32[16,8,8,128]{3,2,1,0:T(8,128)S(1)} async-done(((f32[16,8,8,128]{3,2,1,0:T(8,128)}), f32[16,8,8,128]{3,2,1,0:T(8,128)S(1)}, u32[]{:S(2)}, u32[]{:S(2)}) %all-to-all-start.1) | async-done | bytes 524320 | tf_op jit(solution)/shard_map/all_to_all | solution.py:354
  33.7 17.4 %build_cover.2 = (bf16[4096,4096]{1,0:T(8,128)(2,1)}, f8e5m2[4096,4096]{1,0:T(32,128)(4,1)}, f32[16,96,128]{2,1,0:T(8,128)}) custom-call(s32[16]{0:T(128)} %get-tuple-element.28.tab, s32[2]{0:T(128)} %pad_add_fusion.origin, f32[128,8,128]{2,1,0:T(8,128)} %bitcast.42, f32[16,256]{1,0:T(8,128)} %clut.3, bf16[4096,256]{1,0:T(8,128)(2,1)} %copy.25.est2), custom_call_target="tpu_custom_call" | custom-call | tf_op jit(solution)/shard_map/build_cover/pallas_call | solution.py:207
  51.2 4.9 %all-to-all-start.2 = ((f32[16,96,128]{2,1,0:T(8,128)}), f32[16,96,128]{2,1,0:T(8,128)S(1)}, u32[]{:S(2)}, u32[]{:S(2)}) async-start(f32[16,96,128]{2,1,0:T(8,128)} %get-tuple-element.14), calls=%async_computation.2 | async-start | bytes 1572864 | tf_op jit(solution)/shard_map/all_to_all | solution.py:375
  56.1 11.0 %build_cover.3 = (bf16[4096,4096]{1,0:T(8,128)(2,1)}, f8e5m2[4096,4096]{1,0:T(32,128)(4,1)}, f32[16,96,128]{2,1,0:T(8,128)}) custom-call(s32[16]{0:T(128)} %get-tuple-element.27.tab, s32[2]{0:T(128)} %pad_add_fusion.origin, f32[128,8,128]{2,1,0:T(8,128)} %bitcast.43, f32[16,256]{1,0:T(8,128)} %clut.3, ...), custom_call_target="tpu_custom_call", output_to_operand_aliasing={{0}: (5, {}), {1}: (6, {})} | custom-call | tf_op jit(solution)/shard_map/build_cover/pallas_call | solution.py:207
  69.3 6.5 %all-to-all-start.3 = ((f32[16,96,128]{2,1,0:T(8,128)}), f32[16,96,128]{2,1,0:T(8,128)S(1)}, u32[]{:S(2)}, u32[]{:S(2)}) async-start(f32[16,96,128]{2,1,0:T(8,128)} %get-tuple-element.17), calls=%async_computation.3 | async-start | bytes 1572864 | tf_op jit(solution)/shard_map/all_to_all | solution.py:377
  77.3 11.2 %all-to-all-done.3.refs_1_ = f32[16,96,128]{2,1,0:T(8,128)S(1)} async-done(((f32[16,96,128]{2,1,0:T(8,128)}), f32[16,96,128]{2,1,0:T(8,128)S(1)}, u32[]{:S(2)}, u32[]{:S(2)}) %all-to-all-start.3) | async-done | bytes 786464 | tf_op jit(solution)/shard_map/all_to_all | solution.py:377
  89.5 15.4 %all_to_all.55 = f32[8,96,128]{2,1,0:T(8,128)S(1)} all-to-all(f32[8,96,128]{2,1,0:T(8,128)S(1)} %combine_slots.2), channel_id=1, replica_groups=mesh['row'=16,'col'=8] {'col'}, dimensions={0} | all-to-all | bytes 786432 | tf_op jit(solution)/shard_map/all_to_all | solution.py:385
  105.0 11.3 %all_to_all.56.table = f32[8,96,128]{2,1,0:T(8,128)S(1)} all-to-all(f32[8,96,128]{2,1,0:T(8,128)S(1)} %broadcast_in_dim.72), channel_id=1, replica_groups=mesh['row'=16,'col'=8] {'col'}, dimensions={0} | all-to-all | bytes 786432 | tf_op jit(solution)/shard_map/all_to_all | solution.py:387
  116.3 1.9 pick_slots.2
  118.2 3.9 %all-to-all-start.6 = ((f32[16,2,96,128]{3,2,1,0:T(8,128)}), f32[16,2,96,128]{3,2,1,0:T(8,128)S(1)}, u32[]{:S(2)}, u32[]{:S(2)}) async-start(f32[16,2,96,128]{3,2,1,0:T(8,128)} %pick_slots.2), calls=%async_computation.6 | async-start | bytes 3145728 | tf_op jit(solution)/shard_map/all_to_all | solution.py:391
  122.7 3.7 %copy.27 = f32[12,8,16,256]{3,1,2,0:T(8,128)} copy(f32[12,8,16,256]{3,2,1,0:T(8,128)} %bitcast.50) | data formatting | bytes 3145728
  126.4 19.4 %all-to-all-done.6.ratios = f32[16,2,96,128]{3,2,1,0:T(8,128)S(1)} async-done(((f32[16,2,96,128]{3,2,1,0:T(8,128)}), f32[16,2,96,128]{3,2,1,0:T(8,128)S(1)}, u32[]{:S(2)}, u32[]{:S(2)}) %all-to-all-start.6) | async-done | bytes 1572896 | tf_op jit(solution)/shard_map/all_to_all | solution.py:391
  146.9 21.6 %backward_product.2 = (f32[96,4096]{1,0:T(8,128)}, bf16[4096,256]{1,0:T(8,128)(2,1)}, f32[8,4096]{1,0:T(8,128)}) custom-call(s32[32]{0:T(128)} %sub.46.tab, f32[128,8,128]{2,1,0:T(8,128)} %bitcast.44, f32[16,2,96,128]{3,2,1,0:T(8,128)} %copy-done.1, f32[96,4096]{1,0:T(8,128)} %bitcast.48, bf16[4096,4096]{1,0:T(8,128)(2,1)} %get-tuple-element.18.hi, ...), custom_call_target="tpu_custom_call" | custom-call | tf_op jit(solution)/shard_map/backward_product/pallas_call | solution.py:277
  168.6 15.5 %forward_product.1 = f32[16,2,96,128]{3,2,1,0:T(8,128)} custom-call(s32[32]{0:T(128)} %sub.46.tab, f32[128,8,128]{2,1,0:T(8,128)} %bitcast.45, bf16[4096,256]{1,0:T(8,128)(2,1)} %get-tuple-element.20.est2, bf16[4096,4096]{1,0:T(8,128)(2,1)} %get-tuple-element.18.hi), custom_call_target="tpu_custom_call" | custom-call | tf_op jit(solution)/shard_map/forward_product/pallas_call | solution.py:240
  184.0 25.5 %all_to_all.57.refs_0_ = f32[16,2,96,128]{3,2,1,0:T(8,128)S(1)} all-to-all(f32[16,2,96,128]{3,2,1,0:T(8,128)} %forward_product.1), channel_id=1, replica_groups=mesh['row'=16,'col'=8] {'row'}, dimensions={0} | all-to-all | bytes 3145728 | tf_op jit(solution)/shard_map/all_to_all | solution.py:383
  210.6 13.6 %all_to_all.58 = f32[8,96,128]{2,1,0:T(8,128)S(1)} all-to-all(f32[8,96,128]{2,1,0:T(8,128)S(1)} %combine_slots.3), channel_id=1, replica_groups=mesh['row'=16,'col'=8] {'col'}, dimensions={0} | all-to-all | bytes 786432 | tf_op jit(solution)/shard_map/all_to_all | solution.py:385
  224.3 11.3 %all_to_all.59.table = f32[8,96,128]{2,1,0:T(8,128)S(1)} all-to-all(f32[8,96,128]{2,1,0:T(8,128)S(1)} %broadcast_in_dim.73), channel_id=1, replica_groups=mesh['row'=16,'col'=8] {'col'}, dimensions={0} | all-to-all | bytes 786432 | tf_op jit(solution)/shard_map/all_to_all | solution.py:387
  236.4 25.9 %all_to_all.60.ratios = f32[16,2,96,128]{3,2,1,0:T(8,128)} all-to-all(f32[16,2,96,128]{3,2,1,0:T(8,128)S(1)} %pick_slots.3), channel_id=1, replica_groups=mesh['row'=16,'col'=8] {'row'}, dimensions={0} | all-to-all | bytes 3145728 | tf_op jit(solution)/shard_map/all_to_all | solution.py:391
  262.4 21.0 %backward_product.3 = f32[96,16,256]{2,1,0:T(8,128)} custom-call(s32[32]{0:T(128)} %sub.46.tab, f32[128,8,128]{2,1,0:T(8,128)} %bitcast.46, f32[16,2,96,128]{3,2,1,0:T(8,128)} %all_to_all.60.ratios, f32[96,4096]{1,0:T(8,128)} %get-tuple-element.21.est, bf16[4096,4096]{1,0:T(8,128)(2,1)} %get-tuple-element.18.hi, f8e5m2[4096,4096]{1,0:T(32,128)(4,1)} %get-tuple-element.19.lo, ...), custom_call_target="tpu_custom_call" | custom-call | tf_op jit(solution)/shard_map/backward_product/pallas_call | solution.py:277
  (46 shorter events, 15.5 us)
Async XLA Ops:
  2.8 10.0 %all-to-all-start = ((f32[8,8,128]{2,1,0:T(8,128)}), f32[8,8,128]{2,1,0:T(8,128)S(1)}, u32[]{:S(2)}, u32[]{:S(2)}) async-start(f32[8,8,128]{2,1,0:T(8,128)} %broadcast_in_dim.37), calls=%async_computation | async-start | bytes 65536 | tf_op jit(solution)/shard_map/all_to_all | solution.py:353
  13.6 19.3 %all-to-all-start.1 = ((f32[16,8,8,128]{3,2,1,0:T(8,128)}), f32[16,8,8,128]{3,2,1,0:T(8,128)S(1)}, u32[]{:S(2)}, u32[]{:S(2)}) async-start(f32[16,8,8,128]{3,2,1,0:T(8,128)} %broadcast_in_dim.38), calls=%async_computation.1 | async-start | bytes 1048576 | tf_op jit(solution)/shard_map/all_to_all | solution.py:354
  33.0 0.8 copy-start
  51.2 18.1 %all-to-all-start.2 = ((f32[16,96,128]{2,1,0:T(8,128)}), f32[16,96,128]{2,1,0:T(8,128)S(1)}, u32[]{:S(2)}, u32[]{:S(2)}) async-start(f32[16,96,128]{2,1,0:T(8,128)} %get-tuple-element.14), calls=%async_computation.2 | async-start | bytes 1572864 | tf_op jit(solution)/shard_map/all_to_all | solution.py:375
  69.3 35.6 %copy-start.2 = (s32[1,96,128]{2,1,0:T(8,128)S(1)}, s32[1,96,128]{2,1,0:T(8,128)}, u32[]{:S(2)}) copy-start(s32[1,96,128]{2,1,0:T(8,128)} %param.8) | copy-start | bytes 147460
  69.3 19.2 %all-to-all-start.3 = ((f32[16,96,128]{2,1,0:T(8,128)}), f32[16,96,128]{2,1,0:T(8,128)S(1)}, u32[]{:S(2)}, u32[]{:S(2)}) async-start(f32[16,96,128]{2,1,0:T(8,128)} %get-tuple-element.17), calls=%async_computation.3 | async-start | bytes 1572864 | tf_op jit(solution)/shard_map/all_to_all | solution.py:377
  118.2 27.6 %all-to-all-start.6 = ((f32[16,2,96,128]{3,2,1,0:T(8,128)}), f32[16,2,96,128]{3,2,1,0:T(8,128)S(1)}, u32[]{:S(2)}, u32[]{:S(2)}) async-start(f32[16,2,96,128]{3,2,1,0:T(8,128)} %pick_slots.2), calls=%async_computation.6 | async-start | bytes 3145728 | tf_op jit(solution)/shard_map/all_to_all | solution.py:391
  145.8 1.1 copy-start.1

commit v4 on v3

--- a/solution.py
+++ b/solution.py
@@ -43,10 +43,8 @@
     return live
 
 
-def build_kernel(tab, origin, records, clut, est2, *rest, rows, cols):
-    hi, lo, part, across = rest[-4:]
+def build_kernel(tab, origin, records, clut, est2, hi, lo, part, across, *, rows, cols):
     step = pl.program_id(0)
-    maps = part.shape[1]
 
     @pl.when(any_live(tab, step))
     def _():
@@ -81,15 +79,16 @@
                     top = value.astype(bf16)
                     hi[at, r * cols : (r + 1) * cols] = top
                     lo[at, r * cols : (r + 1) * cols] = (value - top.astype(f32)).astype(LO_TYPE)
-        forward_dot(tab, step, records, est2, hi, part, maps)
-
-
-def forward_dot(tab, step, records, est2, hi, part, maps):
+        forward_dot(tab, step, records, est2, hi, part)
+
+
+def forward_dot(tab, step, records, est2, hi, part):
+    maps = part.shape[2]
     both = jnp.dot(hi[...], est2[...], preferred_element_type=f32)
     total = both[:, :128] + both[:, 128:]
     for k in range(STEP):
         scale = antenna_scale(records[jnp.maximum(tab[step * STEP + k], 0)])
-        part[k] = total[k * 128 : (k + 1) * 128, :].T[:maps, :] * scale
+        part[k, 0] = total[k * 128 : (k + 1) * 128, :].T[:maps, :] * scale
 
 
 def forward_kernel(tab, records, est2, hi, part):
@@ -97,7 +96,7 @@
 
     @pl.when(any_live(tab, step))
     def _():
-        forward_dot(tab, step, records, est2, hi, part.at[:, 0], part.shape[2])
+        forward_dot(tab, step, records, est2, hi, part)
 
 
 def backward_kernel(tab, records, ratios, est, hi, lo, *rest, sweep):
@@ -154,21 +153,18 @@
                 est_out[:, r, :] = est[:, at] * acc[:maps, at] / sens_in[0:1, at]
 
 
-def combine_kernel(tab, *refs):
-    out = refs[-1]
-    recv = refs[:-1]
-    groups = recv[0].shape[0]
+def combine_kernel(tab, recv, out):
+    groups = recv.shape[0]
     out[...] = jnp.zeros_like(out)
-    for j in range(2):
-
-        @pl.loop(0, groups)
-        def _(i):
+
+    @pl.loop(0, groups)
+    def _(i):
+        for j in range(2):
             local = tab[j * groups + i]
 
             @pl.when(local >= 0)
             def _():
-                piece = recv[j][i] if len(recv) == 2 else recv[0][i, j]
-                out[local] = out[local] + piece
+                out[local] = out[local] + recv[i, j]
 
 
 def pick_kernel(tab, table, out):
@@ -192,45 +188,36 @@
     return pl.BlockSpec(shape, lambda *_: (0,) * len(shape))
 
 
-def build(tab, origin, records, clut, est2, maps, rows, cols, half, stored):
+def place_spec(slots, maps):
+    per = slots // 2 // STEP
+    return spec((STEP, 1, maps, 128), lambda i, *_: (i % per, i // per, 0, 0))
+
+
+def build(tab, origin, records, clut, est2, maps, rows, cols):
     slots = tab.shape[0]
     n_pixels = rows * cols
     tall = STEP * 128
-    steps = slots // STEP
-    operands = [records, clut, est2]
-    in_specs = [whole(x.shape) for x in operands]
-    aliases = {}
-    if half:
-        operands += list(stored)
-        in_specs += [pl.BlockSpec(memory_space=pl.ANY)] * 2
-        aliases = {5: 0, 6: 1}
     return pl.pallas_call(
         functools.partial(build_kernel, rows=rows, cols=cols),
         grid_spec=pltpu.PrefetchScalarGridSpec(
             num_scalar_prefetch=2,
-            grid=(steps,),
-            in_specs=in_specs,
+            grid=(slots // STEP,),
+            in_specs=[whole(records.shape), whole(clut.shape), whole(est2.shape)],
             out_specs=[
-                spec((tall, n_pixels), lambda i, *_: (half * steps + i, 0)),
-                spec((tall, n_pixels), lambda i, *_: (half * steps + i, 0)),
-                spec((STEP, maps, 128), lambda i, *_: (i, 0, 0)),
+                spec((tall, n_pixels), lambda i, *_: (i, 0)),
+                spec((tall, n_pixels), lambda i, *_: (i, 0)),
+                place_spec(slots, maps),
             ],
             scratch_shapes=[pltpu.VMEM((STEP, 128, cols), f32)],
         ),
         out_shape=[
-            jax.ShapeDtypeStruct((2 * slots * 128, n_pixels), bf16),
-            jax.ShapeDtypeStruct((2 * slots * 128, n_pixels), LO_TYPE),
-            jax.ShapeDtypeStruct((slots, maps, 128), f32),
+            jax.ShapeDtypeStruct((slots * 128, n_pixels), bf16),
+            jax.ShapeDtypeStruct((slots * 128, n_pixels), LO_TYPE),
+            jax.ShapeDtypeStruct((slots // 2, 2, maps, 128), f32),
         ],
-        input_output_aliases=aliases,
         compiler_params=params(56),
         name="build_cover",
-    )(tab, origin, *operands)
-
-
-def place_spec(slots, maps):
-    per = slots // 2 // STEP
-    return spec((STEP, 1, maps, 128), lambda i, *_: (i % per, i // per, 0, 0))
+    )(tab, origin, records, clut, est2)
 
 
 def forward(tab, records, est2, hi, maps):
@@ -290,19 +277,19 @@
 
 
 def combine(tab, recv, n_out):
-    shape = (n_out,) + recv[0].shape[-2:]
+    shape = (n_out,) + recv.shape[2:]
     return pl.pallas_call(
         combine_kernel,
         grid_spec=pltpu.PrefetchScalarGridSpec(
             num_scalar_prefetch=1,
             grid=(1,),
-            in_specs=[whole(x.shape) for x in recv],
+            in_specs=[whole(recv.shape)],
             out_specs=whole(shape),
         ),
         out_shape=jax.ShapeDtypeStruct(shape, f32),
         compiler_params=params(32),
         name="combine_slots",
-    )(tab, *recv)
+    )(tab, recv)
 
 
 def pick(tab, table):
@@ -333,6 +320,17 @@
         place[:, None, None, :] == jnp.arange(2, dtype=jnp.int32)[None, :, None, None]
     )
     return jnp.sum(jnp.where(hit, lists[:, None, None, :] + 1, 0), axis=3) - 1
+
+
+def exchange(x, both_places):
+    def first(x):
+        got = lax.all_to_all(x[:, 0], "row", 0, 0, tiled=True)
+        return jnp.stack([got, jnp.zeros_like(got)], axis=1)
+
+    def full(x):
+        return lax.all_to_all(x, "row", 0, 0, tiled=True)
+
+    return lax.cond(both_places, full, first, x)
 
 
 def shards(initial_estimate0, clutter, counts, antenna_settings, tile_block_list, tile_block_count):
@@ -365,30 +363,25 @@
     theirs = lax.dynamic_index_in_dim(tables, row, 2, keepdims=False)
     theirs = jnp.where(theirs >= 0, theirs - row * n_col, -1).T.reshape(2 * n_row)
 
+    both_places = jnp.any(tables[:, 1] >= 0)
     origin = jnp.stack([row * rows, col * cols]).astype(jnp.int32)
     est = initial_estimate0.reshape(maps, n_pixels)
     est2 = wide_pair(initial_estimate0.transpose(1, 2, 0).reshape(n_pixels, maps))
     wanted = counts[0].astype(f32)
-    tabs = (tab[:n_row], tab[n_row:])
-
-    hi, lo, part = build(tabs[0], origin, records, clutter, est2, maps, rows, cols, 0, None)
-    recv0 = lax.all_to_all(part, "row", 0, 0, tiled=True)
-    hi, lo, part = build(tabs[1], origin, records, clutter, est2, maps, rows, cols, 1, (hi, lo))
-    recv1 = lax.all_to_all(part, "row", 0, 0, tiled=True)
-    recv = (recv0, recv1)
+
+    hi, lo, part = build(tab, origin, records, clutter, est2, maps, rows, cols)
     sens = None
     for sweep in range(ITERS):
         if sweep > 0:
             part = forward(tab, records, est2, hi, maps)
-            recv = (lax.all_to_all(part, "row", 0, 0, tiled=True),)
-        group_sum = combine(theirs, recv, n_col)
+        group_sum = combine(theirs, exchange(part, both_places), n_col)
         pieces = lax.all_to_all(group_sum, "col", 0, 0, tiled=True)
         ratio = wanted / jnp.sum(pieces, axis=0)
         table = lax.all_to_all(
             jnp.broadcast_to(ratio, (n_col,) + ratio.shape), "col", 0, 0, tiled=True
         )
         sent = pick(theirs, table)
-        back = lax.all_to_all(sent, "row", 0, 0, tiled=True)
+        back = exchange(sent, both_places)
         done = backward(tab, records, back, est, hi, lo, sens, sweep, rows, cols)
         if sweep == 0:
             est, est2, sens = done

time: 285 us -> 264 us (0.926)
  waiting for transfers between devices: 40.8 us -> 14.4 us
  blocking collectives: 103 us -> 125 us
  starting transfers between devices: 27.8 us -> 15.9 us
  Pallas kernels: 91.3 us -> 84.7 us
  local copies, waits for them, and re-layouts: 14.6 us -> 11.3 us
    all_to_all x3 -> x1, waiting for transfers between devices: 31.4 us -> 6.61 us  [shards(): lax.all_to_all(jnp.broadcast_to(ratio, (n_col,) + ratio.shape), 'col', 0,...]
    all_to_all x2 -> x4, blocking collectives: 51.5 us -> 69.2 us  [first(): got = lax.all_to_all(x[:, 0], 'row', 0, 0, tiled=True)]
    all_to_all x2, blocking collectives: 29 us -> 44.5 us  [shards(): pieces = lax.all_to_all(group_sum, 'col', 0, 0, tiled=True)]
    all_to_all x3 -> x1, starting transfers between devices: 15.4 us -> 3.45 us  [shards(): lax.all_to_all(jnp.broadcast_to(ratio, (n_col,) + ratio.shape), 'col', 0,...]
    all_to_all x2 -> x1, blocking collectives: 22.7 us -> 11.3 us  [shards(): lax.all_to_all(jnp.broadcast_to(ratio, (n_col,) + ratio.shape), 'col', 0,...]
    pallas_call x2 -> x1, Pallas kernels: 28.4 us -> 24.7 us  [build(): pl.pallas_call(functools.partial(build_kernel, rows=rows, cols=cols), gri...]
    unnamed x8, local copies, waits for them, and re-layouts: 6.28 us -> 2.94 us
  transfers between devices with their start and end apart: 5 -> 3, of which waited for: 5 -> 3; matrix products, arithmetic and copies ran while one was open for 5% -> 4% of each run, Pallas kernels for 4% -> 0%
where the time goes in v4:
time: 264 us; the launch traced here: 261 us
  blocking collectives  125 us (47%)
  Pallas kernels  84.7 us (32%)
  starting transfers between devices  15.9 us (6%)
  waiting for transfers between devices  14.4 us (5%)
  local copies, waits for them, and re-layouts  11.3 us (4%)
  other arithmetic  7.4 us (3%)
    all_to_all x4, blocking collectives, first(): got = lax.all_to_all(x[:, 0], 'row', 0, 0, tiled=True)  69.2 us
    all_to_all x2, blocking collectives, shards(): pieces = lax.all_to_all(group_sum, 'col', 0, 0, tiled=True)  44.5 us
    pallas_call x2, Pallas kernels, backward(): pl.pallas_call(functools.partial(backward_kernel, sweep=sweep), grid_spec...  41.9 us
    pallas_call x1, Pallas kernels, build(): pl.pallas_call(functools.partial(build_kernel, rows=rows, cols=cols), gri...  24.7 us
    pallas_call x1, Pallas kernels, forward(): pl.pallas_call(forward_kernel, grid_spec=pltpu.PrefetchScalarGridSpec(num...  14.7 us
    all_to_all x1, blocking collectives, shards(): lax.all_to_all(jnp.broadcast_to(ratio, (n_col,) + ratio.shape), 'col', 0,...  11.3 us
    all_to_all x1, starting transfers between devices, shards(): lax.all_to_all(jnp.broadcast_to(mine, (n_row, n_col, 8, 128)), 'row', 0,...  7.88 us
    all_to_all x1, waiting for transfers between devices, shards(): lax.all_to_all(jnp.broadcast_to(mine, (n_row, n_col, 8, 128)), 'row', 0,...  7.26 us
  transfers between devices with their start and end apart: 3, of which 3 were waited for; matrix products, arithmetic and copies ran while one was open for 4% of the time, Pallas kernels for 0%

profile of v4, /device:TPU:0, one launch (start us, length us, event | category | flops | bytes accessed | tf_op | source)
XLA Modules:
  0.0 260.5 jit_solution(12629523281973416701)
XLA Ops:
  2.8 4.6 %all-to-all-start.8 = ((f32[8,8,128]{2,1,0:T(8,128)}), f32[8,8,128]{2,1,0:T(8,128)S(1)}, u32[]{:S(2)}, u32[]{:S(2)}) async-start(f32[8,8,128]{2,1,0:T(8,128)} %broadcast_in_dim.37), calls=%async_computation.8 | async-start | bytes 65536 | tf_op jit(solution)/shard_map/all_to_all | solution.py:351
  8.9 1.6 reshape.393
  13.7 7.9 %all-to-all-start.9 = ((f32[16,8,8,128]{3,2,1,0:T(8,128)}), f32[16,8,8,128]{3,2,1,0:T(8,128)S(1)}, u32[]{:S(2)}, u32[]{:S(2)}) async-start(f32[16,8,8,128]{3,2,1,0:T(8,128)} %broadcast_in_dim.38), calls=%async_computation.9 | async-start | bytes 1048576 | tf_op jit(solution)/shard_map/all_to_all | solution.py:352
  21.5 1.3 fusion.2
  22.9 2.5 copy.91.est2
  25.9 7.3 %all-to-all-done.9 = f32[16,8,8,128]{3,2,1,0:T(8,128)S(1)} async-done(((f32[16,8,8,128]{3,2,1,0:T(8,128)}), f32[16,8,8,128]{3,2,1,0:T(8,128)S(1)}, u32[]{:S(2)}, u32[]{:S(2)}) %all-to-all-start.9) | async-done | bytes 524320 | tf_op jit(solution)/shard_map/all_to_all | solution.py:352
  36.3 24.7 %build_cover.1 = (bf16[4096,4096]{1,0:T(8,128)(2,1)}, f8e5m2[4096,4096]{1,0:T(32,128)(4,1)}, f32[16,2,96,128]{3,2,1,0:T(8,128)S(1)}) custom-call(s32[32]{0:T(128)} %sub.44.tab, s32[2]{0:T(128)} %pad_add_fusion.origin, f32[128,8,128]{2,1,0:T(8,128)} %bitcast.64, f32[16,256]{1,0:T(8,128)} %clut.1, bf16[4096,256]{1,0:T(8,128)(2,1)} %copy.91.est2), custom_call_target="tpu_custom_call" | custom-call | tf_op jit(solution)/shard_map/build_cover/pallas_call | solution.py:200
  61.0 18.2 %conditional.4 = (f32[16,2,96,128]{3,2,1,0:T(8,128)S(1)}) conditional(s32[]{:T(128)} %convert_element_type.52, f32[16,2,96,128]{3,2,1,0:T(8,128)S(1)} %get-tuple-element.31, f32[16,2,96,128]{3,2,1,0:T(8,128)S(1)} %get-tuple-element.31), branch_computations={%region_5.6_spmd, %region_6.7_spmd} | conditional | bytes 5505036 | solution.py:333
  61.1 18.0 %all_to_all.62 = f32[16,96,128]{2,1,0:T(8,128)S(1)} all-to-all(f32[16,96,128]{2,1,0:T(8,128)S(1)} %slice_bitcast_fusion), channel_id=1, replica_groups=mesh['row'=16,'col'=8] {'row'}, dimensions={0} | all-to-all | bytes 1572864 | tf_op jit(solution)/shard_map/cond/branch_0_fun/all_to_all | solution.py:327
  80.2 22.0 %all_to_all.70 = f32[8,96,128]{2,1,0:T(8,128)S(1)} all-to-all(f32[8,96,128]{2,1,0:T(8,128)S(1)} %combine_slots.2), channel_id=1, replica_groups=mesh['row'=16,'col'=8] {'col'}, dimensions={0} | all-to-all | bytes 786432 | tf_op jit(solution)/shard_map/all_to_all | solution.py:378
  103.1 3.5 %all-to-all-start.11 = ((f32[8,96,128]{2,1,0:T(8,128)}), f32[8,96,128]{2,1,0:T(8,128)S(1)}, u32[]{:S(2)}, u32[]{:S(2)}) async-start(f32[8,96,128]{2,1,0:T(8,128)} %broadcast_in_dim.72), calls=%async_computation.11 | async-start | bytes 786432 | tf_op jit(solution)/shard_map/all_to_all | solution.py:380
  106.6 2.2 copy.101
  108.8 6.6 %all-to-all-done.11.table = f32[8,96,128]{2,1,0:T(8,128)S(1)} async-done(((f32[8,96,128]{2,1,0:T(8,128)}), f32[8,96,128]{2,1,0:T(8,128)S(1)}, u32[]{:S(2)}, u32[]{:S(2)}) %all-to-all-start.11) | async-done | bytes 393248 | tf_op jit(solution)/shard_map/all_to_all | solution.py:380
  116.2 17.6 %conditional.5 = (f32[16,2,96,128]{3,2,1,0:T(8,128)S(1)}) conditional(s32[]{:T(128)} %convert_element_type.52, f32[16,2,96,128]{3,2,1,0:T(8,128)S(1)} %pick_slots.2, f32[16,2,96,128]{3,2,1,0:T(8,128)S(1)} %pick_slots.2), branch_computations={%region_8.9_spmd, %region_9.10_spmd} | conditional | bytes 5505036 | solution.py:333
  116.3 17.2 %all_to_all.64 = f32[16,96,128]{2,1,0:T(8,128)S(1)} all-to-all(f32[16,96,128]{2,1,0:T(8,128)S(1)} %slice_bitcast_fusion.1), channel_id=1, replica_groups=mesh['row'=16,'col'=8] {'row'}, dimensions={0} | all-to-all | bytes 1572864 | tf_op jit(solution)/shard_map/cond/branch_0_fun/all_to_all | solution.py:327
  133.8 21.2 %backward_product.2 = (f32[96,4096]{1,0:T(8,128)}, bf16[4096,256]{1,0:T(8,128)(2,1)}, f32[8,4096]{1,0:T(8,128)}) custom-call(s32[32]{0:T(128)} %sub.44.tab, f32[128,8,128]{2,1,0:T(8,128)} %bitcast.65, f32[16,2,96,128]{3,2,1,0:T(8,128)S(1)} %get-tuple-element.38.ratios, f32[96,4096]{1,0:T(8,128)} %bitcast.69, bf16[4096,4096]{1,0:T(8,128)(2,1)} %get-tuple-element.32.hi, ...), custom_call_target="tpu_custom_call" | custom-call | tf_op jit(solution)/shard_map/backward_product/pallas_call | solution.py:264
  155.0 14.7 %forward_product.1 = f32[16,2,96,128]{3,2,1,0:T(8,128)S(1)} custom-call(s32[32]{0:T(128)} %sub.44.tab, f32[128,8,128]{2,1,0:T(8,128)} %bitcast.66, bf16[4096,256]{1,0:T(8,128)(2,1)} %get-tuple-element.34.est2, bf16[4096,4096]{1,0:T(8,128)(2,1)} %get-tuple-element.32.hi), custom_call_target="tpu_custom_call" | custom-call | tf_op jit(solution)/shard_map/forward_product/pallas_call | solution.py:227
  169.7 17.1 %conditional.6 = (f32[16,2,96,128]{3,2,1,0:T(8,128)S(1)}) conditional(s32[]{:T(128)} %convert_element_type.52, f32[16,2,96,128]{3,2,1,0:T(8,128)S(1)} %forward_product.1, f32[16,2,96,128]{3,2,1,0:T(8,128)S(1)} %forward_product.1), branch_computations={%region_10.11_spmd, %region_11.12_spmd} | conditional | bytes 5505036 | solution.py:333
  169.8 16.9 %all_to_all.66 = f32[16,96,128]{2,1,0:T(8,128)S(1)} all-to-all(f32[16,96,128]{2,1,0:T(8,128)S(1)} %slice_bitcast_fusion.2), channel_id=1, replica_groups=mesh['row'=16,'col'=8] {'row'}, dimensions={0} | all-to-all | bytes 1572864 | tf_op jit(solution)/shard_map/cond/branch_0_fun/all_to_all | solution.py:327
  187.8 22.5 %all_to_all.71 = f32[8,96,128]{2,1,0:T(8,128)S(1)} all-to-all(f32[8,96,128]{2,1,0:T(8,128)S(1)} %combine_slots.3), channel_id=1, replica_groups=mesh['row'=16,'col'=8] {'col'}, dimensions={0} | all-to-all | bytes 786432 | tf_op jit(solution)/shard_map/all_to_all | solution.py:378
  210.4 11.3 %all_to_all.72.table = f32[8,96,128]{2,1,0:T(8,128)S(1)} all-to-all(f32[8,96,128]{2,1,0:T(8,128)S(1)} %broadcast_in_dim.73), channel_id=1, replica_groups=mesh['row'=16,'col'=8] {'col'}, dimensions={0} | all-to-all | bytes 786432 | tf_op jit(solution)/shard_map/all_to_all | solution.py:380
  222.5 17.4 %conditional.7 = (f32[16,2,96,128]{3,2,1,0:T(8,128)S(1)}) conditional(s32[]{:T(128)} %convert_element_type.52, f32[16,2,96,128]{3,2,1,0:T(8,128)S(1)} %pick_slots.3, f32[16,2,96,128]{3,2,1,0:T(8,128)S(1)} %pick_slots.3), branch_computations={%region_13.14_spmd, %region_14.15_spmd} | conditional | bytes 5505036 | solution.py:333
  222.5 17.2 %all_to_all.68 = f32[16,96,128]{2,1,0:T(8,128)S(1)} all-to-all(f32[16,96,128]{2,1,0:T(8,128)S(1)} %slice_bitcast_fusion.3), channel_id=1, replica_groups=mesh['row'=16,'col'=8] {'row'}, dimensions={0} | all-to-all | bytes 1572864 | tf_op jit(solution)/shard_map/cond/branch_0_fun/all_to_all | solution.py:327
  239.9 20.6 %backward_product.3 = f32[96,16,256]{2,1,0:T(8,128)} custom-call(s32[32]{0:T(128)} %sub.44.tab, f32[128,8,128]{2,1,0:T(8,128)} %bitcast.67, f32[16,2,96,128]{3,2,1,0:T(8,128)S(1)} %get-tuple-element.40.ratios, f32[96,4096]{1,0:T(8,128)} %get-tuple-element.35.est, bf16[4096,4096]{1,0:T(8,128)(2,1)} %get-tuple-element.32.hi, ...), custom_call_target="tpu_custom_call" | custom-call | tf_op jit(solution)/shard_map/backward_product/pallas_call | solution.py:264
  (55 shorter events, 15.0 us)
Async XLA Ops:
  2.8 10.0 %all-to-all-start.8 = ((f32[8,8,128]{2,1,0:T(8,128)}), f32[8,8,128]{2,1,0:T(8,128)S(1)}, u32[]{:S(2)}, u32[]{:S(2)}) async-start(f32[8,8,128]{2,1,0:T(8,128)} %broadcast_in_dim.37), calls=%async_computation.8 | async-start | bytes 65536 | tf_op jit(solution)/shard_map/all_to_all | solution.py:351
  13.7 19.5 %all-to-all-start.9 = ((f32[16,8,8,128]{3,2,1,0:T(8,128)}), f32[16,8,8,128]{3,2,1,0:T(8,128)S(1)}, u32[]{:S(2)}, u32[]{:S(2)}) async-start(f32[16,8,8,128]{3,2,1,0:T(8,128)} %broadcast_in_dim.38), calls=%async_computation.9 | async-start | bytes 1048576 | tf_op jit(solution)/shard_map/all_to_all | solution.py:352
  33.2 3.1 %copy-start = (f32[16,8,8,128]{3,2,1,0:T(8,128)}, f32[16,8,8,128]{3,2,1,0:T(8,128)S(1)}, u32[]{:S(2)}) copy-start(f32[16,8,8,128]{3,2,1,0:T(8,128)S(1)} %all-to-all-done.9) | copy-start | bytes 1572868
  79.2 23.1 %copy-start.2 = (s32[1,96,128]{2,1,0:T(8,128)S(1)}, s32[1,96,128]{2,1,0:T(8,128)}, u32[]{:S(2)}) copy-start(s32[1,96,128]{2,1,0:T(8,128)} %param.16) | copy-start | bytes 147460
  80.2 26.3 %copy-start.1 = (f32[96,16,256]{2,1,0:T(8,128)S(1)}, f32[96,16,256]{2,1,0:T(8,128)}, u32[]{:S(2)}) copy-start(f32[96,16,256]{2,1,0:T(8,128)} %param.14) | copy-start | bytes 4718596
  103.1 12.3 %all-to-all-start.11 = ((f32[8,96,128]{2,1,0:T(8,128)}), f32[8,96,128]{2,1,0:T(8,128)S(1)}, u32[]{:S(2)}, u32[]{:S(2)}) async-start(f32[8,96,128]{2,1,0:T(8,128)} %broadcast_in_dim.72), calls=%async_computation.11 | async-start | bytes 786432 | tf_op jit(solution)/shard_map/all_to_all | solution.py:380

commit v5 on v4

--- a/solution.py
+++ b/solution.py
@@ -9,7 +9,10 @@
 ITERS = 2
 LOG2E = 1.4426950408889634
 CLUTTER_MAX = 1.5
-STEP = 4
+BUILD_STEP = 4
+FORWARD_STEP = 8
+BACK_STEP = 8
+CHUNK = 512
 STORE = 65536.0
 INV_MAX = 1e37
 SENS_ROWS = 16
@@ -36,20 +39,22 @@
     return record[3:4, :] * (peak * (1.0 / STORE))
 
 
-def any_live(tab, step):
-    live = tab[step * STEP] >= 0
-    for k in range(1, STEP):
-        live = jnp.logical_or(live, tab[step * STEP + k] >= 0)
+def any_live(tab, first, count):
+    live = tab[first] >= 0
+    for k in range(1, count):
+        live = jnp.logical_or(live, tab[first + k] >= 0)
     return live
 
 
 def build_kernel(tab, origin, records, clut, est2, hi, lo, part, across, *, rows, cols):
     step = pl.program_id(0)
 
-    @pl.when(any_live(tab, step))
+    live_step = any_live(tab, step * BUILD_STEP // BACK_STEP * BACK_STEP, BACK_STEP)
+
+    @pl.when(live_step)
     def _():
-        for k in range(STEP):
-            block = tab[step * STEP + k]
+        for k in range(BUILD_STEP):
+            block = tab[step * BUILD_STEP + k]
             live = block >= 0
             record = records[jnp.maximum(block, 0)]
             slope = jnp.where(live, record[4:5, :] * (-LOG2E), 0.0)
@@ -83,18 +88,19 @@
 
 
 def forward_dot(tab, step, records, est2, hi, part):
-    maps = part.shape[2]
+    count, _, maps, _ = part.shape
     both = jnp.dot(hi[...], est2[...], preferred_element_type=f32)
     total = both[:, :128] + both[:, 128:]
-    for k in range(STEP):
-        scale = antenna_scale(records[jnp.maximum(tab[step * STEP + k], 0)])
+    for k in range(count):
+        scale = antenna_scale(records[jnp.maximum(tab[step * count + k], 0)])
         part[k, 0] = total[k * 128 : (k + 1) * 128, :].T[:maps, :] * scale
 
 
 def forward_kernel(tab, records, est2, hi, part):
     step = pl.program_id(0)
-
-    @pl.when(any_live(tab, step))
+    count = part.shape[0]
+
+    @pl.when(any_live(tab, step * count, count))
     def _():
         forward_dot(tab, step, records, est2, hi, part)
 
@@ -111,12 +117,12 @@
     def _():
         acc[...] = jnp.zeros_like(acc)
 
-    @pl.when(any_live(tab, step))
+    @pl.when(any_live(tab, step * BACK_STEP, BACK_STEP))
     def _():
         wide = []
         thin = []
-        for k in range(STEP):
-            block = tab[step * STEP + k]
+        for k in range(BACK_STEP):
+            block = tab[step * BACK_STEP + k]
             live = block >= 0
             scale = antenna_scale(records[jnp.maximum(block, 0)])
             stack = jnp.where(live, ratios[k, 0] * scale, 0.0)
@@ -129,7 +135,7 @@
         wide = jnp.concatenate(wide, axis=1)
         thin = jnp.concatenate(thin, axis=1)
         height = thin.shape[0]
-        chunk = 512
+        chunk = CHUNK
         for at in range(0, n_pixels, chunk):
             both = jnp.dot(wide, hi[:, at : at + chunk], preferred_element_type=f32)
             low = jnp.dot(thin, lo[:, at : at + chunk], preferred_element_type=f32)
@@ -188,27 +194,27 @@
     return pl.BlockSpec(shape, lambda *_: (0,) * len(shape))
 
 
-def place_spec(slots, maps):
-    per = slots // 2 // STEP
-    return spec((STEP, 1, maps, 128), lambda i, *_: (i % per, i // per, 0, 0))
+def place_spec(slots, maps, step):
+    per = slots // 2 // step
+    return spec((step, 1, maps, 128), lambda i, *_: (i % per, i // per, 0, 0))
 
 
 def build(tab, origin, records, clut, est2, maps, rows, cols):
     slots = tab.shape[0]
     n_pixels = rows * cols
-    tall = STEP * 128
+    tall = BUILD_STEP * 128
     return pl.pallas_call(
         functools.partial(build_kernel, rows=rows, cols=cols),
         grid_spec=pltpu.PrefetchScalarGridSpec(
             num_scalar_prefetch=2,
-            grid=(slots // STEP,),
+            grid=(slots // BUILD_STEP,),
             in_specs=[whole(records.shape), whole(clut.shape), whole(est2.shape)],
             out_specs=[
                 spec((tall, n_pixels), lambda i, *_: (i, 0)),
                 spec((tall, n_pixels), lambda i, *_: (i, 0)),
-                place_spec(slots, maps),
+                place_spec(slots, maps, BUILD_STEP),
             ],
-            scratch_shapes=[pltpu.VMEM((STEP, 128, cols), f32)],
+            scratch_shapes=[pltpu.VMEM((BUILD_STEP, 128, cols), f32)],
         ),
         out_shape=[
             jax.ShapeDtypeStruct((slots * 128, n_pixels), bf16),
@@ -223,18 +229,18 @@
 def forward(tab, records, est2, hi, maps):
     slots = tab.shape[0]
     n_pixels = est2.shape[0]
-    tall = STEP * 128
+    tall = FORWARD_STEP * 128
     return pl.pallas_call(
         forward_kernel,
         grid_spec=pltpu.PrefetchScalarGridSpec(
             num_scalar_prefetch=1,
-            grid=(slots // STEP,),
+            grid=(slots // FORWARD_STEP,),
             in_specs=[
                 whole(records.shape),
                 whole(est2.shape),
                 spec((tall, n_pixels), lambda i, *_: (i, 0)),
             ],
-            out_specs=place_spec(slots, maps),
+            out_specs=place_spec(slots, maps, FORWARD_STEP),
         ),
         out_shape=jax.ShapeDtypeStruct((slots // 2, 2, maps, 128), f32),
         compiler_params=params(56),
@@ -245,12 +251,12 @@
 def backward(tab, records, ratios, est, hi, lo, sens, sweep, rows, cols):
     slots = tab.shape[0]
     maps, n_pixels = est.shape
-    tall = STEP * 128
+    tall = BACK_STEP * 128
     height = maps + (SENS_ROWS if sweep == 0 else 0)
     operands = [records, ratios, est, hi, lo]
     in_specs = [
         whole(records.shape),
-        place_spec(slots, maps),
+        place_spec(slots, maps, BACK_STEP),
         whole(est.shape),
         spec((tall, n_pixels), lambda i, *_: (i, 0)),
         spec((tall, n_pixels), lambda i, *_: (i, 0)),
@@ -265,7 +271,7 @@
         functools.partial(backward_kernel, sweep=sweep),
         grid_spec=pltpu.PrefetchScalarGridSpec(
             num_scalar_prefetch=1,
-            grid=(slots // STEP,),
+            grid=(slots // BACK_STEP,),
             in_specs=in_specs,
             out_specs=[whole(shape) for shape, _ in shapes],
             scratch_shapes=[pltpu.VMEM((height, n_pixels), f32)],
@@ -308,18 +314,14 @@
     )(tab, table)
 
 
-def slot_tables(lists, listed, n_groups, per_group):
-    slots = lists.shape[1]
-    index = jnp.arange(slots, dtype=jnp.int32)
-    live = index[None, :] < listed[:, None]
-    group = jnp.where(live, lists // per_group, -1)
-    same = (group[:, :, None] == group[:, None, :]) & (index[None, None, :] < index[None, :, None])
-    place = jnp.sum(same.astype(jnp.int32), axis=2)
-    groups = jnp.arange(n_groups, dtype=jnp.int32)
-    hit = (group[:, None, None, :] == groups[None, None, :, None]) & (
-        place[:, None, None, :] == jnp.arange(2, dtype=jnp.int32)[None, :, None, None]
-    )
-    return jnp.sum(jnp.where(hit, lists[:, None, None, :] + 1, 0), axis=3) - 1
+def slot_table(blocks, listed, n_groups, per_group):
+    index = jnp.arange(blocks.shape[0], dtype=jnp.int32)
+    group = jnp.where(index < listed, blocks // per_group, -1)
+    same = (group[:, None] == group[None, :]) & (index[None, :] < index[:, None])
+    place = jnp.sum(same.astype(jnp.int32), axis=1)
+    key = jnp.where(group >= 0, place * n_groups + group, -1)
+    hit = key[None, :] == jnp.arange(2 * n_groups, dtype=jnp.int32)[:, None]
+    return jnp.sum(jnp.where(hit, blocks[None, :] + 1, 0), axis=1) - 1
 
 
 def exchange(x, both_places):
@@ -342,24 +344,22 @@
     col = lax.axis_index("col")
     slots = tile_block_list.shape[2]
 
-    record = jnp.zeros((8, 128), f32)
-    record = lax.dynamic_update_slice(record, antenna_settings[0], (0, 0))
-    meta = jnp.concatenate(
-        [tile_block_list.reshape(slots), tile_block_count.reshape(1)]
-    ).astype(f32)
-    record = lax.dynamic_update_slice(record, meta[None, :], (5, 0))
+    record = jnp.pad(antenna_settings[0], ((0, 3), (0, 0)))
     mine = lax.all_to_all(jnp.broadcast_to(record, (n_col, 8, 128)), "col", 0, 0, tiled=True)
+    tab = slot_table(tile_block_list.reshape(slots), tile_block_count.reshape(()), n_row, n_col)
+    line = jnp.pad(tab.astype(f32), (0, 128 - 2 * n_row))
+    mine, initial_estimate0 = lax.optimization_barrier((mine, initial_estimate0))
+    here = lax.broadcasted_iota(jnp.int32, mine.shape, 1) == 5
     every = lax.all_to_all(
-        jnp.broadcast_to(mine, (n_row, n_col, 8, 128)), "row", 0, 0, tiled=True
+        jnp.broadcast_to(jnp.where(here, line, mine), (n_row, n_col, 8, 128)),
+        "row",
+        0,
+        0,
+        tiled=True,
     )
     records = every.reshape(n_row * n_col, 8, 128)
-    own = slot_tables(
-        tile_block_list.reshape(1, slots), tile_block_count.reshape(1), n_row, n_col
-    )
-    tab = own.reshape(2 * n_row)
-    column_meta = lax.dynamic_index_in_dim(every[:, :, 5, :], col, 1, keepdims=False)
-    column_meta = column_meta.astype(jnp.int32)
-    tables = slot_tables(column_meta[:, :slots], column_meta[:, slots], n_row, n_col)
+    tables = lax.dynamic_index_in_dim(every[:, :, 5, : 2 * n_row], col, 1, keepdims=False)
+    tables = tables.astype(jnp.int32).reshape(n_row, 2, n_row)
     theirs = lax.dynamic_index_in_dim(tables, row, 2, keepdims=False)
     theirs = jnp.where(theirs >= 0, theirs - row * n_col, -1).T.reshape(2 * n_row)
 

time: 264 us -> 259 us (0.981); the launches traced: 261 us -> 260 us
  Pallas kernels: 84.7 us -> 97.6 us
  blocking collectives: 125 us -> 115 us
    all_to_all x2, blocking collectives: 44.5 us -> 22.8 us  [shards(): pieces = lax.all_to_all(group_sum, 'col', 0, 0, tiled=True)]
    all_to_all x4, blocking collectives: 69.2 us -> 81.3 us  [full(): return lax.all_to_all(x, 'row', 0, 0, tiled=True)]
    pallas_call x1, Pallas kernels: 24.7 us -> 33 us  [build(): pl.pallas_call(functools.partial(build_kernel, rows=rows, cols=cols), gri...]
    pallas_call x2, Pallas kernels: 41.9 us -> 45.2 us  [backward(): pl.pallas_call(functools.partial(backward_kernel, sweep=sweep), grid_spec...]
where the time goes in v5:
time: 259 us; the launch traced here: 260 us
  blocking collectives  115 us (44%)
  Pallas kernels  97.6 us (38%)
  starting transfers between devices  15.9 us (6%)
  waiting for transfers between devices  14.8 us (6%)
  local copies, waits for them, and re-layouts  9.6 us (4%)
  other arithmetic  4.99 us (2%)
    all_to_all x4, blocking collectives, full(): return lax.all_to_all(x, 'row', 0, 0, tiled=True)  81.3 us
    pallas_call x2, Pallas kernels, backward(): pl.pallas_call(functools.partial(backward_kernel, sweep=sweep), grid_spec...  45.2 us
    pallas_call x1, Pallas kernels, build(): pl.pallas_call(functools.partial(build_kernel, rows=rows, cols=cols), gri...  33 us
    all_to_all x2, blocking collectives, shards(): pieces = lax.all_to_all(group_sum, 'col', 0, 0, tiled=True)  22.8 us
    pallas_call x1, Pallas kernels, forward(): pl.pallas_call(forward_kernel, grid_spec=pltpu.PrefetchScalarGridSpec(num...  15.8 us
    all_to_all x1, blocking collectives, shards(): lax.all_to_all(jnp.broadcast_to(ratio, (n_col,) + ratio.shape), 'col', 0,...  11.3 us
    all_to_all x1, starting transfers between devices, shards(): lax.all_to_all(jnp.broadcast_to(jnp.where(here, line, mine), (n_row, n_co...  7.88 us
    all_to_all x1, waiting for transfers between devices, shards(): lax.all_to_all(jnp.broadcast_to(ratio, (n_col,) + ratio.shape), 'col', 0,...  6.61 us
  transfers between devices with their start and end apart: 3, of which 3 were waited for; matrix products, arithmetic and copies ran while one was open for 4% of the time, Pallas kernels for 0%

profile of v5, /device:TPU:0, one launch (start us, length us, event | category | flops | bytes accessed | tf_op | source)
XLA Modules:
  0.0 259.8 jit_solution(17472348704792497015)
XLA Ops:
  1.4 4.6 %all-to-all-start.8 = ((f32[8,8,128]{2,1,0:T(8,128)}), f32[8,8,128]{2,1,0:T(8,128)S(1)}, u32[]{:S(2)}, u32[]{:S(2)}) async-start(f32[8,8,128]{2,1,0:T(8,128)} %broadcast_in_dim.44), calls=%async_computation.8 | async-start | bytes 65536 | tf_op jit(solution)/shard_map/all_to_all | solution.py:348
  8.8 2.6 %all-to-all-done.8 = f32[8,8,128]{2,1,0:T(8,128)S(1)} async-done(((f32[8,8,128]{2,1,0:T(8,128)}), f32[8,8,128]{2,1,0:T(8,128)S(1)}, u32[]{:S(2)}, u32[]{:S(2)}) %all-to-all-start.8) | async-done | bytes 32800 | tf_op jit(solution)/shard_map/all_to_all | solution.py:348
  12.4 7.9 %all-to-all-start.9 = ((f32[16,8,8,128]{3,2,1,0:T(8,128)}), f32[16,8,8,128]{3,2,1,0:T(8,128)S(1)}, u32[]{:S(2)}, u32[]{:S(2)}) async-start(f32[16,8,8,128]{3,2,1,0:T(8,128)} %broadcast_in_dim.45), calls=%async_computation.9 | async-start | bytes 1048576 | tf_op jit(solution)/shard_map/all_to_all | solution.py:353
  21.7 1.7 reduce-precision_convert_fusion
  23.6 2.5 copy.89.est2
  26.1 5.6 %all-to-all-done.9 = f32[16,8,8,128]{3,2,1,0:T(8,128)S(1)} async-done(((f32[16,8,8,128]{3,2,1,0:T(8,128)}), f32[16,8,8,128]{3,2,1,0:T(8,128)S(1)}, u32[]{:S(2)}, u32[]{:S(2)}) %all-to-all-start.9) | async-done | bytes 524320 | tf_op jit(solution)/shard_map/all_to_all | solution.py:353
  33.4 33.0 %build_cover.1 = (bf16[4096,4096]{1,0:T(8,128)(2,1)}, f8e5m2[4096,4096]{1,0:T(32,128)(4,1)}, f32[16,2,96,128]{3,2,1,0:T(8,128)S(1)}) custom-call(s32[32]{0:T(128)} %get-tuple-element.48.tab, s32[2]{0:T(128)} %pad_add_fusion.origin, f32[128,8,128]{2,1,0:T(8,128)} %bitcast.59, f32[16,256]{1,0:T(8,128)} %clut.1, bf16[4096,256]{1,0:T(8,128)(2,1)} %copy.89.est2), custom_call_target="tpu_custom_call" | custom-call | tf_op jit(solution)/shard_map/build_cover/pallas_call | solution.py:206
  66.4 19.0 %conditional.4 = (f32[16,2,96,128]{3,2,1,0:T(8,128)S(1)}) conditional(s32[]{:T(128)} %convert_element_type.38, f32[16,2,96,128]{3,2,1,0:T(8,128)S(1)} %get-tuple-element.35, f32[16,2,96,128]{3,2,1,0:T(8,128)S(1)} %get-tuple-element.35), branch_computations={%region_3.4_spmd, %region_4.5_spmd} | conditional | bytes 5505036 | solution.py:335
  66.4 19.0 %all_to_all.63 = f32[16,2,96,128]{3,2,1,0:T(8,128)S(1)} all-to-all(f32[16,2,96,128]{3,2,1,0:T(8,128)S(1)} %param.1), channel_id=1, replica_groups=mesh['row'=16,'col'=8] {'row'}, dimensions={0} | all-to-all | bytes 3145728 | tf_op jit(solution)/shard_map/cond/branch_1_fun/all_to_all | solution.py:333
  86.5 11.5 %all_to_all.70 = f32[8,96,128]{2,1,0:T(8,128)S(1)} all-to-all(f32[8,96,128]{2,1,0:T(8,128)S(1)} %combine_slots.2), channel_id=1, replica_groups=mesh['row'=16,'col'=8] {'col'}, dimensions={0} | all-to-all | bytes 786432 | tf_op jit(solution)/shard_map/all_to_all | solution.py:378
  98.8 3.5 %all-to-all-start.11 = ((f32[8,96,128]{2,1,0:T(8,128)}), f32[8,96,128]{2,1,0:T(8,128)S(1)}, u32[]{:S(2)}, u32[]{:S(2)}) async-start(f32[8,96,128]{2,1,0:T(8,128)} %broadcast_in_dim.47), calls=%async_computation.11 | async-start | bytes 786432 | tf_op jit(solution)/shard_map/all_to_all | solution.py:380
  102.3 2.2 copy.99
  104.5 6.6 %all-to-all-done.11.table = f32[8,96,128]{2,1,0:T(8,128)S(1)} async-done(((f32[8,96,128]{2,1,0:T(8,128)}), f32[8,96,128]{2,1,0:T(8,128)S(1)}, u32[]{:S(2)}, u32[]{:S(2)}) %all-to-all-start.11) | async-done | bytes 393248 | tf_op jit(solution)/shard_map/all_to_all | solution.py:380
  111.9 21.6 %conditional.5 = (f32[16,2,96,128]{3,2,1,0:T(8,128)S(1)}) conditional(s32[]{:T(128)} %convert_element_type.38, f32[16,2,96,128]{3,2,1,0:T(8,128)S(1)} %pick_slots.2, f32[16,2,96,128]{3,2,1,0:T(8,128)S(1)} %pick_slots.2), branch_computations={%region_6.7_spmd, %region_7.8_spmd} | conditional | bytes 5505036 | solution.py:335
  111.9 21.6 %all_to_all.65 = f32[16,2,96,128]{3,2,1,0:T(8,128)S(1)} all-to-all(f32[16,2,96,128]{3,2,1,0:T(8,128)S(1)} %param.3), channel_id=1, replica_groups=mesh['row'=16,'col'=8] {'row'}, dimensions={0} | all-to-all | bytes 3145728 | tf_op jit(solution)/shard_map/cond/branch_1_fun/all_to_all | solution.py:333
  133.6 23.1 %backward_product.2 = (f32[96,4096]{1,0:T(8,128)}, bf16[4096,256]{1,0:T(8,128)(2,1)}, f32[8,4096]{1,0:T(8,128)}) custom-call(s32[32]{0:T(128)} %get-tuple-element.48.tab, f32[128,8,128]{2,1,0:T(8,128)} %bitcast.60, f32[16,2,96,128]{3,2,1,0:T(8,128)S(1)} %get-tuple-element.42.ratios, f32[96,4096]{1,0:T(8,128)} %bitcast.64, ...), custom_call_target="tpu_custom_call" | custom-call | tf_op jit(solution)/shard_map/backward_product/pallas_call | solution.py:270
  156.6 15.8 %forward_product.1 = f32[16,2,96,128]{3,2,1,0:T(8,128)S(1)} custom-call(s32[32]{0:T(128)} %get-tuple-element.48.tab, f32[128,8,128]{2,1,0:T(8,128)} %bitcast.61, bf16[4096,256]{1,0:T(8,128)(2,1)} %get-tuple-element.38.est2, bf16[4096,4096]{1,0:T(8,128)(2,1)} %get-tuple-element.36.hi), custom_call_target="tpu_custom_call" | custom-call | tf_op jit(solution)/shard_map/forward_product/pallas_call | solution.py:233
  172.5 19.0 %conditional.6 = (f32[16,2,96,128]{3,2,1,0:T(8,128)S(1)}) conditional(s32[]{:T(128)} %convert_element_type.38, f32[16,2,96,128]{3,2,1,0:T(8,128)S(1)} %forward_product.1, f32[16,2,96,128]{3,2,1,0:T(8,128)S(1)} %forward_product.1), branch_computations={%region_8.9_spmd, %region_9.10_spmd} | conditional | bytes 5505036 | solution.py:335
  172.5 19.0 %all_to_all.67 = f32[16,2,96,128]{3,2,1,0:T(8,128)S(1)} all-to-all(f32[16,2,96,128]{3,2,1,0:T(8,128)S(1)} %param.5), channel_id=1, replica_groups=mesh['row'=16,'col'=8] {'row'}, dimensions={0} | all-to-all | bytes 3145728 | tf_op jit(solution)/shard_map/cond/branch_1_fun/all_to_all | solution.py:333
  192.6 11.3 %all_to_all.71 = f32[8,96,128]{2,1,0:T(8,128)S(1)} all-to-all(f32[8,96,128]{2,1,0:T(8,128)S(1)} %combine_slots.3), channel_id=1, replica_groups=mesh['row'=16,'col'=8] {'col'}, dimensions={0} | all-to-all | bytes 786432 | tf_op jit(solution)/shard_map/all_to_all | solution.py:378
  204.0 11.3 %all_to_all.72.table = f32[8,96,128]{2,1,0:T(8,128)S(1)} all-to-all(f32[8,96,128]{2,1,0:T(8,128)S(1)} %broadcast_in_dim.48), channel_id=1, replica_groups=mesh['row'=16,'col'=8] {'col'}, dimensions={0} | all-to-all | bytes 786432 | tf_op jit(solution)/shard_map/all_to_all | solution.py:380
  216.1 21.7 %conditional.7 = (f32[16,2,96,128]{3,2,1,0:T(8,128)S(1)}) conditional(s32[]{:T(128)} %convert_element_type.38, f32[16,2,96,128]{3,2,1,0:T(8,128)S(1)} %pick_slots.3, f32[16,2,96,128]{3,2,1,0:T(8,128)S(1)} %pick_slots.3), branch_computations={%region_11.12_spmd, %region_12.13_spmd} | conditional | bytes 5505036 | solution.py:335
  216.1 21.6 %all_to_all.69 = f32[16,2,96,128]{3,2,1,0:T(8,128)S(1)} all-to-all(f32[16,2,96,128]{3,2,1,0:T(8,128)S(1)} %param.7), channel_id=1, replica_groups=mesh['row'=16,'col'=8] {'row'}, dimensions={0} | all-to-all | bytes 3145728 | tf_op jit(solution)/shard_map/cond/branch_1_fun/all_to_all | solution.py:333
  237.7 22.1 %backward_product.3 = f32[96,16,256]{2,1,0:T(8,128)} custom-call(s32[32]{0:T(128)} %get-tuple-element.48.tab, f32[128,8,128]{2,1,0:T(8,128)} %bitcast.62, f32[16,2,96,128]{3,2,1,0:T(8,128)S(1)} %get-tuple-element.44.ratios, f32[96,4096]{1,0:T(8,128)} %get-tuple-element.39.est, bf16[4096,4096]{1,0:T(8,128)(2,1)} %get-tuple-element.36.hi, ...), custom_call_target="tpu_custom_call" | custom-call | tf_op jit(solution)/shard_map/backward_product/pallas_call | solution.py:270
  (42 shorter events, 11.8 us)
Async XLA Ops:
  0.0 20.2 %copy-start.1 = (f32[96,16,256]{2,1,0:T(8,128)S(1)}, f32[96,16,256]{2,1,0:T(8,128)}, u32[]{:S(2)}) copy-start(f32[96,16,256]{2,1,0:T(8,128)} %param.14) | copy-start | bytes 4718596
  1.4 10.0 %all-to-all-start.8 = ((f32[8,8,128]{2,1,0:T(8,128)}), f32[8,8,128]{2,1,0:T(8,128)S(1)}, u32[]{:S(2)}, u32[]{:S(2)}) async-start(f32[8,8,128]{2,1,0:T(8,128)} %broadcast_in_dim.44), calls=%async_computation.8 | async-start | bytes 65536 | tf_op jit(solution)/shard_map/all_to_all | solution.py:348
  12.4 19.3 %all-to-all-start.9 = ((f32[16,8,8,128]{3,2,1,0:T(8,128)}), f32[16,8,8,128]{3,2,1,0:T(8,128)S(1)}, u32[]{:S(2)}, u32[]{:S(2)}) async-start(f32[16,8,8,128]{3,2,1,0:T(8,128)} %broadcast_in_dim.45), calls=%async_computation.9 | async-start | bytes 1048576 | tf_op jit(solution)/shard_map/all_to_all | solution.py:353
  31.7 1.8 copy-start
  85.4 12.6 %copy-start.3 = (s32[1,96,128]{2,1,0:T(8,128)S(1)}, s32[1,96,128]{2,1,0:T(8,128)}, u32[]{:S(2)}) copy-start(s32[1,96,128]{2,1,0:T(8,128)} %param.16) | copy-start | bytes 147460
  86.5 15.8 %copy-start.2 = (f32[96,16,256]{2,1,0:T(8,128)S(1)}, f32[96,16,256]{2,1,0:T(8,128)}, u32[]{:S(2)}) copy-start(f32[96,16,256]{2,1,0:T(8,128)} %param.14) | copy-start | bytes 4718596
  98.8 12.3 %all-to-all-start.11 = ((f32[8,96,128]{2,1,0:T(8,128)}), f32[8,96,128]{2,1,0:T(8,128)S(1)}, u32[]{:S(2)}, u32[]{:S(2)}) async-start(f32[8,96,128]{2,1,0:T(8,128)} %broadcast_in_dim.47), calls=%async_computation.11 | async-start | bytes 786432 | tf_op jit(solution)/shard_map/all_to_all | solution.py:380
  191.5 12.4 %copy-start.4 = (s32[1,96,128]{2,1,0:T(8,128)S(1)}, s32[1,96,128]{2,1,0:T(8,128)}, u32[]{:S(2)}) copy-start(s32[1,96,128]{2,1,0:T(8,128)} %param.16) | copy-start | bytes 147460

commit v6 on v5

--- a/solution.py
+++ b/solution.py
@@ -10,7 +10,6 @@
 LOG2E = 1.4426950408889634
 CLUTTER_MAX = 1.5
 BUILD_STEP = 4
-FORWARD_STEP = 8
 BACK_STEP = 8
 CHUNK = 512
 STORE = 65536.0
@@ -96,33 +95,28 @@
         part[k, 0] = total[k * 128 : (k + 1) * 128, :].T[:maps, :] * scale
 
 
-def forward_kernel(tab, records, est2, hi, part):
-    step = pl.program_id(0)
-    count = part.shape[0]
-
-    @pl.when(any_live(tab, step * count, count))
-    def _():
-        forward_dot(tab, step, records, est2, hi, part)
-
-
 def backward_kernel(tab, records, ratios, est, hi, lo, *rest, sweep):
     step = pl.program_id(0)
     maps, n_pixels = est.shape
     if sweep == 0:
-        est_out, est2_out, sens_out, acc = rest
+        est_out, sens_out, part, est2, acc = rest
+        steps = pl.num_programs(0) // 2
     else:
         sens_in, est_out, acc = rest
+        steps = pl.num_programs(0)
+    own = jnp.where(step < steps, step, 2 * steps - 1 - step)
+    live_step = any_live(tab, own * BACK_STEP, BACK_STEP)
 
     @pl.when(step == 0)
     def _():
         acc[...] = jnp.zeros_like(acc)
 
-    @pl.when(any_live(tab, step * BACK_STEP, BACK_STEP))
+    @pl.when(jnp.logical_and(live_step, step < steps))
     def _():
         wide = []
         thin = []
         for k in range(BACK_STEP):
-            block = tab[step * BACK_STEP + k]
+            block = tab[own * BACK_STEP + k]
             live = block >= 0
             scale = antenna_scale(records[jnp.maximum(block, 0)])
             stack = jnp.where(live, ratios[k, 0] * scale, 0.0)
@@ -141,7 +135,7 @@
             low = jnp.dot(thin, lo[:, at : at + chunk], preferred_element_type=f32)
             acc[:, at : at + chunk] += both[:height, :] + (both[height:, :] + low)
 
-    @pl.when(step == pl.num_programs(0) - 1)
+    @pl.when(step == steps - 1)
     def _():
         if sweep == 0:
             sens = acc[maps : maps + 1, :]
@@ -150,13 +144,19 @@
             est_out[...] = new
             turned = jnp.concatenate([new, jnp.zeros((128 - maps, n_pixels), f32)], axis=0).T
             top, remainder = split(turned)
-            est2_out[:, :128] = top
-            est2_out[:, 128:] = remainder
+            est2[:, :128] = top
+            est2[:, 128:] = remainder
         else:
             rows, cols = est_out.shape[1:]
             for r in range(rows):
                 at = slice(r * cols, (r + 1) * cols)
                 est_out[:, r, :] = est[:, at] * acc[:maps, at] / sens_in[0:1, at]
+
+    if sweep == 0:
+
+        @pl.when(jnp.logical_and(live_step, step >= steps))
+        def _():
+            forward_dot(tab, own, records, est2, hi, part)
 
 
 def combine_kernel(tab, recv, out):
@@ -226,57 +226,59 @@
     )(tab, origin, records, clut, est2)
 
 
-def forward(tab, records, est2, hi, maps):
-    slots = tab.shape[0]
-    n_pixels = est2.shape[0]
-    tall = FORWARD_STEP * 128
-    return pl.pallas_call(
-        forward_kernel,
-        grid_spec=pltpu.PrefetchScalarGridSpec(
-            num_scalar_prefetch=1,
-            grid=(slots // FORWARD_STEP,),
-            in_specs=[
-                whole(records.shape),
-                whole(est2.shape),
-                spec((tall, n_pixels), lambda i, *_: (i, 0)),
-            ],
-            out_specs=place_spec(slots, maps, FORWARD_STEP),
-        ),
-        out_shape=jax.ShapeDtypeStruct((slots // 2, 2, maps, 128), f32),
-        compiler_params=params(56),
-        name="forward_product",
-    )(tab, records, est2, hi)
-
-
 def backward(tab, records, ratios, est, hi, lo, sens, sweep, rows, cols):
     slots = tab.shape[0]
     maps, n_pixels = est.shape
     tall = BACK_STEP * 128
+    steps = slots // BACK_STEP
+    per = slots // 2 // BACK_STEP
     height = maps + (SENS_ROWS if sweep == 0 else 0)
+
+    def down(i):
+        return jnp.minimum(i, steps - 1)
+
+    def turn(i):
+        return jnp.where(i < steps, i, 2 * steps - 1 - i)
+
+    def up(i):
+        return jnp.minimum(2 * steps - 1 - i, steps - 1)
+
     operands = [records, ratios, est, hi, lo]
     in_specs = [
         whole(records.shape),
-        place_spec(slots, maps, BACK_STEP),
+        spec((BACK_STEP, 1, maps, 128), lambda i, *_: (down(i) % per, down(i) // per, 0, 0)),
         whole(est.shape),
-        spec((tall, n_pixels), lambda i, *_: (i, 0)),
-        spec((tall, n_pixels), lambda i, *_: (i, 0)),
+        spec((tall, n_pixels), lambda i, *_: (turn(i), 0)),
+        spec((tall, n_pixels), lambda i, *_: (down(i), 0)),
     ]
+    scratch = [pltpu.VMEM((height, n_pixels), f32)]
     if sweep == 0:
-        shapes = [((maps, n_pixels), f32), ((n_pixels, 256), bf16), ((8, n_pixels), f32)]
+        out_specs = [
+            whole((maps, n_pixels)),
+            whole((8, n_pixels)),
+            spec((BACK_STEP, 1, maps, 128), lambda i, *_: (up(i) % per, up(i) // per, 0, 0)),
+        ]
+        out_shape = [
+            jax.ShapeDtypeStruct((maps, n_pixels), f32),
+            jax.ShapeDtypeStruct((8, n_pixels), f32),
+            jax.ShapeDtypeStruct((slots // 2, 2, maps, 128), f32),
+        ]
+        scratch = [pltpu.VMEM((n_pixels, 256), bf16)] + scratch
     else:
-        shapes = [((maps, rows, cols), f32)]
+        out_specs = [whole((maps, rows, cols))]
+        out_shape = [jax.ShapeDtypeStruct((maps, rows, cols), f32)]
         operands.append(sens)
         in_specs.append(whole(sens.shape))
     return pl.pallas_call(
         functools.partial(backward_kernel, sweep=sweep),
         grid_spec=pltpu.PrefetchScalarGridSpec(
             num_scalar_prefetch=1,
-            grid=(slots // BACK_STEP,),
+            grid=((2 if sweep == 0 else 1) * steps,),
             in_specs=in_specs,
-            out_specs=[whole(shape) for shape, _ in shapes],
-            scratch_shapes=[pltpu.VMEM((height, n_pixels), f32)],
+            out_specs=out_specs,
+            scratch_shapes=scratch,
         ),
-        out_shape=[jax.ShapeDtypeStruct(shape, dtype) for shape, dtype in shapes],
+        out_shape=out_shape,
         compiler_params=params(56),
         name="backward_product",
     )(tab, *operands)
@@ -372,8 +374,6 @@
     hi, lo, part = build(tab, origin, records, clutter, est2, maps, rows, cols)
     sens = None
     for sweep in range(ITERS):
-        if sweep > 0:
-            part = forward(tab, records, est2, hi, maps)
         group_sum = combine(theirs, exchange(part, both_places), n_col)
         pieces = lax.all_to_all(group_sum, "col", 0, 0, tiled=True)
         ratio = wanted / jnp.sum(pieces, axis=0)
@@ -384,7 +384,7 @@
         back = exchange(sent, both_places)
         done = backward(tab, records, back, est, hi, lo, sens, sweep, rows, cols)
         if sweep == 0:
-            est, est2, sens = done
+            est, sens, part = done
     return done[0]
 
 

time: 259 us -> 251 us (0.969)
  the two profiles are of different devices: /device:TPU:0 before, /device:TPU:1 now
where the time goes in v6:
time: 251 us; the launch traced here: 249 us
  blocking collectives  110 us (44%)
  Pallas kernels  92.8 us (37%)
  starting transfers between devices  17.8 us (7%)
  waiting for transfers between devices  12.3 us (5%)
  local copies, waits for them, and re-layouts  9.56 us (4%)
  other arithmetic  4.93 us (2%)
    all_to_all x4, blocking collectives, full(): return lax.all_to_all(x, 'row', 0, 0, tiled=True)  79.3 us
    pallas_call x2, Pallas kernels, backward(): pl.pallas_call(functools.partial(backward_kernel, sweep=sweep), grid_spec...  56.2 us
    pallas_call x1, Pallas kernels, build(): pl.pallas_call(functools.partial(build_kernel, rows=rows, cols=cols), gri...  33 us
    all_to_all x2, blocking collectives, shards(): pieces = lax.all_to_all(group_sum, 'col', 0, 0, tiled=True)  19.5 us
    all_to_all x1, blocking collectives, shards(): lax.all_to_all(jnp.broadcast_to(ratio, (n_col,) + ratio.shape), 'col', 0,...  11.3 us
    all_to_all x1, starting transfers between devices, shards(): lax.all_to_all(jnp.broadcast_to(jnp.where(here, line, mine), (n_row, n_co...  7.6 us
    all_to_all x1, starting transfers between devices, shards(): lax.all_to_all(jnp.broadcast_to(record, (n_col, 8, 128)), 'col', 0, 0, ti...  5.97 us
    all_to_all x1, waiting for transfers between devices, shards(): lax.all_to_all(jnp.broadcast_to(ratio, (n_col,) + ratio.shape), 'col', 0,...  5.85 us
  transfers between devices with their start and end apart: 3, of which 3 were waited for; matrix products, arithmetic and copies ran while one was open for 4% of the time, Pallas kernels for 0%

profile of v6, /device:TPU:1, one launch (start us, length us, event | category | flops | bytes accessed | tf_op | source)
XLA Modules:
  0.0 249.0 jit_solution(6084246861635114938)
XLA Ops:
  1.4 6.0 %all-to-all-start.8 = ((f32[8,8,128]{2,1,0:T(8,128)}), f32[8,8,128]{2,1,0:T(8,128)S(1)}, u32[]{:S(2)}, u32[]{:S(2)}) async-start(f32[8,8,128]{2,1,0:T(8,128)} %broadcast_in_dim.44), calls=%async_computation.8 | async-start | bytes 65536 | tf_op jit(solution)/shard_map/all_to_all | solution.py:350
  10.1 2.0 all-to-all-done.8
  13.0 7.6 %all-to-all-start.9 = ((f32[16,8,8,128]{3,2,1,0:T(8,128)}), f32[16,8,8,128]{3,2,1,0:T(8,128)S(1)}, u32[]{:S(2)}, u32[]{:S(2)}) async-start(f32[16,8,8,128]{3,2,1,0:T(8,128)} %broadcast_in_dim.45), calls=%async_computation.9 | async-start | bytes 1048576 | tf_op jit(solution)/shard_map/all_to_all | solution.py:355
  20.6 1.4 reshape.151
  22.1 1.7 reduce-precision_convert_fusion
  24.0 2.5 %copy.89.est2 = bf16[4096,256]{1,0:T(8,128)(2,1)} copy(bf16[4096,256]{0,1:T(8,128)(2,1)S(1)} %bitcast.62) | data formatting | bytes 4194304 | tf_op jit(solution)/shard_map/convert_element_type | solution.py:33
  26.5 4.4 %all-to-all-done.9 = f32[16,8,8,128]{3,2,1,0:T(8,128)S(1)} async-done(((f32[16,8,8,128]{3,2,1,0:T(8,128)}), f32[16,8,8,128]{3,2,1,0:T(8,128)S(1)}, u32[]{:S(2)}, u32[]{:S(2)}) %all-to-all-start.9) | async-done | bytes 524320 | tf_op jit(solution)/shard_map/all_to_all | solution.py:355
  32.7 33.0 %build_cover.1 = (bf16[4096,4096]{1,0:T(8,128)(2,1)}, f8e5m2[4096,4096]{1,0:T(32,128)(4,1)}, f32[16,2,96,128]{3,2,1,0:T(8,128)S(1)}) custom-call(s32[32]{0:T(128)} %get-tuple-element.48.tab, s32[2]{0:T(128)} %pad_add_fusion.origin, f32[128,8,128]{2,1,0:T(8,128)} %bitcast.59, f32[16,256]{1,0:T(8,128)} %clut.1, bf16[4096,256]{1,0:T(8,128)(2,1)} %copy.89.est2), custom_call_target="tpu_custom_call" | custom-call | tf_op jit(solution)/shard_map/build_cover/pallas_call | solution.py:206
  65.7 18.3 %conditional.4 = (f32[16,2,96,128]{3,2,1,0:T(8,128)S(1)}) conditional(s32[]{:T(128)} %convert_element_type.38, f32[16,2,96,128]{3,2,1,0:T(8,128)S(1)} %get-tuple-element.35, f32[16,2,96,128]{3,2,1,0:T(8,128)S(1)} %get-tuple-element.35), branch_computations={%region_3.4_spmd, %region_4.5_spmd} | conditional | bytes 5505036 | solution.py:337
  65.7 18.3 %all_to_all.63 = f32[16,2,96,128]{3,2,1,0:T(8,128)S(1)} all-to-all(f32[16,2,96,128]{3,2,1,0:T(8,128)S(1)} %param.1), channel_id=1, replica_groups=mesh['row'=16,'col'=8] {'row'}, dimensions={0} | all-to-all | bytes 3145728 | tf_op jit(solution)/shard_map/cond/branch_1_fun/all_to_all | solution.py:335
  85.1 9.8 %all_to_all.70 = f32[8,96,128]{2,1,0:T(8,128)S(1)} all-to-all(f32[8,96,128]{2,1,0:T(8,128)S(1)} %combine_slots.2), channel_id=1, replica_groups=mesh['row'=16,'col'=8] {'col'}, dimensions={0} | all-to-all | bytes 786432 | tf_op jit(solution)/shard_map/all_to_all | solution.py:378
  95.7 4.2 %all-to-all-start.11 = ((f32[8,96,128]{2,1,0:T(8,128)}), f32[8,96,128]{2,1,0:T(8,128)S(1)}, u32[]{:S(2)}, u32[]{:S(2)}) async-start(f32[8,96,128]{2,1,0:T(8,128)} %broadcast_in_dim.47), calls=%async_computation.11 | async-start | bytes 786432 | tf_op jit(solution)/shard_map/all_to_all | solution.py:380
  99.9 2.2 copy.99
  102.2 5.9 %all-to-all-done.11.table = f32[8,96,128]{2,1,0:T(8,128)S(1)} async-done(((f32[8,96,128]{2,1,0:T(8,128)}), f32[8,96,128]{2,1,0:T(8,128)S(1)}, u32[]{:S(2)}, u32[]{:S(2)}) %all-to-all-start.11) | async-done | bytes 393248 | tf_op jit(solution)/shard_map/all_to_all | solution.py:380
  108.8 21.8 %conditional.5 = (f32[16,2,96,128]{3,2,1,0:T(8,128)S(1)}) conditional(s32[]{:T(128)} %convert_element_type.38, f32[16,2,96,128]{3,2,1,0:T(8,128)S(1)} %pick_slots.2, f32[16,2,96,128]{3,2,1,0:T(8,128)S(1)} %pick_slots.2), branch_computations={%region_6.7_spmd, %region_7.8_spmd} | conditional | bytes 5505036 | solution.py:337
  108.8 21.7 %all_to_all.65 = f32[16,2,96,128]{3,2,1,0:T(8,128)S(1)} all-to-all(f32[16,2,96,128]{3,2,1,0:T(8,128)S(1)} %param.3), channel_id=1, replica_groups=mesh['row'=16,'col'=8] {'row'}, dimensions={0} | all-to-all | bytes 3145728 | tf_op jit(solution)/shard_map/cond/branch_1_fun/all_to_all | solution.py:335
  130.5 34.2 %backward_product.2 = (f32[96,4096]{1,0:T(8,128)}, f32[8,4096]{1,0:T(8,128)}, f32[16,2,96,128]{3,2,1,0:T(8,128)S(1)}) custom-call(s32[32]{0:T(128)} %get-tuple-element.48.tab, f32[128,8,128]{2,1,0:T(8,128)} %bitcast.60, f32[16,2,96,128]{3,2,1,0:T(8,128)S(1)} %get-tuple-element.42.ratios, f32[96,4096]{1,0:T(8,128)} %bitcast.63, ...), custom_call_target="tpu_custom_call" | custom-call | tf_op jit(solution)/shard_map/backward_product/pallas_call | solution.py:272
  164.7 17.6 %conditional.6 = (f32[16,2,96,128]{3,2,1,0:T(8,128)S(1)}) conditional(s32[]{:T(128)} %convert_element_type.38, f32[16,2,96,128]{3,2,1,0:T(8,128)S(1)} %get-tuple-element.38, f32[16,2,96,128]{3,2,1,0:T(8,128)S(1)} %get-tuple-element.38), branch_computations={%region_8.9_spmd, %region_9.10_spmd} | conditional | bytes 5505036 | solution.py:337
  164.7 17.6 %all_to_all.67 = f32[16,2,96,128]{3,2,1,0:T(8,128)S(1)} all-to-all(f32[16,2,96,128]{3,2,1,0:T(8,128)S(1)} %param.5), channel_id=1, replica_groups=mesh['row'=16,'col'=8] {'row'}, dimensions={0} | all-to-all | bytes 3145728 | tf_op jit(solution)/shard_map/cond/branch_1_fun/all_to_all | solution.py:335
  183.4 9.7 %all_to_all.71 = f32[8,96,128]{2,1,0:T(8,128)S(1)} all-to-all(f32[8,96,128]{2,1,0:T(8,128)S(1)} %combine_slots.3), channel_id=1, replica_groups=mesh['row'=16,'col'=8] {'col'}, dimensions={0} | all-to-all | bytes 786432 | tf_op jit(solution)/shard_map/all_to_all | solution.py:378
  193.1 11.3 %all_to_all.72.table = f32[8,96,128]{2,1,0:T(8,128)S(1)} all-to-all(f32[8,96,128]{2,1,0:T(8,128)S(1)} %broadcast_in_dim.48), channel_id=1, replica_groups=mesh['row'=16,'col'=8] {'col'}, dimensions={0} | all-to-all | bytes 786432 | tf_op jit(solution)/shard_map/all_to_all | solution.py:380
  205.2 21.8 %conditional.7 = (f32[16,2,96,128]{3,2,1,0:T(8,128)S(1)}) conditional(s32[]{:T(128)} %convert_element_type.38, f32[16,2,96,128]{3,2,1,0:T(8,128)S(1)} %pick_slots.3, f32[16,2,96,128]{3,2,1,0:T(8,128)S(1)} %pick_slots.3), branch_computations={%region_11.12_spmd, %region_12.13_spmd} | conditional | bytes 5505036 | solution.py:337
  205.2 21.7 %all_to_all.69 = f32[16,2,96,128]{3,2,1,0:T(8,128)S(1)} all-to-all(f32[16,2,96,128]{3,2,1,0:T(8,128)S(1)} %param.7), channel_id=1, replica_groups=mesh['row'=16,'col'=8] {'row'}, dimensions={0} | all-to-all | bytes 3145728 | tf_op jit(solution)/shard_map/cond/branch_1_fun/all_to_all | solution.py:335
  227.0 22.0 %backward_product.3 = f32[96,16,256]{2,1,0:T(8,128)} custom-call(s32[32]{0:T(128)} %get-tuple-element.48.tab, f32[128,8,128]{2,1,0:T(8,128)} %bitcast.61, f32[16,2,96,128]{3,2,1,0:T(8,128)S(1)} %get-tuple-element.44.ratios, f32[96,4096]{1,0:T(8,128)} %get-tuple-element.39.est, bf16[4096,4096]{1,0:T(8,128)(2,1)} %get-tuple-element.36.hi, ...), custom_call_target="tpu_custom_call" | custom-call | tf_op jit(solution)/shard_map/backward_product/pallas_call | solution.py:272
  (39 shorter events, 10.3 us)
Async XLA Ops:
  0.0 20.6 %copy-start.1 = (f32[96,16,256]{2,1,0:T(8,128)S(1)}, f32[96,16,256]{2,1,0:T(8,128)}, u32[]{:S(2)}) copy-start(f32[96,16,256]{2,1,0:T(8,128)} %param.14) | copy-start | bytes 4718596
  1.4 10.7 %all-to-all-start.8 = ((f32[8,8,128]{2,1,0:T(8,128)}), f32[8,8,128]{2,1,0:T(8,128)S(1)}, u32[]{:S(2)}, u32[]{:S(2)}) async-start(f32[8,8,128]{2,1,0:T(8,128)} %broadcast_in_dim.44), calls=%async_computation.8 | async-start | bytes 65536 | tf_op jit(solution)/shard_map/all_to_all | solution.py:350
  13.0 17.9 %all-to-all-start.9 = ((f32[16,8,8,128]{3,2,1,0:T(8,128)}), f32[16,8,8,128]{3,2,1,0:T(8,128)S(1)}, u32[]{:S(2)}, u32[]{:S(2)}) async-start(f32[16,8,8,128]{3,2,1,0:T(8,128)} %broadcast_in_dim.45), calls=%async_computation.9 | async-start | bytes 1048576 | tf_op jit(solution)/shard_map/all_to_all | solution.py:355
  30.9 1.8 copy-start
  84.0 10.9 %copy-start.3 = (s32[1,96,128]{2,1,0:T(8,128)S(1)}, s32[1,96,128]{2,1,0:T(8,128)}, u32[]{:S(2)}) copy-start(s32[1,96,128]{2,1,0:T(8,128)} %param.16) | copy-start | bytes 147460
  85.0 14.9 %copy-start.2 = (f32[96,16,256]{2,1,0:T(8,128)S(1)}, f32[96,16,256]{2,1,0:T(8,128)}, u32[]{:S(2)}) copy-start(f32[96,16,256]{2,1,0:T(8,128)} %param.14) | copy-start | bytes 4718596
  95.7 12.3 %all-to-all-start.11 = ((f32[8,96,128]{2,1,0:T(8,128)}), f32[8,96,128]{2,1,0:T(8,128)S(1)}, u32[]{:S(2)}, u32[]{:S(2)}) async-start(f32[8,96,128]{2,1,0:T(8,128)} %broadcast_in_dim.47), calls=%async_computation.11 | async-start | bytes 786432 | tf_op jit(solution)/shard_map/all_to_all | solution.py:380

commit v7 on v6

--- a/solution.py
+++ b/solution.py
@@ -232,6 +232,9 @@
     tall = BACK_STEP * 128
     steps = slots // BACK_STEP
     per = slots // 2 // BACK_STEP
+    second = jnp.any(tab[slots // 2 :] >= 0)
+    used = jnp.where(second, steps, steps // 2).astype(jnp.int32)
+    tab = jnp.concatenate([tab, used.reshape(1)])
     height = maps + (SENS_ROWS if sweep == 0 else 0)
 
     def down(i):
@@ -248,8 +251,8 @@
         whole(records.shape),
         spec((BACK_STEP, 1, maps, 128), lambda i, *_: (down(i) % per, down(i) // per, 0, 0)),
         whole(est.shape),
-        spec((tall, n_pixels), lambda i, *_: (turn(i), 0)),
-        spec((tall, n_pixels), lambda i, *_: (down(i), 0)),
+        spec((tall, n_pixels), lambda i, tab: (jnp.minimum(turn(i), tab[slots] - 1), 0)),
+        spec((tall, n_pixels), lambda i, tab: (jnp.minimum(down(i), tab[slots] - 1), 0)),
     ]
     scratch = [pltpu.VMEM((height, n_pixels), f32)]
     if sweep == 0:
@@ -326,9 +329,14 @@
     return jnp.sum(jnp.where(hit, blocks[None, :] + 1, 0), axis=1) - 1
 
 
-def exchange(x, both_places):
+def exchange(x, both_places, cuts):
     def first(x):
-        got = lax.all_to_all(x[:, 0], "row", 0, 0, tiled=True)
+        size = x.shape[2] // cuts
+        got = [
+            lax.all_to_all(x[:, 0, c * size : (c + 1) * size], "row", 0, 0, tiled=True)
+            for c in range(cuts)
+        ]
+        got = jnp.concatenate(got, axis=1)
         return jnp.stack([got, jnp.zeros_like(got)], axis=1)
 
     def full(x):
@@ -374,14 +382,14 @@
     hi, lo, part = build(tab, origin, records, clutter, est2, maps, rows, cols)
     sens = None
     for sweep in range(ITERS):
-        group_sum = combine(theirs, exchange(part, both_places), n_col)
+        group_sum = combine(theirs, exchange(part, both_places, 1), n_col)
         pieces = lax.all_to_all(group_sum, "col", 0, 0, tiled=True)
         ratio = wanted / jnp.sum(pieces, axis=0)
         table = lax.all_to_all(
             jnp.broadcast_to(ratio, (n_col,) + ratio.shape), "col", 0, 0, tiled=True
         )
         sent = pick(theirs, table)
-        back = exchange(sent, both_places)
+        back = exchange(sent, both_places, 2)
         done = backward(tab, records, back, est, hi, lo, sens, sweep, rows, cols)
         if sweep == 0:
             est, sens, part = done

time: 251 us -> 247 us (0.984)
  the two profiles are of different devices: /device:TPU:1 before, /device:TPU:0 now
where the time goes in v7:
time: 247 us; the launch traced here: 248 us
  blocking collectives  135 us (55%)
  Pallas kernels  65.4 us (26%)
  starting transfers between devices  15.9 us (6%)
  waiting for transfers between devices  12.9 us (5%)
  local copies, waits for them, and re-layouts  10.4 us (4%)
  other arithmetic  6.42 us (3%)
    all_to_all x6, blocking collectives, first(): lax.all_to_all(x[:, 0, c * size:(c + 1) * size], 'row', 0, 0, tiled=True)  82.3 us
    all_to_all x2, blocking collectives, shards(): pieces = lax.all_to_all(group_sum, 'col', 0, 0, tiled=True)  41.1 us
    pallas_call x2, Pallas kernels, backward(): pl.pallas_call(functools.partial(backward_kernel, sweep=sweep), grid_spec...  35.4 us
    pallas_call x1, Pallas kernels, build(): pl.pallas_call(functools.partial(build_kernel, rows=rows, cols=cols), gri...  26.5 us
    all_to_all x1, blocking collectives, shards(): lax.all_to_all(jnp.broadcast_to(ratio, (n_col,) + ratio.shape), 'col', 0,...  11.3 us
    all_to_all x1, starting transfers between devices, shards(): lax.all_to_all(jnp.broadcast_to(jnp.where(here, line, mine), (n_row, n_co...  7.88 us
    all_to_all x1, waiting for transfers between devices, shards(): lax.all_to_all(jnp.broadcast_to(jnp.where(here, line, mine), (n_row, n_co...  5.57 us
  transfers between devices with their start and end apart: 3, of which 3 were waited for; matrix products, arithmetic and copies ran while one was open for 5% of the time, Pallas kernels for 0%

profile of v7, /device:TPU:0, one launch (start us, length us, event | category | flops | bytes accessed | tf_op | source)
XLA Modules:
  0.0 248.1 jit_solution(4934405948071821186)
XLA Ops:
  1.4 4.6 %all-to-all-start.10 = ((f32[8,8,128]{2,1,0:T(8,128)}), f32[8,8,128]{2,1,0:T(8,128)S(1)}, u32[]{:S(2)}, u32[]{:S(2)}) async-start(f32[8,8,128]{2,1,0:T(8,128)} %broadcast_in_dim.44), calls=%async_computation.10 | async-start | bytes 65536 | tf_op jit(solution)/shard_map/all_to_all | solution.py:358
  8.8 2.7 %all-to-all-done.10 = f32[8,8,128]{2,1,0:T(8,128)S(1)} async-done(((f32[8,8,128]{2,1,0:T(8,128)}), f32[8,8,128]{2,1,0:T(8,128)S(1)}, u32[]{:S(2)}, u32[]{:S(2)}) %all-to-all-start.10) | async-done | bytes 32800 | tf_op jit(solution)/shard_map/all_to_all | solution.py:358
  12.3 7.9 %all-to-all-start.11 = ((f32[16,8,8,128]{3,2,1,0:T(8,128)}), f32[16,8,8,128]{3,2,1,0:T(8,128)S(1)}, u32[]{:S(2)}, u32[]{:S(2)}) async-start(f32[16,8,8,128]{3,2,1,0:T(8,128)} %broadcast_in_dim.45), calls=%async_computation.11 | async-start | bytes 1048576 | tf_op jit(solution)/shard_map/all_to_all | solution.py:363
  23.6 2.5 %copy.99.est2 = bf16[4096,256]{1,0:T(8,128)(2,1)} copy(bf16[4096,256]{0,1:T(8,128)(2,1)S(1)} %bitcast.73) | data formatting | bytes 4194304 | tf_op jit(solution)/shard_map/convert_element_type | solution.py:33
  26.1 5.6 %all-to-all-done.11 = f32[16,8,8,128]{3,2,1,0:T(8,128)S(1)} async-done(((f32[16,8,8,128]{3,2,1,0:T(8,128)}), f32[16,8,8,128]{3,2,1,0:T(8,128)S(1)}, u32[]{:S(2)}, u32[]{:S(2)}) %all-to-all-start.11) | async-done | bytes 524320 | tf_op jit(solution)/shard_map/all_to_all | solution.py:363
  33.4 26.5 %build_cover.1 = (bf16[4096,4096]{1,0:T(8,128)(2,1)}, f8e5m2[4096,4096]{1,0:T(32,128)(4,1)}, f32[16,2,96,128]{3,2,1,0:T(8,128)S(1)}) custom-call(s32[32]{0:T(128)} %get-tuple-element.52.tab, s32[2]{0:T(128)} %pad_add_fusion.1.origin, f32[128,8,128]{2,1,0:T(8,128)} %bitcast.70, f32[16,256]{1,0:T(8,128)} %clut.1, bf16[4096,256]{1,0:T(8,128)(2,1)} %copy.99.est2), custom_call_target="tpu_custom_call" | custom-call | tf_op jit(solution)/shard_map/build_cover/pallas_call | solution.py:206
  60.0 16.4 %conditional.4 = (f32[16,2,96,128]{3,2,1,0:T(8,128)S(1)}) conditional(s32[]{:T(128)} %convert_element_type.38, f32[16,2,96,128]{3,2,1,0:T(8,128)S(1)} %get-tuple-element.35, f32[16,2,96,128]{3,2,1,0:T(8,128)S(1)} %get-tuple-element.35), branch_computations={%region_4.5_spmd, %region_5.6_spmd} | conditional | bytes 5505036 | solution.py:345
  60.0 16.2 %all_to_all.70 = f32[16,96,128]{2,1,0:T(8,128)S(1)} all-to-all(f32[16,96,128]{2,1,0:T(8,128)S(1)} %slice_bitcast_fusion), channel_id=1, replica_groups=mesh['row'=16,'col'=8] {'row'}, dimensions={0} | all-to-all | bytes 1572864 | tf_op jit(solution)/shard_map/cond/branch_0_fun/all_to_all | solution.py:336
  77.4 19.9 %all_to_all.80 = f32[8,96,128]{2,1,0:T(8,128)S(1)} all-to-all(f32[8,96,128]{2,1,0:T(8,128)S(1)} %combine_slots.2), channel_id=1, replica_groups=mesh['row'=16,'col'=8] {'col'}, dimensions={0} | all-to-all | bytes 786432 | tf_op jit(solution)/shard_map/all_to_all | solution.py:386
  98.1 3.5 %all-to-all-start.13 = ((f32[8,96,128]{2,1,0:T(8,128)}), f32[8,96,128]{2,1,0:T(8,128)S(1)}, u32[]{:S(2)}, u32[]{:S(2)}) async-start(f32[8,96,128]{2,1,0:T(8,128)} %broadcast_in_dim.47), calls=%async_computation.13 | async-start | bytes 786432 | tf_op jit(solution)/shard_map/all_to_all | solution.py:388
  103.5 2.2 copy.111
  105.7 4.6 %all-to-all-done.13.table = f32[8,96,128]{2,1,0:T(8,128)S(1)} async-done(((f32[8,96,128]{2,1,0:T(8,128)}), f32[8,96,128]{2,1,0:T(8,128)S(1)}, u32[]{:S(2)}, u32[]{:S(2)}) %all-to-all-start.13) | async-done | bytes 393248 | tf_op jit(solution)/shard_map/all_to_all | solution.py:388
  111.1 26.0 %conditional.5 = (f32[16,2,96,128]{3,2,1,0:T(8,128)S(1)}) conditional(s32[]{:T(128)} %convert_element_type.38, f32[16,2,96,128]{3,2,1,0:T(8,128)S(1)} %pick_slots.2, f32[16,2,96,128]{3,2,1,0:T(8,128)S(1)} %pick_slots.2), branch_computations={%region_7.8_spmd, %region_8.9_spmd} | conditional | flops 196608 | bytes 7077900 | solution.py:345
  111.2 12.9 %all_to_all.72 = f32[16,48,128]{2,1,0:T(8,128)S(1)} all-to-all(f32[16,48,128]{2,1,0:T(8,128)S(1)} %get-tuple-element.45), channel_id=1, replica_groups=mesh['row'=16,'col'=8] {'row'}, dimensions={0} | all-to-all | bytes 786432 | tf_op jit(solution)/shard_map/cond/branch_0_fun/all_to_all | solution.py:336
  124.1 12.6 %all_to_all.73 = f32[16,48,128]{2,1,0:T(8,128)S(1)} all-to-all(f32[16,48,128]{2,1,0:T(8,128)S(1)} %get-tuple-element.46), channel_id=1, replica_groups=mesh['row'=16,'col'=8] {'row'}, dimensions={0} | all-to-all | bytes 786432 | tf_op jit(solution)/shard_map/cond/branch_0_fun/all_to_all | solution.py:336
  137.2 20.8 %backward_product.2 = (f32[96,4096]{1,0:T(8,128)}, f32[8,4096]{1,0:T(8,128)}, f32[16,2,96,128]{3,2,1,0:T(8,128)S(1)}) custom-call(s32[33]{0:T(128)} %pad_add_fusion.tab, f32[128,8,128]{2,1,0:T(8,128)} %bitcast.71, f32[16,2,96,128]{3,2,1,0:T(8,128)S(1)} %get-tuple-element.42.ratios, f32[96,4096]{1,0:T(8,128)} %bitcast.74, ...), custom_call_target="tpu_custom_call" | custom-call | tf_op jit(solution)/shard_map/backward_product/pallas_call | solution.py:275
  158.0 15.3 %conditional.6 = (f32[16,2,96,128]{3,2,1,0:T(8,128)S(1)}) conditional(s32[]{:T(128)} %convert_element_type.38, f32[16,2,96,128]{3,2,1,0:T(8,128)S(1)} %get-tuple-element.38, f32[16,2,96,128]{3,2,1,0:T(8,128)S(1)} %get-tuple-element.38), branch_computations={%region_9.10_spmd, %region_10.11_spmd} | conditional | bytes 5505036 | solution.py:345
  158.1 15.1 %all_to_all.75 = f32[16,96,128]{2,1,0:T(8,128)S(1)} all-to-all(f32[16,96,128]{2,1,0:T(8,128)S(1)} %slice_bitcast_fusion.3), channel_id=1, replica_groups=mesh['row'=16,'col'=8] {'row'}, dimensions={0} | all-to-all | bytes 1572864 | tf_op jit(solution)/shard_map/cond/branch_0_fun/all_to_all | solution.py:336
  174.3 21.2 %all_to_all.81 = f32[8,96,128]{2,1,0:T(8,128)S(1)} all-to-all(f32[8,96,128]{2,1,0:T(8,128)S(1)} %combine_slots.3), channel_id=1, replica_groups=mesh['row'=16,'col'=8] {'col'}, dimensions={0} | all-to-all | bytes 786432 | tf_op jit(solution)/shard_map/all_to_all | solution.py:386
  195.6 11.3 %all_to_all.82.table = f32[8,96,128]{2,1,0:T(8,128)S(1)} all-to-all(f32[8,96,128]{2,1,0:T(8,128)S(1)} %broadcast_in_dim.48), channel_id=1, replica_groups=mesh['row'=16,'col'=8] {'col'}, dimensions={0} | all-to-all | bytes 786432 | tf_op jit(solution)/shard_map/all_to_all | solution.py:388
  207.7 25.8 %conditional.7 = (f32[16,2,96,128]{3,2,1,0:T(8,128)S(1)}) conditional(s32[]{:T(128)} %convert_element_type.38, f32[16,2,96,128]{3,2,1,0:T(8,128)S(1)} %pick_slots.3, f32[16,2,96,128]{3,2,1,0:T(8,128)S(1)} %pick_slots.3), branch_computations={%region_12.13_spmd, %region_13.14_spmd} | conditional | flops 196608 | bytes 7077900 | solution.py:345
  207.8 12.9 %all_to_all.77 = f32[16,48,128]{2,1,0:T(8,128)S(1)} all-to-all(f32[16,48,128]{2,1,0:T(8,128)S(1)} %get-tuple-element.47), channel_id=1, replica_groups=mesh['row'=16,'col'=8] {'row'}, dimensions={0} | all-to-all | bytes 786432 | tf_op jit(solution)/shard_map/cond/branch_0_fun/all_to_all | solution.py:336
  220.7 12.6 %all_to_all.78 = f32[16,48,128]{2,1,0:T(8,128)S(1)} all-to-all(f32[16,48,128]{2,1,0:T(8,128)S(1)} %get-tuple-element.48), channel_id=1, replica_groups=mesh['row'=16,'col'=8] {'row'}, dimensions={0} | all-to-all | bytes 786432 | tf_op jit(solution)/shard_map/cond/branch_0_fun/all_to_all | solution.py:336
  233.5 14.6 %backward_product.3 = f32[96,16,256]{2,1,0:T(8,128)} custom-call(s32[33]{0:T(128)} %pad_add_fusion.tab, f32[128,8,128]{2,1,0:T(8,128)} %bitcast.72, f32[16,2,96,128]{3,2,1,0:T(8,128)S(1)} %get-tuple-element.44.ratios, f32[96,4096]{1,0:T(8,128)} %get-tuple-element.39.est, bf16[4096,4096]{1,0:T(8,128)(2,1)} %get-tuple-element.36.hi, ...), custom_call_target="tpu_custom_call" | custom-call | tf_op jit(solution)/shard_map/backward_product/pallas_call | solution.py:275
  (55 shorter events, 15.5 us)
Async XLA Ops:
  0.0 20.2 %copy-start.1 = (f32[96,16,256]{2,1,0:T(8,128)S(1)}, f32[96,16,256]{2,1,0:T(8,128)}, u32[]{:S(2)}) copy-start(f32[96,16,256]{2,1,0:T(8,128)} %param.14) | copy-start | bytes 4718596
  1.4 10.0 %all-to-all-start.10 = ((f32[8,8,128]{2,1,0:T(8,128)}), f32[8,8,128]{2,1,0:T(8,128)S(1)}, u32[]{:S(2)}, u32[]{:S(2)}) async-start(f32[8,8,128]{2,1,0:T(8,128)} %broadcast_in_dim.44), calls=%async_computation.10 | async-start | bytes 65536 | tf_op jit(solution)/shard_map/all_to_all | solution.py:358
  12.3 19.3 %all-to-all-start.11 = ((f32[16,8,8,128]{3,2,1,0:T(8,128)}), f32[16,8,8,128]{3,2,1,0:T(8,128)S(1)}, u32[]{:S(2)}, u32[]{:S(2)}) async-start(f32[16,8,8,128]{3,2,1,0:T(8,128)} %broadcast_in_dim.45), calls=%async_computation.11 | async-start | bytes 1048576 | tf_op jit(solution)/shard_map/all_to_all | solution.py:363
  31.7 1.8 copy-start
  76.3 20.9 %copy-start.3 = (s32[1,96,128]{2,1,0:T(8,128)S(1)}, s32[1,96,128]{2,1,0:T(8,128)}, u32[]{:S(2)}) copy-start(s32[1,96,128]{2,1,0:T(8,128)} %param.16) | copy-start | bytes 147460
  77.3 24.2 %copy-start.4 = (s32[32]{0:T(128)S(1)}, s32[32]{0:T(128)}, u32[]{:S(2)}) copy-start(s32[32]{0:T(128)} %get-tuple-element.52.tab) | copy-start | bytes 388
  77.3 26.2 %copy-start.2 = (f32[96,16,256]{2,1,0:T(8,128)S(1)}, f32[96,16,256]{2,1,0:T(8,128)}, u32[]{:S(2)}) copy-start(f32[96,16,256]{2,1,0:T(8,128)} %param.14) | copy-start | bytes 4718596
  98.1 12.3 %all-to-all-start.13 = ((f32[8,96,128]{2,1,0:T(8,128)}), f32[8,96,128]{2,1,0:T(8,128)S(1)}, u32[]{:S(2)}, u32[]{:S(2)}) async-start(f32[8,96,128]{2,1,0:T(8,128)} %broadcast_in_dim.47), calls=%async_computation.13 | async-start | bytes 786432 | tf_op jit(solution)/shard_map/all_to_all | solution.py:388

commit v8 on v7

--- a/solution.py
+++ b/solution.py
@@ -11,7 +11,7 @@
 CLUTTER_MAX = 1.5
 BUILD_STEP = 4
 BACK_STEP = 8
-CHUNK = 512
+CHUNK = 2048
 STORE = 65536.0
 INV_MAX = 1e37
 SENS_ROWS = 16

time: 247 us -> 248 us (level); the launches traced: 248 us -> 246 us
  Pallas kernels: 65.4 us -> 56.2 us
  blocking collectives: 135 us -> 142 us
    all_to_all x6, blocking collectives: 82.3 us -> 88.6 us  [first(): lax.all_to_all(x[:, 0, c * size:(c + 1) * size], 'row', 0, 0, tiled=True)]
    pallas_call x2, Pallas kernels: 35.4 us -> 29.5 us  [backward(): pl.pallas_call(functools.partial(backward_kernel, sweep=sweep), grid_spec...]
    pallas_call x1, Pallas kernels: 26.5 us -> 23.3 us  [build(): pl.pallas_call(functools.partial(build_kernel, rows=rows, cols=cols), gri...]
where the time goes in v8:
time: 248 us; the launch traced here: 246 us
  blocking collectives  142 us (57%)
  Pallas kernels  56.2 us (23%)
  starting transfers between devices  15.9 us (6%)
  waiting for transfers between devices  12.9 us (5%)
  local copies, waits for them, and re-layouts  10.4 us (4%)
  other arithmetic  6.42 us (3%)
    all_to_all x6, blocking collectives, first(): lax.all_to_all(x[:, 0, c * size:(c + 1) * size], 'row', 0, 0, tiled=True)  88.6 us
    all_to_all x2, blocking collectives, shards(): pieces = lax.all_to_all(group_sum, 'col', 0, 0, tiled=True)  42.2 us
    pallas_call x2, Pallas kernels, backward(): pl.pallas_call(functools.partial(backward_kernel, sweep=sweep), grid_spec...  29.5 us
    pallas_call x1, Pallas kernels, build(): pl.pallas_call(functools.partial(build_kernel, rows=rows, cols=cols), gri...  23.3 us
    all_to_all x1, blocking collectives, shards(): lax.all_to_all(jnp.broadcast_to(ratio, (n_col,) + ratio.shape), 'col', 0,...  11.3 us
    all_to_all x1, starting transfers between devices, shards(): lax.all_to_all(jnp.broadcast_to(jnp.where(here, line, mine), (n_row, n_co...  7.88 us
    all_to_all x1, waiting for transfers between devices, shards(): lax.all_to_all(jnp.broadcast_to(jnp.where(here, line, mine), (n_row, n_co...  5.57 us
  transfers between devices with their start and end apart: 3, of which 3 were waited for; matrix products, arithmetic and copies ran while one was open for 5% of the time, Pallas kernels for 0%

profile of v8, /device:TPU:0, one launch (start us, length us, event | category | flops | bytes accessed | tf_op | source)
XLA Modules:
  0.0 246.5 jit_solution(8109871021414168094)
XLA Ops:
  1.4 4.6 %all-to-all-start.10 = ((f32[8,8,128]{2,1,0:T(8,128)}), f32[8,8,128]{2,1,0:T(8,128)S(1)}, u32[]{:S(2)}, u32[]{:S(2)}) async-start(f32[8,8,128]{2,1,0:T(8,128)} %broadcast_in_dim.44), calls=%async_computation.10 | async-start | bytes 65536 | tf_op jit(solution)/shard_map/all_to_all | solution.py:358
  8.8 2.7 %all-to-all-done.10 = f32[8,8,128]{2,1,0:T(8,128)S(1)} async-done(((f32[8,8,128]{2,1,0:T(8,128)}), f32[8,8,128]{2,1,0:T(8,128)S(1)}, u32[]{:S(2)}, u32[]{:S(2)}) %all-to-all-start.10) | async-done | bytes 32800 | tf_op jit(solution)/shard_map/all_to_all | solution.py:358
  12.3 7.9 %all-to-all-start.11 = ((f32[16,8,8,128]{3,2,1,0:T(8,128)}), f32[16,8,8,128]{3,2,1,0:T(8,128)S(1)}, u32[]{:S(2)}, u32[]{:S(2)}) async-start(f32[16,8,8,128]{3,2,1,0:T(8,128)} %broadcast_in_dim.45), calls=%async_computation.11 | async-start | bytes 1048576 | tf_op jit(solution)/shard_map/all_to_all | solution.py:363
  23.6 2.5 %copy.99.est2 = bf16[4096,256]{1,0:T(8,128)(2,1)} copy(bf16[4096,256]{0,1:T(8,128)(2,1)S(1)} %bitcast.73) | data formatting | bytes 4194304 | tf_op jit(solution)/shard_map/convert_element_type | solution.py:33
  26.1 5.6 %all-to-all-done.11 = f32[16,8,8,128]{3,2,1,0:T(8,128)S(1)} async-done(((f32[16,8,8,128]{3,2,1,0:T(8,128)}), f32[16,8,8,128]{3,2,1,0:T(8,128)S(1)}, u32[]{:S(2)}, u32[]{:S(2)}) %all-to-all-start.11) | async-done | bytes 524320 | tf_op jit(solution)/shard_map/all_to_all | solution.py:363
  33.4 23.3 %build_cover.1 = (bf16[4096,4096]{1,0:T(8,128)(2,1)}, f8e5m2[4096,4096]{1,0:T(32,128)(4,1)}, f32[16,2,96,128]{3,2,1,0:T(8,128)S(1)}) custom-call(s32[32]{0:T(128)} %get-tuple-element.52.tab, s32[2]{0:T(128)} %pad_add_fusion.1.origin, f32[128,8,128]{2,1,0:T(8,128)} %bitcast.70, f32[16,256]{1,0:T(8,128)} %clut.1, bf16[4096,256]{1,0:T(8,128)(2,1)} %copy.99.est2), custom_call_target="tpu_custom_call" | custom-call | tf_op jit(solution)/shard_map/build_cover/pallas_call | solution.py:206
  56.7 19.6 %conditional.4 = (f32[16,2,96,128]{3,2,1,0:T(8,128)S(1)}) conditional(s32[]{:T(128)} %convert_element_type.38, f32[16,2,96,128]{3,2,1,0:T(8,128)S(1)} %get-tuple-element.35, f32[16,2,96,128]{3,2,1,0:T(8,128)S(1)} %get-tuple-element.35), branch_computations={%region_4.5_spmd, %region_5.6_spmd} | conditional | bytes 5505036 | solution.py:345
  56.8 19.4 %all_to_all.70 = f32[16,96,128]{2,1,0:T(8,128)S(1)} all-to-all(f32[16,96,128]{2,1,0:T(8,128)S(1)} %slice_bitcast_fusion), channel_id=1, replica_groups=mesh['row'=16,'col'=8] {'row'}, dimensions={0} | all-to-all | bytes 1572864 | tf_op jit(solution)/shard_map/cond/branch_0_fun/all_to_all | solution.py:336
  77.4 20.5 %all_to_all.80 = f32[8,96,128]{2,1,0:T(8,128)S(1)} all-to-all(f32[8,96,128]{2,1,0:T(8,128)S(1)} %combine_slots.2), channel_id=1, replica_groups=mesh['row'=16,'col'=8] {'col'}, dimensions={0} | all-to-all | bytes 786432 | tf_op jit(solution)/shard_map/all_to_all | solution.py:386
  98.7 3.5 %all-to-all-start.13 = ((f32[8,96,128]{2,1,0:T(8,128)}), f32[8,96,128]{2,1,0:T(8,128)S(1)}, u32[]{:S(2)}, u32[]{:S(2)}) async-start(f32[8,96,128]{2,1,0:T(8,128)} %broadcast_in_dim.47), calls=%async_computation.13 | async-start | bytes 786432 | tf_op jit(solution)/shard_map/all_to_all | solution.py:388
  104.1 2.2 copy.111
  106.4 4.6 %all-to-all-done.13.table = f32[8,96,128]{2,1,0:T(8,128)S(1)} async-done(((f32[8,96,128]{2,1,0:T(8,128)}), f32[8,96,128]{2,1,0:T(8,128)S(1)}, u32[]{:S(2)}, u32[]{:S(2)}) %all-to-all-start.13) | async-done | bytes 393248 | tf_op jit(solution)/shard_map/all_to_all | solution.py:388
  111.8 26.0 %conditional.5 = (f32[16,2,96,128]{3,2,1,0:T(8,128)S(1)}) conditional(s32[]{:T(128)} %convert_element_type.38, f32[16,2,96,128]{3,2,1,0:T(8,128)S(1)} %pick_slots.2, f32[16,2,96,128]{3,2,1,0:T(8,128)S(1)} %pick_slots.2), branch_computations={%region_7.8_spmd, %region_8.9_spmd} | conditional | flops 196608 | bytes 7077900 | solution.py:345
  111.8 12.9 %all_to_all.72 = f32[16,48,128]{2,1,0:T(8,128)S(1)} all-to-all(f32[16,48,128]{2,1,0:T(8,128)S(1)} %get-tuple-element.45), channel_id=1, replica_groups=mesh['row'=16,'col'=8] {'row'}, dimensions={0} | all-to-all | bytes 786432 | tf_op jit(solution)/shard_map/cond/branch_0_fun/all_to_all | solution.py:336
  124.7 12.6 %all_to_all.73 = f32[16,48,128]{2,1,0:T(8,128)S(1)} all-to-all(f32[16,48,128]{2,1,0:T(8,128)S(1)} %get-tuple-element.46), channel_id=1, replica_groups=mesh['row'=16,'col'=8] {'row'}, dimensions={0} | all-to-all | bytes 786432 | tf_op jit(solution)/shard_map/cond/branch_0_fun/all_to_all | solution.py:336
  137.8 17.7 %backward_product.2 = (f32[96,4096]{1,0:T(8,128)}, f32[8,4096]{1,0:T(8,128)}, f32[16,2,96,128]{3,2,1,0:T(8,128)S(1)}) custom-call(s32[33]{0:T(128)} %pad_add_fusion.tab, f32[128,8,128]{2,1,0:T(8,128)} %bitcast.71, f32[16,2,96,128]{3,2,1,0:T(8,128)S(1)} %get-tuple-element.42.ratios, f32[96,4096]{1,0:T(8,128)} %bitcast.74, ...), custom_call_target="tpu_custom_call" | custom-call | tf_op jit(solution)/shard_map/backward_product/pallas_call | solution.py:275
  155.5 18.4 %conditional.6 = (f32[16,2,96,128]{3,2,1,0:T(8,128)S(1)}) conditional(s32[]{:T(128)} %convert_element_type.38, f32[16,2,96,128]{3,2,1,0:T(8,128)S(1)} %get-tuple-element.38, f32[16,2,96,128]{3,2,1,0:T(8,128)S(1)} %get-tuple-element.38), branch_computations={%region_9.10_spmd, %region_10.11_spmd} | conditional | bytes 5505036 | solution.py:345
  155.5 18.2 %all_to_all.75 = f32[16,96,128]{2,1,0:T(8,128)S(1)} all-to-all(f32[16,96,128]{2,1,0:T(8,128)S(1)} %slice_bitcast_fusion.3), channel_id=1, replica_groups=mesh['row'=16,'col'=8] {'row'}, dimensions={0} | all-to-all | bytes 1572864 | tf_op jit(solution)/shard_map/cond/branch_0_fun/all_to_all | solution.py:336
  174.9 21.8 %all_to_all.81 = f32[8,96,128]{2,1,0:T(8,128)S(1)} all-to-all(f32[8,96,128]{2,1,0:T(8,128)S(1)} %combine_slots.3), channel_id=1, replica_groups=mesh['row'=16,'col'=8] {'col'}, dimensions={0} | all-to-all | bytes 786432 | tf_op jit(solution)/shard_map/all_to_all | solution.py:386
  196.7 11.3 %all_to_all.82.table = f32[8,96,128]{2,1,0:T(8,128)S(1)} all-to-all(f32[8,96,128]{2,1,0:T(8,128)S(1)} %broadcast_in_dim.48), channel_id=1, replica_groups=mesh['row'=16,'col'=8] {'col'}, dimensions={0} | all-to-all | bytes 786432 | tf_op jit(solution)/shard_map/all_to_all | solution.py:388
  208.8 25.8 %conditional.7 = (f32[16,2,96,128]{3,2,1,0:T(8,128)S(1)}) conditional(s32[]{:T(128)} %convert_element_type.38, f32[16,2,96,128]{3,2,1,0:T(8,128)S(1)} %pick_slots.3, f32[16,2,96,128]{3,2,1,0:T(8,128)S(1)} %pick_slots.3), branch_computations={%region_12.13_spmd, %region_13.14_spmd} | conditional | flops 196608 | bytes 7077900 | solution.py:345
  208.9 12.9 %all_to_all.77 = f32[16,48,128]{2,1,0:T(8,128)S(1)} all-to-all(f32[16,48,128]{2,1,0:T(8,128)S(1)} %get-tuple-element.47), channel_id=1, replica_groups=mesh['row'=16,'col'=8] {'row'}, dimensions={0} | all-to-all | bytes 786432 | tf_op jit(solution)/shard_map/cond/branch_0_fun/all_to_all | solution.py:336
  221.8 12.6 %all_to_all.78 = f32[16,48,128]{2,1,0:T(8,128)S(1)} all-to-all(f32[16,48,128]{2,1,0:T(8,128)S(1)} %get-tuple-element.48), channel_id=1, replica_groups=mesh['row'=16,'col'=8] {'row'}, dimensions={0} | all-to-all | bytes 786432 | tf_op jit(solution)/shard_map/cond/branch_0_fun/all_to_all | solution.py:336
  234.7 11.8 %backward_product.3 = f32[96,16,256]{2,1,0:T(8,128)} custom-call(s32[33]{0:T(128)} %pad_add_fusion.tab, f32[128,8,128]{2,1,0:T(8,128)} %bitcast.72, f32[16,2,96,128]{3,2,1,0:T(8,128)S(1)} %get-tuple-element.44.ratios, f32[96,4096]{1,0:T(8,128)} %get-tuple-element.39.est, bf16[4096,4096]{1,0:T(8,128)(2,1)} %get-tuple-element.36.hi, ...), custom_call_target="tpu_custom_call" | custom-call | tf_op jit(solution)/shard_map/backward_product/pallas_call | solution.py:275
  (55 shorter events, 15.5 us)
Async XLA Ops:
  0.0 20.2 %copy-start.1 = (f32[96,16,256]{2,1,0:T(8,128)S(1)}, f32[96,16,256]{2,1,0:T(8,128)}, u32[]{:S(2)}) copy-start(f32[96,16,256]{2,1,0:T(8,128)} %param.14) | copy-start | bytes 4718596
  1.4 10.0 %all-to-all-start.10 = ((f32[8,8,128]{2,1,0:T(8,128)}), f32[8,8,128]{2,1,0:T(8,128)S(1)}, u32[]{:S(2)}, u32[]{:S(2)}) async-start(f32[8,8,128]{2,1,0:T(8,128)} %broadcast_in_dim.44), calls=%async_computation.10 | async-start | bytes 65536 | tf_op jit(solution)/shard_map/all_to_all | solution.py:358
  12.3 19.3 %all-to-all-start.11 = ((f32[16,8,8,128]{3,2,1,0:T(8,128)}), f32[16,8,8,128]{3,2,1,0:T(8,128)S(1)}, u32[]{:S(2)}, u32[]{:S(2)}) async-start(f32[16,8,8,128]{3,2,1,0:T(8,128)} %broadcast_in_dim.45), calls=%async_computation.11 | async-start | bytes 1048576 | tf_op jit(solution)/shard_map/all_to_all | solution.py:363
  31.7 1.8 copy-start
  76.3 21.5 %copy-start.3 = (s32[1,96,128]{2,1,0:T(8,128)S(1)}, s32[1,96,128]{2,1,0:T(8,128)}, u32[]{:S(2)}) copy-start(s32[1,96,128]{2,1,0:T(8,128)} %param.16) | copy-start | bytes 147460
  77.3 24.8 %copy-start.4 = (s32[32]{0:T(128)S(1)}, s32[32]{0:T(128)}, u32[]{:S(2)}) copy-start(s32[32]{0:T(128)} %get-tuple-element.52.tab) | copy-start | bytes 388
  77.3 26.8 %copy-start.2 = (f32[96,16,256]{2,1,0:T(8,128)S(1)}, f32[96,16,256]{2,1,0:T(8,128)}, u32[]{:S(2)}) copy-start(f32[96,16,256]{2,1,0:T(8,128)} %param.14) | copy-start | bytes 4718596
  98.7 12.3 %all-to-all-start.13 = ((f32[8,96,128]{2,1,0:T(8,128)}), f32[8,96,128]{2,1,0:T(8,128)S(1)}, u32[]{:S(2)}, u32[]{:S(2)}) async-start(f32[8,96,128]{2,1,0:T(8,128)} %broadcast_in_dim.47), calls=%async_computation.13 | async-start | bytes 786432 | tf_op jit(solution)/shard_map/all_to_all | solution.py:388
